TPU v7x, 32 devices: a whole 2x2x4 slice. The times are simulated.
32 devices in a mesh: seq: 4 (over x, core), mp: 8 (over z, y).
Axes of the slice: x: 2, y: 2, z: 4, core: 2. Of those that a mesh axis runs over, the one named last changes fastest.
Arguments:
- tokens: bfloat16 [2, 6144, 1024], P(None, ('seq', 'mp')), may hold values from -6 to 6
- ln1_gain: float32 [1024], replicated, may hold values from 0.1 to 1.9
- ln1_bias: float32 [1024], replicated, may hold values from -1.75 to 1.75
- ln2_gain: float32 [1024], replicated, may hold values from 0.1 to 1.9
- ln2_bias: float32 [1024], replicated, may hold values from -1.75 to 1.75
- q_weight: bfloat16 [1024, 1024], P('seq', 'mp'), may hold values from -0.1875 to 0.1875
- k_weight: bfloat16 [1024, 1024], P('seq', 'mp'), may hold values from -0.1875 to 0.1875
- value_weight: bfloat16 [1024, 1024], P('seq', 'mp'), may hold values from -0.1875 to 0.1875
- out_weight: bfloat16 [1024, 1024], P('mp', 'seq'), may hold values from -2 to 2
- up_weight: bfloat16 [1024, 4096], P('seq', 'mp'), may hold values from -0.1875 to 0.1875
- down_weight: bfloat16 [4096, 1024], P('mp', 'seq'), may hold values from -0.09375 to 0.09375
- lengths: int32 [2, 4, 3], P(None, 'seq'), may hold values from 1 to 1024, 1536 in all within a row
- cotangent: bfloat16 [2, 6144, 1024], P(None, ('seq', 'mp')), may hold values from -12 to 12
Outputs:
- mixed: bfloat16 [2, 6144, 1024], P(None, ('seq', 'mp'))
- grad_tokens: float32 [2, 6144, 1024], P(None, ('seq', 'mp'))
- grad_ln1_gain: float32 [1024], replicated
- grad_ln1_bias: float32 [1024], replicated
- grad_ln2_gain: float32 [1024], replicated
- grad_ln2_bias: float32 [1024], replicated
- grad_q_weight: float32 [1024, 1024], P('seq', 'mp')
- grad_k_weight: float32 [1024, 1024], P('seq', 'mp')
- grad_v_weight: float32 [1024, 1024], P('seq', 'mp')
- grad_out_weight: float32 [1024, 1024], P('mp', 'seq')
- grad_up_weight: float32 [1024, 4096], P('seq', 'mp')
- grad_down_weight: float32 [4096, 1024], P('mp', 'seq')
Inputs may be any that keep to these rules, and one draw needn't show every extreme that they name: lengths[m, s] lists the 3 documents of row group s of micro-batch m in order; each row sums to 1536, and its longest document holds exactly 1024 tokens.
All inputs are finite; a program needn't handle non-finite values.
Results may differ from a plain program's by a relative error of at most 0.013.
Values may be sent and summed in bfloat16 or wider, within the bound.
No kernel may reach another device: no remote copies, remote signals or barrier semaphores. Data moves between devices by JAX's collectives and lax.ppermute only.
A program may use at most 192 MiB of HBM per device.

v0:
```python
from functools import partial
import math

import jax
import jax.numpy as jnp
from jax import lax
from jax.sharding import PartitionSpec as P

HEAD_DIM = 64
ROT = 16
FEATS = 64


def prime_list(wanted):
    found_primes = []
    candidate = 2
    while len(found_primes) < wanted:
        if all((candidate % earlier != 0 for earlier in found_primes)):
            found_primes.append(candidate)
        candidate += 1
    return found_primes


def feature_maps(head_width, feature_count):
    primes_found = prime_list(head_width)
    uniform_rows = [
        [
            min(max((row_idx + 0.5) * math.sqrt(prime_val) % 1.0, 0.001), 0.999)
            for prime_val in primes_found
        ]
        for row_idx in range(feature_count)
    ]
    uniform_pts = jnp.asarray(uniform_rows, jnp.float32)
    points = math.sqrt(2.0) * lax.erf_inv(2.0 * uniform_pts - 1.0)
    cosine_rows = [
        [
            math.sqrt(2.0 / head_width)
            * math.cos(math.pi * (cell_idx + 0.5) * freq_idx / head_width)
            * (math.sqrt(0.5) if freq_idx == 0 else 1.0)
            for cell_idx in range(head_width)
        ]
        for freq_idx in range(head_width)
    ]
    cosine = jnp.asarray(cosine_rows, jnp.float32)
    project = jnp.dot(points, cosine, precision=lax.Precision.HIGHEST)
    project = jnp.transpose(project) * (1.0 / math.sqrt(head_width))
    weighting = 1.0 / (1.0 + jnp.sum(points * points, axis=1) / head_width)
    return (project, weighting)


def rotate_heads(values, offset):
    half_dims = ROT // 2
    inverse = 10000.0 ** (-jnp.arange(half_dims, dtype=jnp.float32) * 2.0 / ROT)
    angles = offset[:, None] * inverse[None, :]
    cosine = jnp.cos(angles)[None, :, :]
    sine_part = jnp.sin(angles)[None, :, :]
    first_half = values[..., :half_dims]
    second = values[..., half_dims:ROT]
    return jnp.concatenate(
        [
            first_half * cosine - second * sine_part,
            second * cosine + first_half * sine_part,
            values[..., ROT:],
        ],
        axis=-1,
    )


def layer_norm(values, gain_vec, bias_vec):
    centered = values - jnp.mean(values, axis=-1, keepdims=True)
    variance = jnp.mean(centered * centered, axis=-1, keepdims=True)
    return centered * lax.rsqrt(variance + 1e-05) * gain_vec + bias_vec


def exact_gelu(values):
    return jax.nn.gelu(values, approximate=False)


def doc_layout(doc_lengths, number_of_tokens):
    doc_ends = jnp.cumsum(doc_lengths).astype(jnp.int32)
    starts = (doc_ends - doc_lengths).astype(jnp.int32)
    places = jnp.arange(number_of_tokens, dtype=jnp.int32)
    segment = jnp.sum((places[:, None] >= doc_ends[None, :]).astype(jnp.int32), axis=1).astype(
        jnp.int32
    )
    member = segment[:, None] == jnp.arange(doc_lengths.shape[0], dtype=jnp.int32)[None, :]
    offset = places - jnp.sum(jnp.where(member, starts[None, :], 0), axis=1).astype(jnp.int32)
    return (segment, offset.astype(jnp.float32))


def contract_rows(left_side, right_side):
    return lax.dot_general(
        left_side, right_side, (((0,), (0,)), ((), ())), preferred_element_type=jnp.float32
    )


def contract_cols(left_side, right_side):
    return lax.dot_general(
        left_side, right_side, (((1,), (1,)), ((), ())), preferred_element_type=jnp.float32
    )


def local_attention(plain_query_rows, key_raw, value_raw, segment, offset, project, weighting):
    maximal_precision_mode = lax.Precision.HIGHEST
    number_of_tokens = plain_query_rows.shape[0]
    head_count = plain_query_rows.shape[1] // HEAD_DIM

    def heads_first(values):
        return jnp.transpose(values.reshape(number_of_tokens, head_count, HEAD_DIM), (1, 0, 2))

    rot_query = rotate_heads(heads_first(plain_query_rows), offset)
    rot_key = rotate_heads(heads_first(key_raw), offset)
    value_heads = heads_first(value_raw)
    feat_query = (
        jnp.exp(jnp.einsum("htd,df->htf", rot_query, project, precision=maximal_precision_mode))
        * weighting
    )
    feat_key = jnp.exp(
        jnp.einsum("htd,df->htf", rot_key, project, precision=maximal_precision_mode)
    )
    rows_per_block = min(512, number_of_tokens)
    block_count = number_of_tokens // rows_per_block

    def split_blocks(values):
        return jnp.transpose(
            values.reshape((head_count, block_count, rows_per_block, values.shape[2])), (1, 0, 2, 3)
        )

    def block_step(carry, pieces):
        kv_state, totals, previous = carry
        block_of_queries, block_of_keys, value_block, block_segment = pieces
        places = jnp.arange(block_segment.shape[0], dtype=jnp.int32)
        attention_scores = jnp.einsum(
            "ugy,uky->ugk", block_of_queries, block_of_keys, precision=maximal_precision_mode
        )
        allowed = (places[:, None] >= places[None, :]) & (
            block_segment[:, None] == block_segment[None, :]
        )
        attention_scores = jnp.where(allowed[None, :, :], attention_scores, 0.0)
        numerator = jnp.einsum(
            "hqk,hkd->hqd", attention_scores, value_block, precision=maximal_precision_mode
        )
        denominator = jnp.sum(attention_scores, axis=2)
        carried_in = (block_segment == previous)[None, :]
        numerator = numerator + jnp.where(
            carried_in[:, :, None],
            jnp.einsum(
                "hqf,hfd->hqd", block_of_queries, kv_state, precision=maximal_precision_mode
            ),
            0.0,
        )
        denominator = denominator + jnp.where(
            carried_in,
            jnp.einsum("hqf,hf->hq", block_of_queries, totals, precision=maximal_precision_mode),
            0.0,
        )
        final_output = block_segment[-1]
        carried_over = final_output == previous
        trailing_mask = (block_segment == final_output).astype(jnp.float32)
        new_state = jnp.where(carried_over, kv_state, 0.0) + jnp.einsum(
            "hrf,hrd,r->hfd",
            block_of_keys,
            value_block,
            trailing_mask,
            precision=maximal_precision_mode,
        )
        new_totals = jnp.where(carried_over, totals, 0.0) + jnp.einsum(
            "hrf,r->hf", block_of_keys, trailing_mask, precision=maximal_precision_mode
        )
        return ((new_state, new_totals, final_output), numerator / denominator[:, :, None])

    start_carry = (
        jnp.zeros((head_count, FEATS, HEAD_DIM), jnp.float32),
        jnp.zeros((head_count, FEATS), jnp.float32),
        jnp.array(-1, jnp.int32),
    )
    _, outputs = lax.scan(
        jax.checkpoint(block_step),
        start_carry,
        (
            split_blocks(feat_query),
            split_blocks(feat_key),
            split_blocks(value_heads),
            segment.reshape(block_count, rows_per_block),
        ),
    )
    joined = jnp.transpose(outputs, (1, 0, 2, 3)).reshape(head_count, number_of_tokens, HEAD_DIM)
    return jnp.transpose(joined, (1, 0, 2)).reshape(number_of_tokens, head_count * HEAD_DIM)


def local(
    tokens,
    ln1_gain,
    ln1_bias,
    ln2_gain,
    ln2_bias,
    q_weight,
    k_weight,
    value_weight,
    out_weight,
    up_weight,
    down_weight,
    lengths,
    cotangent,
):
    micro_count = tokens.shape[0]
    local_rows = tokens.shape[1]
    group_rows = local_rows * lax.axis_size("mp")
    seq_count = lax.axis_size("seq")
    project, weighting = feature_maps(HEAD_DIM, FEATS)
    grad_sums = [
        jnp.zeros((q_weight.shape[0] * seq_count, q_weight.shape[1]), jnp.float32),
        jnp.zeros((k_weight.shape[0] * seq_count, k_weight.shape[1]), jnp.float32),
        jnp.zeros((value_weight.shape[0] * seq_count, value_weight.shape[1]), jnp.float32),
        jnp.zeros((out_weight.shape[0], out_weight.shape[1] * seq_count), jnp.float32),
        jnp.zeros((up_weight.shape[0] * seq_count, up_weight.shape[1]), jnp.float32),
        jnp.zeros((down_weight.shape[0], down_weight.shape[1] * seq_count), jnp.float32),
    ]
    norm_sums = [
        jnp.zeros_like(ln1_gain),
        jnp.zeros_like(ln1_bias),
        jnp.zeros_like(ln2_gain),
        jnp.zeros_like(ln2_bias),
    ]
    mixed_parts = []
    grad_parts = []
    for micro_step in range(micro_count):
        full_weights = (
            lax.all_gather(q_weight, "seq", axis=0, tiled=True),
            lax.all_gather(k_weight, "seq", axis=0, tiled=True),
            lax.all_gather(value_weight, "seq", axis=0, tiled=True),
            lax.all_gather(out_weight, "seq", axis=1, tiled=True),
            lax.all_gather(up_weight, "seq", axis=0, tiled=True),
            lax.all_gather(down_weight, "seq", axis=1, tiled=True),
        )
        w_query, w_key, w_value, w_out, w_up, w_down = full_weights
        rows_in = tokens[micro_step].astype(jnp.float32)
        normed_one, pull_one = jax.vjp(layer_norm, rows_in, ln1_gain, ln1_bias)
        normed_two, pull_two = jax.vjp(layer_norm, rows_in, ln2_gain, ln2_bias)
        group_one, group_two = (
            lax.all_gather(normed_one.astype(jnp.bfloat16), "mp", axis=0, tiled=True),
            lax.all_gather(normed_two.astype(jnp.bfloat16), "mp", axis=0, tiled=True),
        )
        plain_query_rows = jnp.dot(group_one, w_query, preferred_element_type=jnp.float32)
        key_raw = jnp.dot(group_one, w_key, preferred_element_type=jnp.float32)
        value_raw = jnp.dot(group_one, w_value, preferred_element_type=jnp.float32)
        segment, offset = doc_layout(lengths[micro_step, 0], group_rows)
        attend = partial(
            local_attention, segment=segment, offset=offset, project=project, weighting=weighting
        )
        context, pull_attn = jax.vjp(attend, plain_query_rows, key_raw, value_raw)
        context_low = context.astype(jnp.bfloat16)
        hidden = jnp.dot(group_two, w_up, preferred_element_type=jnp.float32)
        activated, pull_gelu = jax.vjp(exact_gelu, hidden)
        activated_low = activated.astype(jnp.bfloat16)
        context_rows = lax.slice_in_dim(context_low, 0, lax.axis_size("mp") * local_rows, axis=0)
        active_rows = lax.slice_in_dim(activated_low, 0, lax.axis_size("mp") * local_rows, axis=0)
        branch_sum = lax.psum_scatter(
            jnp.dot(context_rows, w_out, preferred_element_type=jnp.float32)
            + jnp.dot(active_rows, w_down, preferred_element_type=jnp.float32),
            "mp",
            scatter_dimension=0,
            tiled=True,
        )
        mixed_parts.append((rows_in + branch_sum).astype(jnp.bfloat16))
        grad_group = lax.all_gather(cotangent[micro_step], "mp", axis=0, tiled=True)
        grad_context = contract_cols(grad_group, w_out)
        grad_activated = contract_cols(grad_group, w_down)
        grad_hidden = pull_gelu(grad_activated)[0].astype(jnp.bfloat16)
        grad_query_f, grad_key_f, grad_value_f = pull_attn(grad_context)
        grad_query = grad_query_f.astype(jnp.bfloat16)
        grad_key = grad_key_f.astype(jnp.bfloat16)
        grad_value = grad_value_f.astype(jnp.bfloat16)
        micro_grads = (
            contract_rows(group_one, grad_query),
            contract_rows(group_one, grad_key),
            contract_rows(group_one, grad_value),
            contract_rows(context_low, grad_group),
            contract_rows(group_two, grad_hidden),
            contract_rows(activated_low, grad_group),
        )
        grad_sums = [total + term for total, term in zip(grad_sums, micro_grads)]
        part_one = (
            contract_cols(grad_query, w_query)
            + contract_cols(grad_key, w_key)
            + contract_cols(grad_value, w_value)
        )
        part_two = contract_cols(grad_hidden, w_up)
        sum_one, sum_two = (
            lax.psum_scatter(
                part_one.astype(jnp.bfloat16), "mp", scatter_dimension=0, tiled=True
            ).astype(jnp.float32),
            lax.psum_scatter(
                part_two.astype(jnp.bfloat16), "mp", scatter_dimension=0, tiled=True
            ).astype(jnp.float32),
        )
        grad_in_one, grad_gain_one, grad_bias_one = pull_one(sum_one)
        grad_in_two, grad_gain_two, grad_bias_two = pull_two(sum_two)
        grad_parts.append(cotangent[micro_step].astype(jnp.float32) + grad_in_one + grad_in_two)
        norm_sums = [
            norm_sums[0] + grad_gain_one,
            norm_sums[1] + grad_bias_one,
            norm_sums[2] + grad_gain_two,
            norm_sums[3] + grad_bias_two,
        ]
    weight_grads = (
        lax.psum_scatter(
            grad_sums[0].astype(jnp.bfloat16), "seq", scatter_dimension=0, tiled=True
        ).astype(jnp.float32),
        lax.psum_scatter(
            grad_sums[1].astype(jnp.bfloat16), "seq", scatter_dimension=0, tiled=True
        ).astype(jnp.float32),
        lax.psum_scatter(
            grad_sums[2].astype(jnp.bfloat16), "seq", scatter_dimension=0, tiled=True
        ).astype(jnp.float32),
        lax.psum_scatter(
            grad_sums[3].astype(jnp.bfloat16), "seq", scatter_dimension=1, tiled=True
        ).astype(jnp.float32),
        lax.psum_scatter(
            grad_sums[4].astype(jnp.bfloat16), "seq", scatter_dimension=0, tiled=True
        ).astype(jnp.float32),
        lax.psum_scatter(
            grad_sums[5].astype(jnp.bfloat16), "seq", scatter_dimension=1, tiled=True
        ).astype(jnp.float32),
    )
    norm_grads = lax.psum((norm_sums[0], norm_sums[1], norm_sums[2], norm_sums[3]), ("seq", "mp"))
    return (
        jnp.stack(mixed_parts),
        jnp.stack(grad_parts),
        norm_grads[0],
        norm_grads[1],
        norm_grads[2],
        norm_grads[3],
        weight_grads[0],
        weight_grads[1],
        weight_grads[2],
        weight_grads[3],
        weight_grads[4],
        weight_grads[5],
    )


def solution(mesh):
    in_specs = (
        P(None, ("seq", "mp"), None),
        P(),
        P(),
        P(),
        P(),
        P("seq", "mp"),
        P("seq", "mp"),
        P("seq", "mp"),
        P("mp", "seq"),
        P("seq", "mp"),
        P("mp", "seq"),
        P(None, "seq", None),
        P(None, ("seq", "mp"), None),
    )
    out_specs = (
        P(None, ("seq", "mp"), None),
        P(None, ("seq", "mp"), None),
        P(),
        P(),
        P(),
        P(),
        P("seq", "mp"),
        P("seq", "mp"),
        P("seq", "mp"),
        P("mp", "seq"),
        P("seq", "mp"),
        P("mp", "seq"),
    )
    return jax.shard_map(local, mesh=mesh, in_specs=in_specs, out_specs=out_specs, check_vma=False)
```

profile of v0, /device:TPU:0, one launch (start us, length us, event | category | flops | bytes accessed | tf_op | source)
XLA Modules:
  0.0 1164.3 jit_solution(13924311496966079492)
XLA Ops:
  20.3 7.7 all_gather.43
  27.9 5.8 all_gather.45
  35.7 5.9 all_gather.44
  41.5 6.3 all_gather.46
  48.9 27.5 %all-gather.19.cloned.1.call-done = bf16[1536,1024]{1,0:T(8,128)(2,1)} async-done(((bf16[192,1024]{1,0:T(8,128)(2,1)}), bf16[1536,1024]{1,0:T(8,128)(2,1)}) %all-gather.19.cloned.1.call-update) | async-done | bytes 3145744 | tf_op jit(solution)/shard_map/all_gather | solution.py:241
  76.4 3.1 fusion.383
  81.2 56.1 %all-gather.11.cloned.1.call-done = bf16[1536,1024]{1,0:T(8,128)(2,1)} async-done(((bf16[192,1024]{1,0:T(8,128)(2,1)}), bf16[1536,1024]{1,0:T(8,128)(2,1)}) %all-gather.11.cloned.1.call-update) | async-done | bytes 3145744 | tf_op jit(solution)/shard_map/all_gather | solution.py:241
  137.3 3.1 fusion.379
  156.1 2.9 convolution_exponential_fusion.1
  170.6 50.6 %while.95 = (s32[]{:T(128)}, f32[2,64,64]{2,1,0:T(8,128)S(1)}, f32[2,64]{1,0:T(2,128)S(1)}, s32[]{:T(128)}, bf16[3,2,512,64]{2,3,1,0:T(8,128)(2,1)}, /*index=5*/...) while((s32[]{:T(128)}, f32[2,64,64]{2,1,0:T(8,128)S(1)}, ...), condition=%wide.region_17.18_spmd.clone, body=%wide.region_15.17_spmd.clone.sunk | while | flops 910208896 | bytes 8145129 | solution.py:177
  172.4 3.0 select_reduce_fusion.11
  177.7 3.3 fusion.628
  189.2 3.0 select_reduce_fusion.11
  194.6 3.3 fusion.628
  206.1 3.0 select_reduce_fusion.11
  211.5 3.3 fusion.628
  221.3 3.1 fusion.240
  227.9 79.3 %while.97 = (s32[]{:T(128)}, f32[2,64,64]{2,1,0:T(8,128)}, f32[2,64]{1,0:T(2,128)S(1)}, f32[3,2,512,64]{2,3,1,0:T(8,128)}, f32[3,2,512,64]{2,3,1,0:T(8,128)}, /*...) while((s32[]{:T(128)}, f32[2,64,64]{2,1,0:T(8,128)}, ...), condition=%wide.region_32.33_spmd.clone, body=%wide.region_29.32_spmd.clone.sunk | while | flops 2675472384 | bytes 24581376 | solution.py:177
  319.0 2.8 convolution_exponential_fusion.3
  332.4 42.4 %while.94 = (s32[]{:T(128)}, f32[2,64,64]{2,1,0:T(8,128)S(1)}, f32[2,64]{1,0:T(2,128)S(1)}, s32[]{:T(128)}, bf16[3,2,512,64]{2,3,1,0:T(8,128)(2,1)}, /*index=5*/...) while((s32[]{:T(128)}, f32[2,64,64]{2,1,0:T(8,128)S(1)}, ...), condition=%wide.region_8.9_spmd.clone, body=%wide.region_6.8_spmd.clone.sunk | while | flops 910208896 | bytes 8145645 | solution.py:177
  332.9 3.0 select_reduce_fusion.10
  337.8 3.3 fusion.613
  347.1 3.0 select_reduce_fusion.10
  351.9 3.3 fusion.613
  361.2 3.0 select_reduce_fusion.10
  366.0 3.3 fusion.613
  374.8 3.1 fusion.248
  380.5 68.0 %while.96 = (s32[]{:T(128)}, f32[2,64,64]{2,1,0:T(8,128)S(1)}, f32[2,64]{1,0:T(2,128)S(1)}, f32[3,2,512,64]{2,3,1,0:T(8,128)}, f32[3,2,512,64]{2,3,1,0:T(8,128)}...) while((s32[]{:T(128)}, f32[2,64,64]{2,1,0:T(8,128)S(1)}, ...), condition=%wide.region_22.23_spmd.clone, body=%wide.region_19.22_spmd.clone.sunk | while | flops 2675472384 | bytes 24581376 | solution.py:177
  463.1 2.9 fusion.389
  468.7 3.0 fusion.391
  477.9 12.0 %multiply_convert_fusion.1 = (bf16[1536,512]{1,0:T(8,128)(2,1)}, f32[1536,512]{1,0:T(8,128)}, f32[1536,512]{1,0:T(8,128)}) fusion(bf16[1536,1024]{1,0:T(8,128)(2,1)} %all-gather.13.cloned.1.call-done, bf16[1024,512]{1,0:T(8,128)(2,1)} %all-gather.15.cloned.1.call-done), kind=kOutput, calls=%fused_computation.309 | convolution fusion | flops 1661730816 | bytes 12058624 | tf_op jit(solution)/shard_map/dot_general | solution.py:253
  489.8 12.0 %multiply_convert_fusion = (bf16[1536,512]{1,0:T(8,128)(2,1)}, f32[1536,512]{1,0:T(8,128)}, f32[1536,512]{1,0:T(8,128)}) fusion(bf16[1536,1024]{1,0:T(8,128)(2,1)} %all-gather.21.cloned.1.call-done, bf16[1024,512]{1,0:T(8,128)(2,1)} %all-gather.15.cloned.1.call-done), kind=kOutput, calls=%fused_computation.296 | convolution fusion | flops 1661730816 | bytes 12058624 | tf_op jit(solution)/shard_map/dot_general | solution.py:253
  501.9 6.1 add_convert_fusion.3
  516.8 2.8 add_convert_fusion.5
  519.7 4.3 fusion.234
  540.6 3.5 convolution_convert_fusion.1
  545.4 3.5 convolution_convert_fusion
  552.6 3.7 convolution_add_fusion.8
  559.6 3.7 convolution_add_fusion.9
  569.6 5.3 reduce-scatter.33.cloned.1.call-done
  576.7 25.4 %reduce-scatter.35.cloned.1.call-done = bf16[512,256]{1,0:T(8,128)(2,1)} async-done(((bf16[512,1024]{1,0:T(8,128)(2,1)}), bf16[512,256]{1,0:T(8,128)(2,1)}) %reduce-scatter.35.cloned.1.call-update) | async-done | bytes 262160 | tf_op jit(solution)/shard_map/reduce_scatter | solution.py:322
  603.9 76.0 %reduce-scatter.21.cloned.1.call-done = bf16[192,1024]{1,0:T(8,128)(2,1)} async-done(((bf16[1536,1024]{1,0:T(8,128)(2,1)}), bf16[192,1024]{1,0:T(8,128)(2,1)}) %reduce-scatter.21.cloned.1.call-update) | async-done | bytes 393232 | tf_op jit(solution)/shard_map/reduce_scatter | solution.py:290
  679.9 76.9 %reduce-scatter.17.cloned.1.call-done = bf16[192,1024]{1,0:T(8,128)(2,1)} async-done(((bf16[1536,1024]{1,0:T(8,128)(2,1)}), bf16[192,1024]{1,0:T(8,128)(2,1)}) %reduce-scatter.17.cloned.1.call-update) | async-done | bytes 393232 | tf_op jit(solution)/shard_map/reduce_scatter | solution.py:290
  758.4 75.1 %reduce-scatter.19.cloned.1.call-done = bf16[192,1024]{1,0:T(8,128)(2,1)} async-done(((bf16[1536,1024]{1,0:T(8,128)(2,1)}), bf16[192,1024]{1,0:T(8,128)(2,1)}) %reduce-scatter.19.cloned.1.call-update) | async-done | bytes 393232 | tf_op jit(solution)/shard_map/reduce_scatter | solution.py:293
  833.5 76.9 %reduce-scatter.23.cloned.1.call-done = bf16[192,1024]{1,0:T(8,128)(2,1)} async-done(((bf16[1536,1024]{1,0:T(8,128)(2,1)}), bf16[192,1024]{1,0:T(8,128)(2,1)}) %reduce-scatter.23.cloned.1.call-update) | async-done | bytes 393232 | tf_op jit(solution)/shard_map/reduce_scatter | solution.py:293
  915.2 43.5 %all-reduce.12 = (f32[1024]{0:T(1024)}, f32[1024]{0:T(1024)}, f32[1024]{0:T(1024)}, f32[1024]{0:T(1024)}) all-reduce(f32[1024]{0:T(1024)S(1)} %add.341, f32[1024]{0:T(1024)S(1)} %add.342, f32[1024]{0:T(1024)S(1)} %add.343, f32[1024]{0:T(1024)S(1)} %add.344), channel_id=1, replica_groups=mesh['seq'=4,'mp'=8] {'seq','mp'}, use_global_device_ids=true, to_apply=%region_41.42 | all-reduce | flops 4096 | bytes 32768 | tf_op jit(solution)/shard_map/psum | solution.py:326
  960.3 71.9 %reduce-scatter.15.cloned.1.call-done = f32[192,1024]{1,0:T(8,128)} async-done(((f32[1536,1024]{1,0:T(8,128)}), f32[192,1024]{1,0:T(8,128)}) %reduce-scatter.15.cloned.1.call-update) | async-done | bytes 786448 | tf_op jit(solution)/shard_map/reduce_scatter | solution.py:258
  1032.2 120.7 %reduce-scatter.13.cloned.1.call-done = f32[192,1024]{1,0:T(8,128)} async-done(((f32[1536,1024]{1,0:T(8,128)}), f32[192,1024]{1,0:T(8,128)}) %reduce-scatter.13.cloned.1.call-update) | async-done | bytes 786448 | tf_op jit(solution)/shard_map/reduce_scatter | solution.py:258
  (648 shorter events, 336.2 us)
Async XLA Ops:
  7.2 7.1 copy-start.48
  7.2 69.2 %all-gather.19.cloned.1.call-start = ((), (), s32[]{:S(2)}) async-start(), calls=%async_computation.17 | async-start | bytes 3538944 | tf_op jit(solution)/shard_map/all_gather | solution.py:241
  13.5 123.8 %all-gather.11.cloned.1.call-start = ((), (), s32[]{:S(2)}) async-start(), calls=%async_computation.12 | async-start | bytes 3538944 | tf_op jit(solution)/shard_map/all_gather | solution.py:241
  14.2 13.7 %copy-start.75 = (bf16[256,128]{1,0:T(8,128)(2,1)S(1)}, bf16[256,128]{1,0:T(8,128)(2,1)}, u32[]{:S(2)}) copy-start(bf16[256,128]{1,0:T(8,128)(2,1)} %param.28) | copy-start | bytes 196612
  14.2 207.0 %all-gather.25.cloned.1.call-start = ((), (), s32[]{:S(2)}) async-start(), calls=%async_computation.31 | async-start | bytes 3538944 | tf_op jit(solution)/shard_map/all_gather | solution.py:266
  15.3 18.5 %copy-start.95 = (s32[2,1,3]{2,1,0:T(1,128)S(1)}, s32[2,1,3]{2,1,0:T(1,128)}, u32[]{:S(2)}) copy-start(s32[2,1,3]{2,1,0:T(1,128)} %param.34) | copy-start | bytes 76
  15.3 20.4 %copy-start.76 = (bf16[256,128]{1,0:T(8,128)(2,1)S(1)}, bf16[256,128]{1,0:T(8,128)(2,1)}, u32[]{:S(2)}) copy-start(bf16[256,128]{1,0:T(8,128)(2,1)} %param.30) | copy-start | bytes 196612
  15.3 26.2 %copy-start.77 = (bf16[128,256]{1,0:T(8,128)(2,1)S(1)}, bf16[128,256]{1,0:T(8,128)(2,1)}, u32[]{:S(2)}) copy-start(bf16[128,256]{1,0:T(8,128)(2,1)} %param.31) | copy-start | bytes 196612
  15.3 359.5 %all-gather.23.cloned.1.call-start = ((), (), s32[]{:S(2)}) async-start(), calls=%async_computation.30 | async-start | bytes 3538944 | tf_op jit(solution)/shard_map/all_gather | solution.py:266
  15.9 461.9 %all-gather.15.cloned.1.call-start = ((), (), s32[]{:S(2)}) async-start(), calls=%async_computation.14 | async-start | bytes 1310720 | tf_op jit(solution)/shard_map/all_gather | solution.py:233
  16.5 461.4 %all-gather.13.cloned.1.call-start = ((), (), s32[]{:S(2)}) async-start(), calls=%async_computation.13 | async-start | bytes 3538944 | tf_op jit(solution)/shard_map/all_gather | solution.py:242
  17.1 472.7 %all-gather.21.cloned.1.call-start = ((), (), s32[]{:S(2)}) async-start(), calls=%async_computation.18 | async-start | bytes 3538944 | tf_op jit(solution)/shard_map/all_gather | solution.py:242
  17.8 484.0 %all-gather.17.cloned.1.call-start = ((), (), s32[]{:S(2)}) async-start(), calls=%async_computation.15 | async-start | bytes 1310720 | tf_op jit(solution)/shard_map/all_gather | solution.py:234
  18.6 544.9 %reduce-scatter.27.cloned.1.call-start = ((), (), s32[]{:S(2)}) async-start(), calls=%async_computation.25 | async-start | bytes 327680 | tf_op jit(solution)/shard_map/reduce_scatter | solution.py:310
  18.7 60.8 %copy-start.10 = (bf16[3,2,512,64]{2,3,1,0:T(8,128)(2,1)}, bf16[3,2,512,64]{2,3,1,0:T(8,128)(2,1)S(1)}, u32[]{:S(2)}) copy-start(bf16[3,2,512,64]{2,3,1,0:T(8,128)(2,1)S(1)} %fusion.373) | copy-start | bytes 1179652
  33.8 45.7 %copy-start.22 = (bf16[1024,128]{1,0:T(8,128)(2,1)}, bf16[1024,128]{1,0:T(8,128)(2,1)S(1)}, u32[]{:S(2)}) copy-start(bf16[1024,128]{1,0:T(8,128)(2,1)S(1)} %all_gather.45) | copy-start | bytes 786436
  41.5 285.2 %copy-start.18 = (bf16[1024,128]{1,0:T(8,128)(2,1)}, bf16[1024,128]{1,0:T(8,128)(2,1)S(1)}, u32[]{:S(2)}) copy-start(bf16[1024,128]{1,0:T(8,128)(2,1)S(1)} %all_gather.44) | copy-start | bytes 786436
  80.3 60.1 %copy-start = (bf16[1536,1024]{1,0:T(8,128)(2,1)S(1)}, bf16[1536,1024]{1,0:T(8,128)(2,1)}, u32[]{:S(2)}) copy-start(bf16[1536,1024]{1,0:T(8,128)(2,1)} %all-gather.19.cloned.1.call-done) | copy-start | bytes 9437188
  227.9 80.8 %copy-start.51 = (f32[64,64,1]{1,0,2:T(8,128)S(1)}, f32[64,64,1]{1,0,2:T(8,128)}, u32[]{:S(2)}) copy-start(f32[64,64,1]{1,0,2:T(8,128)} %constant.421) | copy-start | bytes 49156
  227.9 80.8 %copy-start.94 = (f32[64]{0:T(128)S(1)}, f32[64]{0:T(128)}, u32[]{:S(2)}) copy-start(f32[64]{0:T(128)} %constant.420) | copy-start | bytes 772
  316.4 10.3 copy-start.3
  332.4 42.4 %copy-start.20 = (bf16[128,1024]{1,0:T(8,128)(2,1)S(1)}, bf16[128,1024]{1,0:T(8,128)(2,1)}, u32[]{:S(2)}) copy-start(bf16[128,1024]{1,0:T(8,128)(2,1)} %all_gather.46) | copy-start | bytes 786436
  456.3 19.9 %copy-start.33 = (bf16[3,2,8,8,512]{4,3,0,2,1:T(8,128)(2,1)}, bf16[3,2,8,8,512]{4,3,0,2,1:T(8,128)(2,1)S(1)}, u32[]{:S(2)}) copy-start(bf16[3,2,8,8,512]{4,3,0,2,1:T(8,128)(2,1)S(1)} %copy.187) | copy-start | bytes 1179652
  461.0 104.0 %reduce-scatter.25.cloned.1.call-start = ((), (), s32[]{:S(2)}) async-start(), calls=%async_computation.24 | async-start | bytes 327680 | tf_op jit(solution)/shard_map/reduce_scatter | solution.py:307
  468.6 98.0 %reduce-scatter.29.cloned.1.call-start = ((), (), s32[]{:S(2)}) async-start(), calls=%async_computation.26 | async-start | bytes 327680 | tf_op jit(solution)/shard_map/reduce_scatter | solution.py:313
  473.5 94.6 %reduce-scatter.31.cloned.1.call-start = ((), (), s32[]{:S(2)}) async-start(), calls=%async_computation.27 | async-start | bytes 327680 | tf_op jit(solution)/shard_map/reduce_scatter | solution.py:316
  477.8 97.1 %reduce-scatter.33.cloned.1.call-start = ((), (), s32[]{:S(2)}) async-start(), calls=%async_computation.28 | async-start | bytes 1310720 | tf_op jit(solution)/shard_map/reduce_scatter | solution.py:319
  501.9 6.2 copy-start.96
  519.6 82.5 %reduce-scatter.35.cloned.1.call-start = ((), (), s32[]{:S(2)}) async-start(), calls=%async_computation.29 | async-start | bytes 1310720 | tf_op jit(solution)/shard_map/reduce_scatter | solution.py:322
  526.9 153.0 %reduce-scatter.21.cloned.1.call-start = ((), (), s32[]{:S(2)}) async-start(), calls=%async_computation.22 | async-start | bytes 3538944 | tf_op jit(solution)/shard_map/reduce_scatter | solution.py:290
  533.1 223.7 %reduce-scatter.17.cloned.1.call-start = ((), (), s32[]{:S(2)}) async-start(), calls=%async_computation.20 | async-start | bytes 3538944 | tf_op jit(solution)/shard_map/reduce_scatter | solution.py:290
  538.8 294.7 %reduce-scatter.19.cloned.1.call-start = ((), (), s32[]{:S(2)}) async-start(), calls=%async_computation.21 | async-start | bytes 3538944 | tf_op jit(solution)/shard_map/reduce_scatter | solution.py:293
  544.0 366.3 %reduce-scatter.23.cloned.1.call-start = ((), (), s32[]{:S(2)}) async-start(), calls=%async_computation.23 | async-start | bytes 3538944 | tf_op jit(solution)/shard_map/reduce_scatter | solution.py:293
  549.0 483.2 %reduce-scatter.15.cloned.1.call-start = ((), (), s32[]{:S(2)}) async-start(), calls=%async_computation.19 | async-start | bytes 7077888 | tf_op jit(solution)/shard_map/reduce_scatter | solution.py:258
  556.3 596.7 %reduce-scatter.13.cloned.1.call-start = ((), (), s32[]{:S(2)}) async-start(), calls=%async_computation.16 | async-start | bytes 7077888 | tf_op jit(solution)/shard_map/reduce_scatter | solution.py:258
  563.4 193.4 %copy-start.7 = (bf16[2,192,1024]{2,1,0:T(8,128)(2,1)S(1)}, bf16[2,192,1024]{2,1,0:T(8,128)(2,1)}, u32[]{:S(2)}) copy-start(bf16[2,192,1024]{2,1,0:T(8,128)(2,1)} %param.23) | copy-start | bytes 2359300
  563.4 193.4 %copy-start.73 = (f32[1024]{0:T(1024)S(1)}, f32[1024]{0:T(1024)}, u32[]{:S(2)}) copy-start(f32[1024]{0:T(1024)} %param.24) | copy-start | bytes 12292
  563.4 193.4 %copy-start.79 = (f32[192]{0:T(256)S(1)}, f32[192]{0:T(256)}, u32[]{:S(2)}) copy-start(f32[192]{0:T(256)} %copy-done.78) | copy-start | bytes 2308
  563.4 193.4 %copy-start.81 = (f32[192]{0:T(256)S(1)}, f32[192]{0:T(256)}, u32[]{:S(2)}) copy-start(f32[192]{0:T(256)} %copy-done.80) | copy-start | bytes 2308
  563.4 195.0 %copy-start.92 = (f32[192]{0:T(256)S(1)}, f32[192]{0:T(256)}, u32[]{:S(2)}) copy-start(f32[192]{0:T(256)} %copy-done.91) | copy-start | bytes 2308
  563.4 195.0 %copy-start.90 = (f32[192]{0:T(256)S(1)}, f32[192]{0:T(256)}, u32[]{:S(2)}) copy-start(f32[192]{0:T(256)} %copy-done.89) | copy-start | bytes 2308
  563.4 346.9 %copy-start.72 = (f32[1024]{0:T(1024)S(1)}, f32[1024]{0:T(1024)}, u32[]{:S(2)}) copy-start(f32[1024]{0:T(1024)} %param.26) | copy-start | bytes 12292
  563.5 346.9 %copy-start.83 = (f32[192]{0:T(256)S(1)}, f32[192]{0:T(256)}, u32[]{:S(2)}) copy-start(f32[192]{0:T(256)} %copy-done.82) | copy-start | bytes 2308
  563.5 346.9 %copy-start.88 = (f32[192]{0:T(256)S(1)}, f32[192]{0:T(256)}, u32[]{:S(2)}) copy-start(f32[192]{0:T(256)} %copy-done.87) | copy-start | bytes 2308
  679.9 278.8 %copy-start.36 = (bf16[192,1024]{1,0:T(8,128)(2,1)S(1)}, bf16[192,1024]{1,0:T(8,128)(2,1)}, u32[]{:S(2)}) copy-start(bf16[192,1024]{1,0:T(8,128)(2,1)} %reduce-scatter.21.cloned.1.call-done) | copy-start | bytes 1179652
  910.3 48.4 %copy-start.38 = (bf16[192,1024]{1,0:T(8,128)(2,1)S(1)}, bf16[192,1024]{1,0:T(8,128)(2,1)}, u32[]{:S(2)}) copy-start(bf16[192,1024]{1,0:T(8,128)(2,1)} %reduce-scatter.23.cloned.1.call-done) | copy-start | bytes 1179652
  910.4 242.6 %copy-start.39 = (bf16[192,1024]{1,0:T(8,128)(2,1)S(1)}, bf16[192,1024]{1,0:T(8,128)(2,1)}, u32[]{:S(2)}) copy-start(bf16[192,1024]{1,0:T(8,128)(2,1)} %reduce-scatter.17.cloned.1.call-done) | copy-start | bytes 1179652
  910.4 242.6 %copy-start.40 = (bf16[192,1024]{1,0:T(8,128)(2,1)S(1)}, bf16[192,1024]{1,0:T(8,128)(2,1)}, u32[]{:S(2)}) copy-start(bf16[192,1024]{1,0:T(8,128)(2,1)} %reduce-scatter.19.cloned.1.call-done) | copy-start | bytes 1179652
  (83 other events, 249.5 us)
Sparse Core Ops, SparseCore 0:
  13.6 62.7 all-gather.18
  78.5 58.6 all-gather.10
  139.4 58.6 all-gather.24
  200.2 58.6 all-gather.22
  260.3 15.3 all-gather.14
  277.8 60.1 all-gather.12
  340.2 58.8 all-gather.20
  400.6 15.4 all-gather.16
  461.2 19.0 reduce-scatter.26
  482.5 20.0 reduce-scatter.24
  505.1 20.0 reduce-scatter.28
  527.4 20.0 reduce-scatter.30
  550.0 24.7 reduce-scatter.32
  577.2 24.8 reduce-scatter.34
  605.5 74.3 reduce-scatter.20
  683.3 73.4 reduce-scatter.16
  760.2 73.2 reduce-scatter.18
  836.9 73.3 reduce-scatter.22
  913.9 118.2 reduce-scatter.14
  1035.6 117.2 reduce-scatter.12
where the time goes:
time: 1180 us; the launch traced here: 1160 us
  waiting for transfers between devices  616 us (52%)
  matrix products  281 us (24%)
  local copies, waits for them, and re-layouts  104 us (9%)
  blocking collectives  69.1 us (6%)
  other arithmetic  58.9 us (5%)
  loops' own time  18.2 us (2%)
  between operations  16 us (1%)
    reduce_scatter x2, waiting for transfers between devices, local(): lax.psum_scatter(jnp.dot(context_rows, w_out, preferred_element_type=jnp....  193 us
    reduce_scatter x2, waiting for transfers between devices, local(): lax.psum_scatter(part_one.astype(jnp.bfloat16), 'mp', scatter_dimension=0...  153 us
    reduce_scatter x2, waiting for transfers between devices, local(): lax.psum_scatter(part_two.astype(jnp.bfloat16), 'mp', scatter_dimension=0...  152 us
    all_gather x2, waiting for transfers between devices, local(): lax.all_gather(normed_one.astype(jnp.bfloat16), 'mp', axis=0, tiled=True)  83.5 us
    dot_general x24, matrix products, block_step(): jnp.einsum('ugy,uky->ugk', block_of_queries, block_of_keys, precision=max...  55 us
    dot_general x24, matrix products, block_step(): jnp.einsum('hqk,hkd->hqd', attention_scores, value_block, precision=maxim...  54.8 us
    psum x1, blocking collectives, local(): lax.psum((norm_sums[0], norm_sums[1], norm_sums[2], norm_sums[3]), ('seq'...  43.5 us
    dot_general x12, matrix products, contract_cols(): lax.dot_general(left_side, right_side, (((1,), (1,)), ((), ())), preferre...  32.5 us
  transfers between devices with their start and end apart: 20, of which 10 were waited for; matrix products, arithmetic and copies ran while one was open for 36% of the time, Pallas kernels for 0%

commit v1 on v0

--- a/solution.py
+++ b/solution.py
@@ -1,14 +1,25 @@
-from functools import partial
+import functools
 import math
 
 import jax
 import jax.numpy as jnp
+import numpy as np
 from jax import lax
+from jax.experimental import pallas as pl
+from jax.experimental.pallas import tpu as pltpu
 from jax.sharding import PartitionSpec as P
 
 HEAD_DIM = 64
 ROT = 16
 FEATS = 64
+STATE_ROWS = 80
+AXES = ("seq", "mp")
+BF16 = jnp.bfloat16
+F32 = jnp.float32
+VMEM_LIMIT = 56 * 1024 * 1024
+NN = (((1,), (0,)), ((), ()))
+NT = (((1,), (1,)), ((), ()))
+TN = (((0,), (0,)), ((), ()))
 
 
 def prime_list(wanted):
@@ -188,7 +199,7 @@
     return jnp.transpose(joined, (1, 0, 2)).reshape(number_of_tokens, head_count * HEAD_DIM)
 
 
-def local(
+def plain_local(
     tokens,
     ln1_gain,
     ln1_bias,
@@ -245,7 +256,7 @@
         key_raw = jnp.dot(group_one, w_key, preferred_element_type=jnp.float32)
         value_raw = jnp.dot(group_one, w_value, preferred_element_type=jnp.float32)
         segment, offset = doc_layout(lengths[micro_step, 0], group_rows)
-        attend = partial(
+        attend = functools.partial(
             local_attention, segment=segment, offset=offset, project=project, weighting=weighting
         )
         context, pull_attn = jax.vjp(attend, plain_query_rows, key_raw, value_raw)
@@ -340,7 +351,958 @@
     )
 
 
+def mm(left, right, dims=NN):
+    return lax.dot_general(left, right, dims, preferred_element_type=F32)
+
+
+def split(values):
+    high = values.astype(BF16)
+    return high, (values - high.astype(F32)).astype(BF16)
+
+
+def mm3(values, high, low, dims=NN):
+    first, second = split(values)
+    return mm(first, high, dims) + (mm(second, high, dims) + mm(first, low, dims))
+
+
+def lane_head(shape):
+    return lax.broadcasted_iota(jnp.int32, shape, len(shape) - 1) // HEAD_DIM
+
+
+def block_diag(state):
+    width = state.shape[1]
+    tall = jnp.concatenate([state] * (width // HEAD_DIM), axis=0)
+    rows = lax.broadcasted_iota(jnp.int32, tall.shape, 0) // HEAD_DIM
+    return jnp.where(rows == lane_head(tall.shape), tall, 0.0)
+
+
+def diag_blocks(full):
+    width = full.shape[1]
+    lanes = lane_head((HEAD_DIM, width))
+    total = jnp.zeros((HEAD_DIM, width), F32)
+    for head in range(width // HEAD_DIM):
+        part = full[head * HEAD_DIM : (head + 1) * HEAD_DIM, :]
+        total = total + jnp.where(lanes == head, part, 0.0)
+    return total
+
+
+def head_sums(values):
+    width = values.shape[1]
+    rows = lax.broadcasted_iota(jnp.int32, (width, width), 0) // HEAD_DIM
+    ones = jnp.where(rows == lane_head((width, width)), 1.0, 0.0).astype(BF16)
+    high, low = split(values)
+    return mm(high, ones) + mm(low, ones)
+
+
+def swap_halves(values):
+    width = values.shape[1]
+    half = ROT // 2
+    lane = lax.broadcasted_iota(jnp.int32, values.shape, 1) % HEAD_DIM
+    return jnp.where(
+        lane < half, pltpu.roll(values, width - half, 1), pltpu.roll(values, half, 1)
+    )
+
+
+def turn(values, cos, sin):
+    reps = values.shape[1] // cos.shape[1]
+    cosw = jnp.concatenate([cos] * reps, axis=1)
+    sinw = jnp.concatenate([sin] * reps, axis=1)
+    return values * cosw + swap_halves(values) * sinw
+
+
+def normalize(values):
+    centered = values - jnp.mean(values, axis=-1, keepdims=True)
+    variance = jnp.mean(centered * centered, axis=-1, keepdims=True)
+    scale = lax.rsqrt(variance + 1e-05)
+    return centered * scale, scale
+
+
+class Rows:
+    def __init__(self, scal, seq, chunk, docs):
+        rows = chunk // 2
+        self.here = scal[1] * chunk
+        low = self.here + scal[2] * rows
+        high = self.here + (1 - scal[2]) * rows - rows
+
+        def places(shape, axis):
+            count = lax.broadcasted_iota(jnp.int32, shape, axis)
+            return jnp.where(count < rows, count + low, count + high)
+
+        self.place = places((chunk, 1), 0)
+        self.across = places((1, chunk), 1)
+        self.start = jnp.zeros((chunk, 1), jnp.int32)
+        end = jnp.zeros((chunk, 1), jnp.int32)
+        base = 4 + seq * 2 * docs
+        for doc in range(docs):
+            first, last = scal[base + doc], scal[base + docs + doc]
+            inside = (self.place >= first) & (self.place < last)
+            self.start = jnp.where(inside, first, self.start)
+            end = jnp.where(inside, last, end)
+        self.came = self.start < self.here
+        self.goes = end > self.here + chunk
+
+    def mask(self):
+        return (self.across >= self.start) & (self.across <= self.place)
+
+
+def whole(array):
+    zeros = (0,) * array.ndim
+    return (array, tuple(array.shape), lambda *_: zeros)
+
+
+def by_seq(array):
+    rest = (0,) * (array.ndim - 1)
+    return (array, (1,) + tuple(array.shape[1:]), lambda i, s: (i,) + rest)
+
+
+def own_seq(array):
+    rest, most = (0,) * (array.ndim - 1), array.shape[0] - 1
+    return (array, (1,) + tuple(array.shape[1:]), lambda i, s: (jnp.minimum(i, most),) + rest)
+
+
+def away_seq(array):
+    rest, count = (0,) * (array.ndim - 1), array.shape[0]
+    return (
+        array, (1,) + tuple(array.shape[1:]), lambda i, s: (jnp.maximum(i - count, 0),) + rest
+    )
+
+
+def new(shape, kind):
+    return jax.ShapeDtypeStruct(shape, kind)
+
+
+def call(name, body, scal, grid, ins, outs, scratch=()):
+    return pl.pallas_call(
+        body,
+        name=name,
+        grid_spec=pltpu.PrefetchScalarGridSpec(
+            num_scalar_prefetch=1,
+            grid=grid or (1,),
+            in_specs=[pl.BlockSpec(block, index) for _, block, index in ins],
+            out_specs=[pl.BlockSpec(block, index) for _, block, index in outs],
+            scratch_shapes=list(scratch),
+        ),
+        out_shape=[array for array, _, _ in outs],
+        compiler_params=pltpu.CompilerParams(
+            dimension_semantics=("arbitrary",) * max(len(grid), 1), vmem_limit_bytes=VMEM_LIMIT
+        ),
+    )(scal, *[array for array, _, _ in ins])
+
+
+class Shape:
+    def __init__(self, pairs, chunks, dim, half_units, half_ff, chunk, docs):
+        self.pairs, self.chunks, self.dim = pairs, chunks, dim
+        self.hu, self.hf, self.chunk, self.docs = half_units, half_ff, chunk, docs
+        self.dp = dim // pairs
+        self.width, self.ff = chunks * half_units, chunks * half_ff
+
+    def cols(self, scal, slot):
+        start = ((scal[0] + slot) % self.pairs) * self.dp
+        return pl.ds(pl.multiple_of(start, 128), self.dp)
+
+
+def fill_rows(sh, target, blocks, first, size, at):
+    for slot in range(sh.pairs):
+        for j in range(sh.chunks):
+            part = blocks[slot * sh.chunks + j][first : first + size, :]
+            target[slot, at + j * size : at + (j + 1) * size, :] = part
+
+
+def pack_body(scal, q, k, v, out, up, down, keep_a, send_a, send_u, send_d):
+    low = scal[3] == 0
+    parts_keep, parts_send = [], []
+    for ref in (q, k, v):
+        flat = jnp.transpose(ref[...].astype(F32))
+        half = flat.shape[0] // 2
+        parts_keep.append(jnp.where(low, flat[:half], flat[half:]))
+        parts_send.append(jnp.where(low, flat[half:], flat[:half]))
+    flat = out[...].astype(F32)
+    half = flat.shape[0] // 2
+    parts_keep.append(jnp.where(low, flat[:half], flat[half:]))
+    parts_send.append(jnp.where(low, flat[half:], flat[:half]))
+    keep_a[...] = jnp.concatenate(parts_keep, 0).astype(BF16)
+    send_a[...] = jnp.concatenate(parts_send, 0).astype(BF16)
+    half = up.shape[1] // 2
+    send_u[...] = jnp.where(low, up[:, half:], up[:, :half])
+    half = down.shape[0] // 2
+    send_d[...] = jnp.where(low, down[half:, :], down[:half, :])
+
+
+def join_a_body(scal, keep, got, block):
+    low = scal[3] == 0
+    size = keep.shape[1]
+    block[:, :size] = jnp.where(low, keep[...], got[...])
+    block[:, size:] = jnp.where(low, got[...], keep[...])
+
+
+def join_u_body(scal, up, got, block):
+    low = scal[3] == 0
+    rows, half = up.shape[0], up.shape[1] // 2
+    keep = jnp.where(low, up[:, :half], up[:, half:])
+    block[:rows, :] = jnp.where(low, keep, got[...])
+    block[rows:, :] = jnp.where(low, got[...], keep)
+
+
+def join_d_body(scal, down, got, block):
+    low = scal[3] == 0
+    cols, half = down.shape[1], down.shape[0] // 2
+    keep = jnp.where(low, down[:half, :], down[half:, :])
+    block[:, :cols] = jnp.where(low, keep, got[...])
+    block[:, cols:] = jnp.where(low, got[...], keep)
+
+
+def norm_body(scal, own, away, g1, b1, g2, b2, one, two):
+    own_turn = pl.program_id(0) < pl.num_programs(0) // 2
+    x = jnp.where(own_turn, own[0], away[0]).astype(F32)
+    n, _ = normalize(x)
+    one[0] = (n * g1[...] + b1[...]).astype(BF16)
+    two[0] = (n * g2[...] + b2[...]).astype(BF16)
+
+
+def attend_body(sh, scal, normed, cos, sin, ph, pw, wts, *refs):
+    blocks = refs[: sh.pairs * sh.chunks]
+    fq_out, fk_out, v_out, num_out, den_out, st_out, wt = refs[sh.pairs * sh.chunks :]
+    width, seq = sh.width, pl.program_id(0)
+
+    @pl.when(seq == 0)
+    def _():
+        for kind in range(3):
+            fill_rows(sh, wt, blocks, kind * sh.hu, sh.hu, kind * width)
+
+    qkv = mm(normed[0, :, sh.cols(scal, 0)], wt[0], NT)
+    for slot in range(1, sh.pairs):
+        qkv = qkv + mm(normed[0, :, sh.cols(scal, slot)], wt[slot], NT)
+
+    def feats(values):
+        return jnp.exp(mm3(turn(values, cos[0], sin[0]), ph[...], pw[...]))
+
+    fqb = (feats(qkv[:, :width]) * wts[...]).astype(BF16)
+    fk = feats(qkv[:, width : 2 * width])
+    fkb = fk.astype(BF16)
+    v = qkv[:, 2 * width :]
+    vb = v.astype(BF16)
+    fq_out[0] = fqb
+    fk_out[0] = fkb
+    v_out[0] = v
+    rows = Rows(scal, seq, sh.chunk, sh.docs)
+    mask = rows.mask()
+    lanes = lane_head(vb.shape)
+    num = jnp.zeros(vb.shape, F32)
+    den = jnp.zeros(vb.shape, F32)
+    for head in range(width // HEAD_DIM):
+        mine = lanes == head
+        scores = mm(jnp.where(mine, fqb, 0), fkb, NT)
+        scores = jnp.where(mask, scores, 0.0).astype(BF16)
+        both = mm(scores, jnp.where(mine, vb, 1))
+        num = jnp.where(mine, both, num)
+        den = jnp.where(mine, pltpu.roll(both, HEAD_DIM, 1), den)
+    num_out[0] = num
+    den_out[0] = den
+    kept = jnp.where(rows.goes, fk, 0.0)
+    store_state(sh, scal, st_out, mm(kept.astype(BF16), vb, TN), kept)
+
+
+def store_state(sh, scal, st_out, sums, totals):
+    tail = jnp.broadcast_to(
+        jnp.sum(totals, axis=0, keepdims=True), (STATE_ROWS - HEAD_DIM, sh.width)
+    )
+    state = jnp.concatenate([diag_blocks(sums), tail], axis=0)
+    st_out[0] = pltpu.roll(state, scal[1] * sh.hu, 1)
+
+
+def load_state(sh, scal, carry):
+    state = pltpu.roll(carry[0], (sh.width - scal[1] * sh.hu) % sh.width, 1)
+    return state[:HEAD_DIM], state[HEAD_DIM : HEAD_DIM + 1]
+
+
+def up_body(sh, scal, normed, *refs):
+    blocks = refs[: sh.pairs * sh.chunks]
+    act_out, slope_out, wu = refs[sh.pairs * sh.chunks :]
+
+    @pl.when(pl.program_id(0) == 0)
+    def _():
+        for slot in range(sh.pairs):
+            for j in range(sh.chunks):
+                wu[slot, :, j * sh.hf : (j + 1) * sh.hf] = blocks[slot * sh.chunks + j][...]
+
+    hidden = mm(normed[0, :, sh.cols(scal, 0)], wu[0])
+    for slot in range(1, sh.pairs):
+        hidden = hidden + mm(normed[0, :, sh.cols(scal, slot)], wu[slot])
+    cdf = 0.5 + 0.5 * lax.erf(hidden * math.sqrt(0.5))
+    act_out[0] = (hidden * cdf).astype(BF16)
+    bell = jnp.exp(-0.5 * hidden * hidden) * math.sqrt(0.5 / math.pi)
+    slope_out[0] = (cdf + hidden * bell).astype(BF16)
+
+
+def fill_out(sh, blocks_a, blocks_d, wo, wd):
+    fill_rows(sh, wo, blocks_a, 3 * sh.hu, sh.hu, 0)
+    fill_rows(sh, wd, blocks_d, 0, sh.hf, 0)
+
+
+def branch_body(sh, scal, num, den, fq, carry, act, *refs):
+    count = sh.pairs * sh.chunks
+    blocks_a, blocks_d = refs[:count], refs[count : 2 * count]
+    ctx_out, rden_out, own_out, away_out, wo, wd = refs[2 * count :]
+    seq = pl.program_id(0)
+
+    @pl.when(seq == 0)
+    def _():
+        fill_out(sh, blocks_a, blocks_d, wo, wd)
+
+    fqb = fq[0]
+    sums, totals = load_state(sh, scal, carry)
+    more_num = mm(fqb, block_diag(sums).astype(BF16))
+    more_den = head_sums(fqb.astype(F32) * totals)
+    came = Rows(scal, seq, sh.chunk, sh.docs).came
+    inverse = 1.0 / (den[0] + jnp.where(came, more_den, 0.0))
+    ctx = (num[0] + jnp.where(came, more_num, 0.0)) * inverse
+    ctx_out[0] = ctx
+    rden_out[0] = inverse
+    ctxb = ctx.astype(BF16)
+    half = pl.num_programs(0) // 2
+    for slot in range(sh.pairs):
+        part = (mm(act[0], wd[slot]) + mm(ctxb, wo[slot])).astype(BF16)
+
+        @pl.when(seq < half)
+        def _():
+            own_out[0, :, sh.cols(scal, slot)] = part
+
+        @pl.when(seq >= half)
+        def _():
+            away_out[0, :, sh.cols(scal, slot)] = part
+
+
+def pick(own, away, scal, sh, slot):
+    first = pl.program_id(0) < pl.num_programs(0) // 2
+    cols = sh.cols(scal, slot)
+    return jnp.where(first, own[0, :, cols], away[0, :, cols])
+
+
+def hidden_body(sh, scal, own, away, slope, *refs):
+    blocks = refs[: sh.pairs * sh.chunks]
+    out, wd = refs[sh.pairs * sh.chunks :]
+
+    @pl.when(pl.program_id(0) == 0)
+    def _():
+        fill_rows(sh, wd, blocks, 0, sh.hf, 0)
+
+    grad = mm(pick(own, away, scal, sh, 0), wd[0], NT)
+    for slot in range(1, sh.pairs):
+        grad = grad + mm(pick(own, away, scal, sh, slot), wd[slot], NT)
+    out[0] = (grad * slope[0].astype(F32)).astype(BF16)
+
+
+def back_body(sh, scal, own, away, fq, fk, vals, ctx, rden, carry, cos, sin, ph, pw, *refs):
+    blocks = refs[: sh.pairs * sh.chunks]
+    dq_out, dk_out, dv_out, st_out, wo = refs[sh.pairs * sh.chunks :]
+    width, seq = sh.width, pl.program_id(0)
+
+    @pl.when(seq == 0)
+    def _():
+        fill_rows(sh, wo, blocks, 3 * sh.hu, sh.hu, 0)
+
+    gctx = mm(pick(own, away, scal, sh, 0), wo[0], NT)
+    for slot in range(1, sh.pairs):
+        gctx = gctx + mm(pick(own, away, scal, sh, slot), wo[slot], NT)
+    inverse = rden[0]
+    dnum = gctx * inverse
+    dden = -head_sums(gctx * ctx[0]) * inverse
+    fqb, fkb, v = fq[0], fk[0], vals[0]
+    rows = Rows(scal, seq, sh.chunk, sh.docs)
+    mask = rows.mask()
+    lanes = lane_head(v.shape)
+    lane = lax.broadcasted_iota(jnp.int32, v.shape, 1) % HEAD_DIM
+    dn_high, dn_low = split(dnum)
+    v_high, v_low = split(v)
+    dd_high = dden.astype(BF16).astype(F32)
+    roll = lambda values, steps: pltpu.roll(values, steps * HEAD_DIM, 1)
+    den_part = jnp.where(lane == 0, dd_high, jnp.where(lane == 1, dden - dd_high, 0.0))
+    left = [
+        dn_high,
+        roll(dn_low.astype(F32), 1).astype(BF16),
+        roll(den_part, 2).astype(BF16),
+        roll(dn_high.astype(F32), 3).astype(BF16),
+    ]
+    right = [
+        v_high,
+        roll(v_high.astype(F32), 1).astype(BF16),
+        jnp.ones(v.shape, BF16),
+        roll(v_low.astype(F32), 3).astype(BF16),
+    ]
+
+    def lay_out(parts, head):
+        group = (lanes - head) & 3
+        low = jnp.where(group == 0, parts[0], parts[1])
+        high = jnp.where(group == 2, parts[2], parts[3])
+        return jnp.where(group < 2, low, high)
+
+    dfq = jnp.zeros(v.shape, F32)
+    dfk = jnp.zeros(v.shape, F32)
+    dv = jnp.zeros(v.shape, F32)
+    for head in range(width // HEAD_DIM):
+        mine = lanes == head
+        dscores = mm(lay_out(left, head), lay_out(right, head), NT)
+        dscores = jnp.where(mask, dscores, 0.0).astype(BF16)
+        scores = mm(jnp.where(mine, fqb, 0), fkb, NT)
+        scores = jnp.where(mask, scores, 0.0).astype(BF16)
+        dfq = jnp.where(mine, mm(dscores, fkb), dfq)
+        dfk = jnp.where(mine, mm(dscores, fqb, TN), dfk)
+        dv = jnp.where(mine, mm(scores, dn_high, TN), dv)
+    sums, totals = load_state(sh, scal, carry)
+    more = mm(dn_high, block_diag(sums).astype(BF16), NT) + dden * totals
+    dfq = dfq + jnp.where(rows.came, more, 0.0)
+    fqf = fqb.astype(F32)
+    used = jnp.where(rows.came, fqf, 0.0)
+    store_state(sh, scal, st_out, mm(used.astype(BF16), dn_high, TN), used * dden)
+    turned = mm3(dfq * fqf, ph[...], pw[...], NT)
+    dq_out[0] = turn(turned, cos[0], -sin[0]).astype(BF16)
+    dk_out[0] = dfk
+    dv_out[0] = dv
+
+
+def last_body(sh, scal, dfk, dv, fk, vals, carry, cos, sin, ph, pw, dk_out, dv_out):
+    fkb = fk[0]
+    sums, totals = load_state(sh, scal, carry)
+    state = block_diag(sums).astype(BF16)
+    goes = Rows(scal, pl.program_id(0), sh.chunk, sh.docs).goes
+    more_k = mm(vals[0].astype(BF16), state, NT) + totals
+    total_k = dfk[0] + jnp.where(goes, more_k, 0.0)
+    dv_out[0] = (dv[0] + jnp.where(goes, mm(fkb, state), 0.0)).astype(BF16)
+    turned = mm3(total_k * fkb.astype(F32), ph[...], pw[...], NT)
+    dk_out[0] = turn(turned, cos[0], -sin[0]).astype(BF16)
+
+
+def down_grad_body(sh, with_got, scal, act, ctx, own, away, *refs):
+    half = own.shape[0]
+    scratch = refs[-1]
+    j = pl.program_id(0)
+
+    @pl.when(j == 0)
+    def _():
+        scratch[...] = mm(ctx[:half, :].astype(BF16), own[...], TN) + mm(
+            ctx[half:, :].astype(BF16), away[...], TN
+        )
+
+    grad = mm(act[:half, :], own[...], TN) + mm(act[half:, :], away[...], TN)
+    low = scratch[pl.ds(pl.multiple_of(j * sh.hu, 8), sh.hu), :]
+    store_block(with_got, refs[:-1], (grad, low), j)
+
+
+def store_block(with_got, refs, parts, j):
+    at = 0
+    for part in parts:
+        rows = slice(at, at + part.shape[0])
+        at += part.shape[0]
+        if not with_got:
+            refs[0][0, rows, :] = part.astype(BF16)
+            continue
+        value = (part + refs[0][0, rows, :].astype(F32)).astype(BF16)
+        for step, out in enumerate(refs[1:]):
+
+            @pl.when(j == step)
+            def _():
+                out[rows, :] = value
+
+
+def up_grad_body(sh, with_got, scal, normed, grad, *refs):
+    store_block(with_got, refs, (mm(normed[...], grad[...], TN),), pl.program_id(0))
+
+
+def qkv_grad_body(sh, with_got, scal, dq, dk, dv, normed, *refs):
+    for kind, ref in enumerate((dq, dk, dv)):
+        refs[-1][kind] = mm(ref[...], normed[...], TN)
+    for j in range(sh.chunks):
+        rows = slice(j * sh.hu, (j + 1) * sh.hu)
+        value = jnp.concatenate([refs[-1][kind, rows, :] for kind in range(3)], axis=0)
+        if with_got:
+            refs[1 + j][...] = (value + refs[0][j].astype(F32)).astype(BF16)
+        else:
+            refs[0][j] = value.astype(BF16)
+
+
+def rows_grad_body(sh, scal, dq, dk, dv, gh, own, away, g1, g2, *refs):
+    count = sh.pairs * sh.chunks
+    blocks_a, blocks_u = refs[:count], refs[count : 2 * count]
+    own_out, away_out, sums, wt, wu, n_ref = refs[2 * count :]
+    seq = pl.program_id(0)
+    half = pl.num_programs(0) // 2
+
+    @pl.when(seq == 0)
+    def _():
+        for kind in range(3):
+            fill_rows(sh, wt, blocks_a, kind * sh.hu, sh.hu, kind * sh.width)
+        for slot in range(sh.pairs):
+            for j in range(sh.chunks):
+                wu[slot, :, j * sh.hf : (j + 1) * sh.hf] = blocks_u[slot * sh.chunks + j][...]
+        sums[...] = jnp.zeros(sums.shape, F32)
+
+    x = jnp.where(seq < half, own[0], away[0]).astype(F32)
+    n_ref[...] = normalize(x)[0]
+    for slot in range(sh.pairs):
+        cols = sh.cols(scal, slot)
+        one = mm(dq[0], wt[slot, : sh.width, :])
+        one = one + mm(dk[0], wt[slot, sh.width : 2 * sh.width, :])
+        one = one + mm(dv[0], wt[slot, 2 * sh.width :, :])
+        two = mm(gh[0], wu[slot], NT)
+        n = n_ref[:, cols]
+        for at, value in enumerate((one * n, one, two * n, two)):
+            line = slice(at, at + 1)
+            sums[line, cols] = sums[line, cols] + jnp.sum(value, axis=0, keepdims=True)
+        e = (one * g1[:, cols] + two * g2[:, cols]).astype(BF16)
+
+        @pl.when(seq < half)
+        def _():
+            own_out[0, :, cols] = e
+
+        @pl.when(seq >= half)
+        def _():
+            away_out[0, :, cols] = e
+
+
+def tokens_grad_body(scal, mine, got, tokens, cot, out):
+    e = mine[0].astype(F32) + got[0].astype(F32)
+    n, scale = normalize(tokens[0].astype(F32))
+    shift = jnp.mean(e, axis=-1, keepdims=True) + n * jnp.mean(e * n, axis=-1, keepdims=True)
+    out[0] = cot[0].astype(F32) + scale * (e - shift)
+
+
+def cut_cols_body(scal, first, second, keep, send):
+    total = (first[...].astype(F32) + second[...].astype(F32)).astype(BF16)
+    half = total.shape[1] // 2
+    low = scal[3] == 0
+    keep[...] = jnp.where(low, total[:, :half], total[:, half:])
+    send[...] = jnp.where(low, total[:, half:], total[:, :half])
+
+
+def cut_rows_body(scal, first, second, keep, send):
+    total = (first[...].astype(F32) + second[...].astype(F32)).astype(BF16)
+    half = total.shape[0] // 2
+    low = scal[3] == 0
+    keep[...] = jnp.where(low, total[:half], total[half:])
+    send[...] = jnp.where(low, total[half:], total[:half])
+
+
+def end_down_body(sh, scal, keep, got, down, out):
+    low = scal[3] == 0
+    mine, other = keep[...].astype(F32), got[...].astype(F32)
+    first, second = jnp.where(low, mine, other), jnp.where(low, other, mine)
+    down[: sh.hf, :] = first[: sh.hf]
+    down[sh.hf :, :] = second[: sh.hf]
+    out[: sh.hu, :] = first[sh.hf :]
+    out[sh.hu :, :] = second[sh.hf :]
+
+
+def end_up_body(sh, scal, keep, got, up):
+    low = scal[3] == 0
+    mine, other = keep[...].astype(F32), got[...].astype(F32)
+    up[:, : sh.hf] = jnp.where(low, mine, other)
+    up[:, sh.hf :] = jnp.where(low, other, mine)
+
+
+def end_qkv_body(sh, scal, keep, got, *outs):
+    low = scal[3] == 0
+    mine, other = keep[...].astype(F32), got[...].astype(F32)
+    first, second = jnp.where(low, mine, other), jnp.where(low, other, mine)
+    for kind, out in enumerate(outs):
+        rows = slice(kind * sh.hu, (kind + 1) * sh.hu)
+        out[...] = jnp.transpose(jnp.concatenate([first[rows], second[rows]], axis=0))
+
+
+class Layout:
+    def __init__(self):
+        self.seqs, self.parts = lax.axis_size("seq"), lax.axis_size("mp")
+        self.pairs, self.chunks = self.seqs // 2, self.parts // 2
+        seq, part = lax.axis_index("seq"), lax.axis_index("mp")
+        self.pair, self.core = seq // 2, seq % 2
+        self.hi, self.lo = part // 2, part % 2
+
+    def move(self, values, rule):
+        links = []
+        for seq in range(self.seqs):
+            for part in range(self.parts):
+                there = rule(seq // 2, seq % 2, part // 2, part % 2)
+                if there is not None:
+                    pair, core, hi, lo = there
+                    goal = (pair * 2 + core) * self.parts + hi * 2 + lo
+                    links.append((seq * self.parts + part, goal))
+        return lax.ppermute(values, AXES, links)
+
+    def core_swap(self, values):
+        return self.move(values, lambda p, c, h, l: (p, 1 - c, h, l))
+
+    def lo_swap(self, values):
+        return self.move(values, lambda p, c, h, l: (p, c, h, 1 - l))
+
+    def pair_step(self, values, way):
+        return self.move(values, lambda p, c, h, l: ((p + way) % self.pairs, c, h, l))
+
+    def hi_step(self, values, way):
+        return self.move(values, lambda p, c, h, l: (p, c, (h + way) % self.chunks, l))
+
+
+def gather_blocks(lay, block):
+    ring = [block]
+    for _ in range(lay.chunks - 1):
+        ring.append(lay.hi_step(ring[-1], -1))
+    blocks = list(ring)
+    for _ in range(lay.pairs - 1):
+        ring = [lay.pair_step(part, -1) for part in ring]
+        blocks += ring
+    return blocks
+
+
+def combine_states(lay, local, straddles, size, backward):
+    reach = local
+    found = jnp.zeros_like(local)
+    step = 1
+    while step < lay.chunks:
+        base = (lay.hi // (2 * step)) * (2 * step)
+        upper = (lay.hi & step) > 0
+        middle = (base + step) * size
+        last = step * 2 >= lay.chunks
+
+        def rule(p, c, h, l, step=step, last=last):
+            sender = ((h & step) == 0) != backward
+            return (p, c, h ^ step, l) if sender or not last else None
+
+        got = lay.move(reach.astype(BF16), rule).astype(F32)
+        scale = lambda edge: straddles(middle, edge)[:, None, None]
+        if backward:
+            here = (lay.hi + 1) * size
+            keeps = jnp.where(upper, 0.0, scale(here))
+            edge = base * size
+        else:
+            here = lay.hi * size
+            keeps = jnp.where(upper, scale(here), 0.0)
+            edge = (base + 2 * step) * size
+        found = found + keeps * got
+        if not last:
+            far = scale(edge)
+            mine_far = upper if backward else jnp.logical_not(upper)
+            reach = jnp.where(mine_far, far * reach + got, reach + far * got)
+        step *= 2
+    return found
+
+
+def erf_inverse(target):
+    low, high = -6.0, 6.0
+    for _ in range(60):
+        middle = 0.5 * (low + high)
+        low, high = (middle, high) if math.erf(middle) < target else (low, middle)
+    guess = 0.5 * (low + high)
+    for _ in range(3):
+        gap = math.erf(guess) - target
+        guess -= gap * math.exp(guess * guess) * math.sqrt(math.pi) / 2.0
+    return guess
+
+
+@functools.lru_cache(None)
+def tables(heads):
+    primes = prime_list(HEAD_DIM)
+    points = np.zeros((FEATS, HEAD_DIM))
+    for row in range(FEATS):
+        for col in range(HEAD_DIM):
+            share = min(max((row + 0.5) * math.sqrt(primes[col]) % 1.0, 0.001), 0.999)
+            points[row, col] = math.sqrt(2.0) * erf_inverse(2.0 * float(np.float32(share)) - 1.0)
+    cells = np.arange(HEAD_DIM)
+    cosine = np.cos(np.pi * (cells[None, :] + 0.5) * cells[:, None] / HEAD_DIM)
+    cosine = cosine * math.sqrt(2.0 / HEAD_DIM)
+    cosine[0] *= math.sqrt(0.5)
+    project = np.kron(np.eye(heads), (points @ cosine).T / math.sqrt(HEAD_DIM))
+    project = project.astype(np.float32)
+    high = project.astype(BF16)
+    low = (project - high.astype(np.float32)).astype(BF16)
+    weighting = 1.0 / (1.0 + np.sum(points * points, axis=1) / HEAD_DIM)
+    return high, low, np.tile(weighting, heads)[None, :].astype(np.float32)
+
+
+def team_local(
+    tokens,
+    ln1_gain,
+    ln1_bias,
+    ln2_gain,
+    ln2_bias,
+    q_weight,
+    k_weight,
+    value_weight,
+    out_weight,
+    up_weight,
+    down_weight,
+    lengths,
+    cotangent,
+):
+    lay = Layout()
+    micro, rows, dim = tokens.shape
+    drows, units = q_weight.shape
+    docs = lengths.shape[2]
+    chunk = 2 * rows
+    half_units, half_ff = units // 2, up_weight.shape[1] // 2
+    sh = Shape(lay.pairs, lay.chunks, dim, half_units, half_ff, chunk, docs)
+    width, ff, dp = sh.width, sh.ff, sh.dp
+    count = 2 * micro
+    total = count * chunk
+    whole_rows = lambda array: array.reshape(total, array.shape[-1])
+    bind = lambda body, *first: functools.partial(body, *first)
+    gains = [vec.reshape(1, dim) for vec in (ln1_gain, ln1_bias, ln2_gain, ln2_bias)]
+
+    own_lengths = lengths[:, 0]
+    table = jnp.stack([own_lengths, lay.core_swap(own_lengths)]).reshape(count, docs)
+    ends = jnp.cumsum(table, axis=1)
+    starts = ends - table
+    scal = jnp.concatenate(
+        [
+            jnp.stack([lay.pair, lay.hi, lay.lo, lay.core]).astype(jnp.int32),
+            jnp.concatenate([starts, ends], axis=1).reshape(-1).astype(jnp.int32),
+        ]
+    )
+    places = jnp.stack([lay.core, lay.core, lay.core, lay.core]).astype(jnp.int32)
+    core_only = places
+
+    block_shape = [(4 * half_units, drows), (drows, half_ff), (half_ff, drows)]
+    keep_a, send_a, send_u, send_d = call(
+        "pack", pack_body, core_only, (),
+        [whole(w) for w in (q_weight, k_weight, value_weight, out_weight, up_weight, down_weight)],
+        [whole(new(shape, BF16)) for shape in [block_shape[0]] + block_shape],
+    )
+    got_a = lay.core_swap(send_a)
+    tokens_beside = lay.lo_swap(tokens)
+    (block,) = call(
+        "join_a", join_a_body, core_only, (), [whole(keep_a), whole(got_a)],
+        [whole(new((4 * half_units, 2 * drows), BF16))],
+    )
+    blocks_a = gather_blocks(lay, block)
+    got_u = lay.core_swap(send_u)
+    (block,) = call(
+        "join_u", join_u_body, core_only, (), [whole(up_weight), whole(got_u)],
+        [whole(new((2 * drows, half_ff), BF16))],
+    )
+    blocks_u = gather_blocks(lay, block)
+    got_d = lay.core_swap(send_d)
+    (block,) = call(
+        "join_d", join_d_body, core_only, (), [whole(down_weight), whole(got_d)],
+        [whole(new((half_ff, 2 * drows), BF16))],
+    )
+    blocks_d = gather_blocks(lay, block)
+    in_a, in_u, in_d = ([whole(b) for b in blocks] for blocks in (blocks_a, blocks_u, blocks_d))
+
+    def pair_rows(values, beside):
+        own = jnp.stack([values, beside], 1).reshape(micro, chunk, dim)
+        return own, lay.core_swap(own)
+
+    x_own, x_away = pair_rows(tokens, tokens_beside)
+    g_own, g_away = pair_rows(cotangent, lay.lo_swap(cotangent))
+
+    here = lay.hi * chunk
+    step = jnp.arange(rows, dtype=jnp.int32)
+    places = jnp.concatenate([here + lay.lo * rows + step, here + (1 - lay.lo) * rows + step])
+    start = jnp.zeros((count, chunk), jnp.int32)
+    for doc in range(docs):
+        first = starts[:, doc : doc + 1]
+        start = jnp.where(places[None, :] >= first, first, start)
+    offset = (places[None, :] - start).astype(F32)
+    lane = np.arange(128) % HEAD_DIM
+    turned = lane < ROT
+    inverse = np.where(turned, 10000.0 ** (-(lane % (ROT // 2)) * 2.0 / ROT), 0.0)
+    side = np.where(turned, np.where(lane < ROT // 2, -1.0, 1.0), 0.0)
+    angles = offset[:, :, None] * jnp.asarray(inverse, F32)[None, None, :]
+    cos = jnp.cos(angles)
+    sin = jnp.sin(angles) * jnp.asarray(side, F32)[None, None, :]
+    high, low, weighting = tables(width // HEAD_DIM)
+    maps = [whole(jnp.asarray(high)), whole(jnp.asarray(low))]
+    turns = [by_seq(cos), by_seq(sin)]
+
+    def straddles(first, second):
+        lower, higher = jnp.minimum(first, second), jnp.maximum(first, second)
+        return jnp.any((starts < lower) & (ends > higher), axis=1).astype(F32)
+
+    rows_new = lambda size, kind: by_seq(new((count, chunk, size), kind))
+    state_new = by_seq(new((count, STATE_ROWS, width), F32))
+    n_one, n_two = call(
+        "norms", norm_body, scal, (count,),
+        [own_seq(x_own), away_seq(x_away)] + [whole(vec) for vec in gains],
+        [rows_new(dim, BF16), rows_new(dim, BF16)],
+    )
+    fq, fk, vals, num, den, state = call(
+        "attend", bind(attend_body, sh), scal, (count,),
+        [by_seq(n_one)] + turns + maps + [whole(jnp.asarray(weighting))] + in_a,
+        [rows_new(width, BF16)] * 2 + [rows_new(width, F32)] * 3 + [state_new],
+        [pltpu.VMEM((sh.pairs, 3 * width, dp), BF16)],
+    )
+    carry = combine_states(lay, state, straddles, chunk, False)
+    act, slope = call(
+        "up", bind(up_body, sh), scal, (count,), [by_seq(n_two)] + in_u,
+        [rows_new(ff, BF16)] * 2, [pltpu.VMEM((sh.pairs, dp, ff), BF16)],
+    )
+    out_scratch = [
+        pltpu.VMEM((sh.pairs, width, dp), BF16), pltpu.VMEM((sh.pairs, ff, dp), BF16)
+    ]
+    halves_new = [
+        own_seq(new((micro, chunk, dim), BF16)), away_seq(new((micro, chunk, dim), BF16))
+    ]
+    ctx, rden, own, away = call(
+        "branch", bind(branch_body, sh), scal, (count,),
+        [by_seq(a) for a in (num, den, fq, carry, act)] + in_a + in_d,
+        [rows_new(width, F32)] * 2 + halves_new, out_scratch,
+    )
+
+    def team_sum(own, away):
+        got = lay.core_swap(away)
+        both = own.astype(F32) + got.astype(F32)
+        return both[:, :rows], lay.lo_swap(both[:, rows:].astype(BF16))
+
+    mine, got = team_sum(own, away)
+    mixed = (tokens.astype(F32) + mine + got.astype(F32)).astype(BF16)
+
+    (grad_hidden,) = call(
+        "hidden_grad", bind(hidden_body, sh), scal, (count,),
+        [own_seq(g_own), away_seq(g_away), by_seq(slope)] + in_d,
+        [rows_new(ff, BF16)], [pltpu.VMEM((sh.pairs, ff, dp), BF16)],
+    )
+    dq, dk_part, dv_part, dstate = call(
+        "attend_back", bind(back_body, sh), scal, (count,),
+        [own_seq(g_own), away_seq(g_away)]
+        + [by_seq(a) for a in (fq, fk, vals, ctx, rden, carry)] + turns + maps + in_a,
+        [rows_new(width, BF16), rows_new(width, F32), rows_new(width, F32), state_new],
+        [pltpu.VMEM((sh.pairs, width, dp), BF16)],
+    )
+    dcarry = combine_states(lay, dstate, straddles, chunk, True)
+    dk, dv = call(
+        "keys_back", bind(last_body, sh), scal, (count,),
+        [by_seq(a) for a in (dk_part, dv_part, fk, vals, dcarry)] + turns + maps,
+        [rows_new(width, BF16)] * 2,
+    )
+
+    def cols_of(array, slot):
+        pairs = sh.pairs
+        index = lambda *ids: (0, (ids[-1][0] + slot) % pairs)
+        return (array, (array.shape[0], dp), index)
+
+    def lanes_of(array, size):
+        return (array, (array.shape[0], size), lambda j, s: (0, j))
+
+    def block_of(array):
+        rest = tuple(array.shape[1:])
+        return (array, (1,) + rest, lambda j, s: (j,) + (0,) * len(rest))
+
+    def scatter(name, body, shape, ins, scratch, grid):
+        got = None
+        for slot in range(sh.pairs - 1, -1, -1):
+            stacked = new((sh.chunks,) + shape, BF16)
+            take = block_of if grid else whole
+            extra = [] if got is None else [take(got)]
+            final = slot == 0
+            outs = [whole(new(shape, BF16))] * sh.chunks if final else [take(stacked)]
+            parts = call(
+                name + str(slot), bind(body, sh, got is not None), scal, grid,
+                ins(slot) + extra, outs, scratch,
+            )
+            if not final:
+                got = lay.pair_step(parts[0], 1)
+        term = parts[sh.chunks - 1]
+        for j in range(sh.chunks - 2, -1, -1):
+            term = lay.hi_step(term, 1)
+            if j:
+                term = (term.astype(F32) + parts[j].astype(F32)).astype(BF16)
+        return term, parts[0]
+
+    g_rows = [g.reshape(total // 2, dim) for g in (g_own, g_away)]
+    grid = (sh.chunks,)
+    down_ends = scatter(
+        "down_grad", down_grad_body, (half_ff + half_units, dp),
+        lambda slot: [lanes_of(whole_rows(act), half_ff), whole(whole_rows(ctx))]
+        + [cols_of(g, slot) for g in g_rows],
+        [pltpu.VMEM((width, dp), F32)], grid,
+    )
+    up_ends = scatter(
+        "up_grad", up_grad_body, (dp, half_ff),
+        lambda slot: [cols_of(whole_rows(n_two), slot), lanes_of(whole_rows(grad_hidden), half_ff)],
+        [], grid,
+    )
+    qkv_ends = scatter(
+        "qkv_grad", qkv_grad_body, (3 * half_units, dp),
+        lambda slot: [whole(whole_rows(a)) for a in (dq, dk, dv)]
+        + [cols_of(whole_rows(n_one), slot)],
+        [pltpu.VMEM((3, width, dp), F32)], (),
+    )
+
+    own, away, sums = call(
+        "rows_grad", bind(rows_grad_body, sh), scal, (count,),
+        [by_seq(a) for a in (dq, dk, dv, grad_hidden)] + [own_seq(x_own), away_seq(x_away)]
+        + [whole(gains[0]), whole(gains[2])] + in_a + in_u,
+        halves_new + [whole(new((8, dim), F32))],
+        [
+            pltpu.VMEM((sh.pairs, 3 * width, dp), BF16),
+            pltpu.VMEM((sh.pairs, dp, ff), BF16),
+            pltpu.VMEM((chunk, dim), F32),
+        ],
+    )
+    mine, got = team_sum(own, away)
+    (grad_tokens,) = call(
+        "tokens_grad", tokens_grad_body, scal, (micro,),
+        [by_seq(a) for a in (mine, got, tokens, cotangent)],
+        [by_seq(new((micro, rows, dim), F32))],
+    )
+    sums = sums[:4]
+    sums = sums + lay.core_swap(sums)
+    sums = sums + lay.lo_swap(sums)
+    step = 1
+    while step < lay.pairs:
+        sums = sums + lay.move(sums, lambda p, c, h, l, step=step: (p ^ step, c, h, l))
+        step *= 2
+    step = 1
+    while step < lay.chunks:
+        sums = sums + lay.move(sums, lambda p, c, h, l, step=step: (p, c, h ^ step, l))
+        step *= 2
+
+    def trade(name, body, ends, shape):
+        keep, send = call(
+            name, body, core_only, (), [whole(part) for part in ends],
+            [whole(new(shape, BF16))] * 2,
+        )
+        return [whole(keep), whole(lay.core_swap(send))]
+
+    grad_down, grad_out = call(
+        "end_down", bind(end_down_body, sh), core_only, (),
+        trade("cut_down", cut_cols_body, down_ends, (half_ff + half_units, drows)),
+        [whole(new(down_weight.shape, F32)), whole(new(out_weight.shape, F32))],
+    )
+    (grad_up,) = call(
+        "end_up", bind(end_up_body, sh), core_only, (),
+        trade("cut_up", cut_rows_body, up_ends, (drows, half_ff)),
+        [whole(new(up_weight.shape, F32))],
+    )
+    grads = call(
+        "end_qkv", bind(end_qkv_body, sh), core_only, (),
+        trade("cut_qkv", cut_cols_body, qkv_ends, (3 * half_units, drows)),
+        [whole(new(q_weight.shape, F32))] * 3,
+    )
+    return (
+        mixed,
+        grad_tokens,
+        sums[0],
+        sums[1],
+        sums[2],
+        sums[3],
+        grads[0],
+        grads[1],
+        grads[2],
+        grad_out,
+        grad_up,
+        grad_down,
+    )
+
+
 def solution(mesh):
+    seqs, parts = mesh.shape["seq"], mesh.shape["mp"]
+
+    def body(*args):
+        units = args[5].shape[1]
+        teams = seqs % 2 == 0 and parts % 2 == 0 and (units // HEAD_DIM) % 2 == 0
+        chunks = parts // 2
+        if teams and chunks & (chunks - 1) == 0 and parts * units == 16 * HEAD_DIM:
+            return team_local(*args)
+        return plain_local(*args)
+
     in_specs = (
         P(None, ("seq", "mp"), None),
         P(),
@@ -370,4 +1332,4 @@
         P("seq", "mp"),
         P("mp", "seq"),
     )
-    return jax.shard_map(local, mesh=mesh, in_specs=in_specs, out_specs=out_specs, check_vma=False)
+    return jax.shard_map(body, mesh=mesh, in_specs=in_specs, out_specs=out_specs, check_vma=False)

time: 1180 us -> 357 us (0.30); the launches traced: 1160 us -> 355 us
  waiting for transfers between devices: 616 us -> 85.7 us
  matrix products: 281 us -> 0 us
  Pallas kernels: 0 us -> 169 us
  local copies, waits for them, and re-layouts: 104 us -> 15.1 us
  blocking collectives: 69.1 us -> 0 us
  starting transfers between devices: 1.39 us -> 63.6 us
  other arithmetic: 58.9 us -> 20.8 us
  loops' own time: 18.2 us -> 0 us
  between operations: 16 us -> 1.11 us
    reduce_scatter x12 -> x0, waiting for transfers between devices: 528 us -> none  [the longest x2 193 us: local(): lax.psum_scatter(jnp.dot(context_rows, w_out, preferred_element_type=jnp....]
    dot_general x158 -> x0, matrix products: 281 us -> none  [the longest x24 55 us: block_step(): jnp.einsum('ugy,uky->ugk', block_of_queries, block_of_keys, precision=max...]
    pallas_call x0 -> x25, Pallas kernels: none -> 169 us  [call(): pl.pallas_call(body, name=name, grid_spec=pltpu.PrefetchScalarGridSpec(nu...]
    ppermute x0 -> x57, waiting for transfers between devices: none -> 85.7 us  [move(): return lax.ppermute(values, AXES, links)]
    all_gather x8 -> x0, waiting for transfers between devices: 83.6 us -> none  [the longest x2 83.5 us: local(): lax.all_gather(normed_one.astype(jnp.bfloat16), 'mp', axis=0, tiled=True)]
    ppermute x0 -> x57, starting transfers between devices: none -> 63.6 us  [move(): return lax.ppermute(values, AXES, links)]
    psum x1 -> x0, blocking collectives: 43.5 us -> none  [local(): lax.psum((norm_sums[0], norm_sums[1], norm_sums[2], norm_sums[3]), ('seq'...]
    all_gather x4 -> x0, blocking collectives: 25.6 us -> none  [the longest x1 7.65 us: local(): lax.all_gather(k_weight, 'seq', axis=0, tiled=True)]
  transfers between devices with their start and end apart: 20 -> 57, of which waited for: 10 -> 19; matrix products, arithmetic and copies ran while one was open for 36% -> 7% of each run, Pallas kernels for 0% -> 41%
where the time goes in v1:
time: 357 us; the launch traced here: 355 us
  Pallas kernels  169 us (47%)
  waiting for transfers between devices  85.7 us (24%)
  starting transfers between devices  63.6 us (18%)
  other arithmetic  20.8 us (6%)
  local copies, waits for them, and re-layouts  15.1 us (4%)
    pallas_call x25, Pallas kernels, call(): pl.pallas_call(body, name=name, grid_spec=pltpu.PrefetchScalarGridSpec(nu...  169 us
    ppermute x57, waiting for transfers between devices, move(): return lax.ppermute(values, AXES, links)  85.7 us
    ppermute x57, starting transfers between devices, move(): return lax.ppermute(values, AXES, links)  63.6 us
    unnamed x72, local copies, waits for them, and re-layouts  8.35 us
  transfers between devices with their start and end apart: 57, of which 19 were waited for; matrix products, arithmetic and copies ran while one was open for 7% of the time, Pallas kernels for 41%

profile of v1, /device:TPU:0, one launch (start us, length us, event | category | flops | bytes accessed | tf_op | source)
XLA Modules:
  0.0 355.1 jit_solution(6885181275313739818)
XLA Ops:
  0.6 3.1 collective-permute-start.1
  3.7 17.8 %collective-permute-done.1 = bf16[2,192,1024]{2,1,0:T(8,128)(2,1)S(1)} collective-permute-done((bf16[2,192,1024]{2,1,0:T(8,128)(2,1)}, bf16[2,192,1024]{2,1,0:T(8,128)(2,1)S(1)}, u32[]{:S(2)}, u32[]{:S(2)}) %collective-permute-start.1) | collective-permute-done | bytes 786464 | tf_op jit(solution)/shard_map/ppermute | solution.py:928
  24.6 2.7 pack.1
  30.8 2.4 join_a.1.refs_0_
  33.1 3.6 %collective-permute-start.4 = (bf16[256,512]{1,0:T(8,128)(2,1)}, bf16[256,512]{1,0:T(8,128)(2,1)S(1)}, u32[]{:S(2)}, u32[]{:S(2)}) collective-permute-start(bf16[256,512]{1,0:T(8,128)(2,1)} %join_a.1.refs_0_), channel_id=1, source_target_pairs={{0,6},{1,7},{2,0},{3,1},{4,2},{5,3},{6,4},{7,5},{8,14},{9,15},{10,... | collective-permute-start | bytes 786440 | tf_op jit(solution)/shard_map/ppermute | solution.py:928
  37.5 2.4 join_d.1.refs_8_.refs_0_
  41.2 2.4 join_u.1.refs_0_.refs_8_
  44.0 3.9 %collective-permute-start.5 = (bf16[256,512]{1,0:T(8,128)(2,1)S(1)}, bf16[256,512]{1,0:T(8,128)(2,1)S(1)}, u32[]{:S(2)}, u32[]{:S(2)}) collective-permute-start(bf16[256,512]{1,0:T(8,128)(2,1)S(1)} %collective-permute-done.4.refs_1_), channel_id=1, source_target_pairs={{0,6},{1,7},{2,0},{3,1},{4,2},{5,3},{6,4},{7,5},{8,14},{9,15},{10,... | collective-permute-start | bytes 786440 | tf_op jit(solution)/shard_map/ppermute | solution.py:928
  51.1 3.9 %collective-permute-done.14.refs_1_.refs_9_ = bf16[512,256]{1,0:T(8,128)(2,1)} collective-permute-done((bf16[512,256]{1,0:T(8,128)(2,1)}, bf16[512,256]{1,0:T(8,128)(2,1)}, u32[]{:S(2)}, u32[]{:S(2)}) %collective-permute-start.14) | collective-permute-done | bytes 262176 | tf_op jit(solution)/shard_map/ppermute | solution.py:928
  56.5 3.0 collective-permute-done.5.refs_2_
  59.5 4.3 %collective-permute-start.15 = (bf16[512,256]{1,0:T(8,128)(2,1)}, bf16[512,256]{1,0:T(8,128)(2,1)}, u32[]{:S(2)}, u32[]{:S(2)}) collective-permute-start(bf16[512,256]{1,0:T(8,128)(2,1)} %collective-permute-done.14.refs_1_.refs_9_), channel_id=1, source_target_pairs={{0,6},{1,7},{2,0},{3,1},{4,2},{5,3},{6,4},{7,5},{8,14},{9,15},{10,... | collective-permute-start | bytes 786440 | tf_op jit(solution)/shard_map/ppermute | solution.py:928
  64.4 6.4 %collective-permute-done.15.refs_2_.refs_10_ = bf16[512,256]{1,0:T(8,128)(2,1)} collective-permute-done((bf16[512,256]{1,0:T(8,128)(2,1)}, bf16[512,256]{1,0:T(8,128)(2,1)}, u32[]{:S(2)}, u32[]{:S(2)}) %collective-permute-start.15) | collective-permute-done | bytes 262176 | tf_op jit(solution)/shard_map/ppermute | solution.py:928
  76.0 4.3 %fusion.2 = (f32[4,384,128]{2,1,0:T(8,128)}, f32[4,384,128]{2,1,0:T(8,128)}) fusion(f32[128]{0:T(128)S(1)} %copy-done.34, f32[128]{0:T(128)S(1)} %copy-done.35, f32[4,384]{1,0:T(4,128)S(1)} %subtract_convert_fusion), kind=kLoop, calls=%fused_computation.11 | loop fusion | flops 393216 | bytes 1580032 | tf_op jit(solution)/shard_map/mul | solution.py:1109
  80.3 3.8 %collective-permute-done.9.refs_6_ = bf16[256,512]{1,0:T(8,128)(2,1)S(1)} collective-permute-done((bf16[256,512]{1,0:T(8,128)(2,1)S(1)}, bf16[256,512]{1,0:T(8,128)(2,1)S(1)}, u32[]{:S(2)}, u32[]{:S(2)}) %collective-permute-start.9) | collective-permute-done | bytes 262176 | tf_op jit(solution)/shard_map/ppermute | solution.py:928
  84.2 4.3 %collective-permute-start.23 = (bf16[256,512]{1,0:T(8,128)(2,1)}, bf16[256,512]{1,0:T(8,128)(2,1)}, u32[]{:S(2)}, u32[]{:S(2)}) collective-permute-start(bf16[256,512]{1,0:T(8,128)(2,1)} %collective-permute-done.22.refs_9_.refs_1_), channel_id=1, source_target_pairs={{0,6},{1,7},{2,0},{3,1},{4,2},{5,3},{6,4},{7,5},{8,14},{9,15},{10,... | collective-permute-start | bytes 786440 | tf_op jit(solution)/shard_map/ppermute | solution.py:928
  89.3 7.1 %norms.1 = (bf16[4,384,1024]{2,1,0:T(8,128)(2,1)}, bf16[4,384,1024]{2,1,0:T(8,128)(2,1)}) custom-call(s32[28]{0:T(128)} %concatenate.10.scal, bf16[2,384,1024]{2,1,0:T(8,128)(2,1)} %bitcast.10.own, bf16[2,384,1024]{2,1,0:T(8,128)(2,1)} %collective-permute-done.2.away, f32[1,1024]{1,0:T(1,128)} %bitcast.61, f32[1,1024]{1,0:T(1,128)} %bitcast.65, ...), custom_call_target="tpu_custom_call" | custom-call | tf_op jit(solution)/shard_map/norms/pallas_call | solution.py:475
  96.5 15.8 %attend.1 = (bf16[4,384,256]{2,1,0:T(8,128)(2,1)}, bf16[4,384,256]{2,1,0:T(8,128)(2,1)}, f32[4,384,256]{2,1,0:T(8,128)}, f32[4,384,256]{2,1,0:T(8,128)}, f32[4,384,256]{2,1,0:T(8,128)}, /*index=5*/f32[4,80,256]{2,1,0:T(8,128)}) custom-call(s32[28]{0:T(128)} %concatenate.10.scal, bf16[4,384,1024]{2,1,0:T(8,128)(2,1)} %get-tuple-element.62.normed, ...), custom_call_target="tpu_custom_call" | custom-call | tf_op jit(solution)/shard_map/attend/pallas_call | solution.py:475
  117.9 2.5 collective-permute-done.11
  128.8 2.2 collective-permute-done.19.refs_6_.refs_14_
  132.5 4.1 %collective-permute-done.20.refs_7_.refs_15_ = bf16[512,256]{1,0:T(8,128)(2,1)} collective-permute-done((bf16[512,256]{1,0:T(8,128)(2,1)}, bf16[512,256]{1,0:T(8,128)(2,1)}, u32[]{:S(2)}, u32[]{:S(2)}) %collective-permute-start.20) | collective-permute-done | bytes 262176 | tf_op jit(solution)/shard_map/ppermute | solution.py:928
  138.6 10.0 %up.5 = (bf16[4,384,1024]{2,1,0:T(8,128)(2,1)}, bf16[4,384,1024]{2,1,0:T(8,128)(2,1)}) custom-call(s32[28]{0:T(128)} %concatenate.10.scal, bf16[4,384,1024]{2,1,0:T(8,128)(2,1)} %get-tuple-element.69.normed, bf16[512,256]{1,0:T(8,128)(2,1)} %join_u.1.refs_0_.refs_8_, bf16[512,256]{1,0:T(8,128)(2,1)} %collective-permute-done.14.refs_1_.refs_9_, ...), custom_call_target="tpu_custom_call" | custom-call | tf_op jit(solution)/shard_map/up/pallas_call | solution.py:475
  152.2 16.6 %branch.1 = (f32[4,384,256]{2,1,0:T(8,128)}, f32[4,384,256]{2,1,0:T(8,128)}, bf16[2,384,1024]{2,1,0:T(8,128)(2,1)}, bf16[2,384,1024]{2,1,0:T(8,128)(2,1)}) custom-call(s32[28]{0:T(128)} %concatenate.10.scal, f32[4,384,256]{2,1,0:T(8,128)} %get-tuple-element.65.num, f32[4,384,256]{2,1,0:T(8,128)} %get-tuple-element.66.den, ...), custom_call_target="tpu_custom_call" | custom-call | tf_op jit(solution)/shard_map/branch/pallas_call | solution.py:475
  170.0 19.4 %attend_back.1 = (bf16[4,384,256]{2,1,0:T(8,128)(2,1)}, f32[4,384,256]{2,1,0:T(8,128)}, f32[4,384,256]{2,1,0:T(8,128)}, f32[4,80,256]{2,1,0:T(8,128)}) custom-call(s32[28]{0:T(128)} %concatenate.10.scal, bf16[2,384,1024]{2,1,0:T(8,128)(2,1)} %bitcast.35, bf16[2,384,1024]{2,1,0:T(8,128)(2,1)} %copy-done.1, bf16[4,384,256]{2,1,0:T(8,128)(2,1)} %get-tuple-element.67.fq, ...), custom_call_target="tpu_custom_call" | custom-call | tf_op jit(solution)/shard_map/attend_back/pallas_call | solution.py:475
  190.9 8.8 %hidden_grad.1.gh = bf16[4,384,1024]{2,1,0:T(8,128)(2,1)} custom-call(s32[28]{0:T(128)} %concatenate.10.scal, bf16[2,384,1024]{2,1,0:T(8,128)(2,1)} %bitcast.36, bf16[2,384,1024]{2,1,0:T(8,128)(2,1)} %copy-done.1, bf16[4,384,1024]{2,1,0:T(8,128)(2,1)} %get-tuple-element.85.slope, bf16[256,512]{1,0:T(8,128)(2,1)} %join_d.1.refs_8_.refs_0_, ...), custom_call_target="tpu_custom_call" | custom-call | tf_op jit(solution)/shard_map/hidden_grad/pallas_call | solution.py:475
  199.7 6.4 %up_grad1.1 = bf16[4,512,256]{2,1,0:T(8,128)(2,1)} custom-call(s32[28]{0:T(128)} %concatenate.10.scal, bf16[1536,1024]{1,0:T(8,128)(2,1)} %bitcast.43, bf16[1536,1024]{1,0:T(8,128)(2,1)} %bitcast.32), custom_call_target="tpu_custom_call" | custom-call | tf_op jit(solution)/shard_map/up_grad1/pallas_call | solution.py:475
  208.3 8.3 %collective-permute-done.34 = bf16[4,80,256]{2,1,0:T(8,128)(2,1)S(1)} collective-permute-done((bf16[4,80,256]{2,1,0:T(8,128)(2,1)S(1)}, bf16[4,80,256]{2,1,0:T(8,128)(2,1)S(1)}, u32[]{:S(2)}, u32[]{:S(2)}) %collective-permute-start.34) | collective-permute-done | bytes 163872 | tf_op jit(solution)/shard_map/ppermute | solution.py:928
  217.5 7.4 %keys_back.1 = (bf16[4,384,256]{2,1,0:T(8,128)(2,1)}, bf16[4,384,256]{2,1,0:T(8,128)(2,1)}) custom-call(s32[28]{0:T(128)} %concatenate.10.scal, f32[4,384,256]{2,1,0:T(8,128)} %get-tuple-element.80.dfk, f32[4,384,256]{2,1,0:T(8,128)} %get-tuple-element.81.dv, bf16[4,384,256]{2,1,0:T(8,128)(2,1)} %get-tuple-element.75.fk, ...), custom_call_target="tpu_custom_call" | custom-call | tf_op jit(solution)/shard_map/keys_back/pallas_call | solution.py:475
  224.9 5.1 %qkv_grad1.1 = bf16[4,192,512]{2,1,0:T(8,128)(2,1)} custom-call(s32[28]{0:T(128)} %concatenate.10.scal, bf16[1536,256]{1,0:T(8,128)(2,1)} %bitcast.49, bf16[1536,256]{1,0:T(8,128)(2,1)} %bitcast.51, bf16[1536,256]{1,0:T(8,128)(2,1)} %bitcast.53, bf16[1536,1024]{1,0:T(8,128)(2,1)} %bitcast.39), custom_call_target="tpu_custom_call" | custom-call | tf_op jit(solution)/shard_map/qkv_grad1/pallas_call | solution.py:475
  231.5 7.3 %down_grad1.1 = bf16[4,320,512]{2,1,0:T(8,128)(2,1)} custom-call(s32[28]{0:T(128)} %concatenate.10.scal, bf16[1536,1024]{1,0:T(8,128)(2,1)} %bitcast.41, f32[1536,256]{1,0:T(8,128)} %bitcast.47, bf16[768,1024]{1,0:T(8,128)(2,1)} %bitcast.37, bf16[768,1024]{1,0:T(8,128)(2,1)} %bitcast.45), custom_call_target="tpu_custom_call" | custom-call | tf_op jit(solution)/shard_map/down_grad1/pallas_call | solution.py:475
  239.3 16.0 %rows_grad.1 = (bf16[2,384,1024]{2,1,0:T(8,128)(2,1)}, bf16[2,384,1024]{2,1,0:T(8,128)(2,1)}, f32[8,1024]{1,0:T(8,128)}) custom-call(s32[28]{0:T(128)} %concatenate.10.scal, bf16[4,384,256]{2,1,0:T(8,128)(2,1)} %get-tuple-element.79.dq, bf16[4,384,256]{2,1,0:T(8,128)(2,1)} %get-tuple-element.83.dk, bf16[4,384,256]{2,1,0:T(8,128)(2,1)} %get-tuple-element.84.dv, ...), custom_call_target="tpu_custom_call" | custom-call | tf_op jit(solution)/shard_map/rows_grad/pallas_call | solution.py:475
  257.3 6.7 %up_grad0.1 = (bf16[512,256]{1,0:T(8,128)(2,1)}, bf16[512,256]{1,0:T(8,128)(2,1)}, bf16[512,256]{1,0:T(8,128)(2,1)}, bf16[512,256]{1,0:T(8,128)(2,1)}) custom-call(s32[28]{0:T(128)} %concatenate.10.scal, bf16[1536,1024]{1,0:T(8,128)(2,1)} %bitcast.44, bf16[1536,1024]{1,0:T(8,128)(2,1)} %bitcast.33, bf16[4,512,256]{2,1,0:T(8,128)(2,1)} %copy-done.18), custom_call_target="tpu_custom_call" | custom-call | tf_op jit(solution)/shard_map/up_grad0/pallas_call | solution.py:475
  269.3 2.5 collective-permute-done.39
  272.7 5.3 %qkv_grad0.1 = (bf16[192,512]{1,0:T(8,128)(2,1)}, bf16[192,512]{1,0:T(8,128)(2,1)}, bf16[192,512]{1,0:T(8,128)(2,1)}, bf16[192,512]{1,0:T(8,128)(2,1)}) custom-call(s32[28]{0:T(128)} %concatenate.10.scal, bf16[1536,256]{1,0:T(8,128)(2,1)} %bitcast.50, bf16[1536,256]{1,0:T(8,128)(2,1)} %bitcast.52, bf16[1536,256]{1,0:T(8,128)(2,1)} %bitcast.54, ...), custom_call_target="tpu_custom_call" | custom-call | tf_op jit(solution)/shard_map/qkv_grad0/pallas_call | solution.py:475
  279.3 2.7 collective-permute-start.54
  282.0 5.7 %collective-permute-done.43 = bf16[192,512]{1,0:T(8,128)(2,1)S(1)} collective-permute-done((bf16[192,512]{1,0:T(8,128)(2,1)}, bf16[192,512]{1,0:T(8,128)(2,1)S(1)}, u32[]{:S(2)}, u32[]{:S(2)}) %collective-permute-start.43) | collective-permute-done | bytes 196640 | tf_op jit(solution)/shard_map/ppermute | solution.py:928
  290.3 2.9 collective-permute-done.54
  296.1 8.0 %down_grad0.1 = (bf16[320,512]{1,0:T(8,128)(2,1)}, bf16[320,512]{1,0:T(8,128)(2,1)}, bf16[320,512]{1,0:T(8,128)(2,1)}, bf16[320,512]{1,0:T(8,128)(2,1)}) custom-call(s32[28]{0:T(128)} %concatenate.10.scal, bf16[1536,1024]{1,0:T(8,128)(2,1)} %bitcast.42, f32[1536,256]{1,0:T(8,128)} %bitcast.48, bf16[768,1024]{1,0:T(8,128)(2,1)} %bitcast.38, ...), custom_call_target="tpu_custom_call" | custom-call | tf_op jit(solution)/shard_map/down_grad0/pallas_call | solution.py:475
  309.4 6.9 %collective-permute-done.48 = bf16[320,512]{1,0:T(8,128)(2,1)S(1)} collective-permute-done((bf16[320,512]{1,0:T(8,128)(2,1)}, bf16[320,512]{1,0:T(8,128)(2,1)S(1)}, u32[]{:S(2)}, u32[]{:S(2)}) %collective-permute-start.48) | collective-permute-done | bytes 327712 | tf_op jit(solution)/shard_map/ppermute | solution.py:928
  316.3 2.2 collective-permute-start.30
  319.4 8.1 %collective-permute-done.49 = bf16[320,512]{1,0:T(8,128)(2,1)S(1)} collective-permute-done((bf16[320,512]{1,0:T(8,128)(2,1)S(1)}, bf16[320,512]{1,0:T(8,128)(2,1)S(1)}, u32[]{:S(2)}, u32[]{:S(2)}) %collective-permute-start.49) | collective-permute-done | bytes 327712 | tf_op jit(solution)/shard_map/ppermute | solution.py:928
  328.5 2.5 cut_up.1
  330.9 2.4 cut_qkv.1
  335.1 2.5 end_up.1
  338.3 2.4 end_qkv.1
  342.8 2.6 cut_down.1
  345.3 2.4 fusion.1
  348.4 2.5 end_down.1
  350.9 4.2 %tokens_grad.1 = f32[2,192,1024]{2,1,0:T(8,128)} custom-call(s32[28]{0:T(128)} %concatenate.10.scal, f32[2,192,1024]{2,1,0:T(8,128)} %slice.61.mine, bf16[2,192,1024]{2,1,0:T(8,128)(2,1)} %collective-permute-done.36.got, bf16[2,192,1024]{2,1,0:T(8,128)(2,1)} %tokens.1, bf16[2,192,1024]{2,1,0:T(8,128)(2,1)} %cot.1), custom_call_target="tpu_custom_call" | custom-call | tf_op jit(solution)/shard_map/tokens_grad/pallas_call | solution.py:475
  (208 shorter events, 76.3 us)
Async XLA Ops:
  0.6 20.8 %collective-permute-start.1 = (bf16[2,192,1024]{2,1,0:T(8,128)(2,1)}, bf16[2,192,1024]{2,1,0:T(8,128)(2,1)S(1)}, u32[]{:S(2)}, u32[]{:S(2)}) collective-permute-start(bf16[2,192,1024]{2,1,0:T(8,128)(2,1)} %tokens.1), channel_id=1, source_target_pairs={{0,1},{1,0},{2,3},{3,2},{4,5},{5,4},{6,7},{7,6},{8,9},{9,8},{10,11... | collective-permute-start | bytes 2359304 | tf_op jit(solution)/shard_map/ppermute | solution.py:928
  24.0 64.4 %collective-permute-start.2 = (bf16[2,384,1024]{2,1,0:T(8,128)(2,1)}, bf16[2,384,1024]{2,1,0:T(8,128)(2,1)}, u32[]{:S(2)}, u32[]{:S(2)}) collective-permute-start(bf16[2,384,1024]{2,1,0:T(8,128)(2,1)} %bitcast.10.own), channel_id=1, source_target_pairs={{0,8},{1,9},{2,10},{3,11},{4,12},{5,13},{6,14},{7,15},{8,0},{9,1},... | collective-permute-start | bytes 4718600 | tf_op jit(solution)/shard_map/ppermute | solution.py:928
  27.9 35.9 %collective-permute-start.31 = (bf16[2,192,1024]{2,1,0:T(8,128)(2,1)S(1)}, bf16[2,192,1024]{2,1,0:T(8,128)(2,1)S(1)}, u32[]{:S(2)}, u32[]{:S(2)}) collective-permute-start(bf16[2,192,1024]{2,1,0:T(8,128)(2,1)S(1)} %copy-done.8), channel_id=1, source_target_pairs={{0,1},{1,0},{2,3},{3,2},{4,5},{5,4},{6,7},{7,6},{8,9},{9,8},{10,11... | collective-permute-start | bytes 2359304 | tf_op jit(solution)/shard_map/ppermute | solution.py:928
  29.6 10.9 %collective-permute-start.13 = (bf16[256,256]{1,0:T(8,128)(2,1)}, bf16[256,256]{1,0:T(8,128)(2,1)S(1)}, u32[]{:S(2)}, u32[]{:S(2)}) collective-permute-start(bf16[256,256]{1,0:T(8,128)(2,1)} %get-tuple-element.70), channel_id=1, source_target_pairs={{0,8},{1,9},{2,10},{3,11},{4,12},{5,13},{6,14},{7,15},{8,0},{9,1},... | collective-permute-start | bytes 393224 | tf_op jit(solution)/shard_map/ppermute | solution.py:928
  33.1 10.9 %collective-permute-start.4 = (bf16[256,512]{1,0:T(8,128)(2,1)}, bf16[256,512]{1,0:T(8,128)(2,1)S(1)}, u32[]{:S(2)}, u32[]{:S(2)}) collective-permute-start(bf16[256,512]{1,0:T(8,128)(2,1)} %join_a.1.refs_0_), channel_id=1, source_target_pairs={{0,6},{1,7},{2,0},{3,1},{4,2},{5,3},{6,4},{7,5},{8,14},{9,15},{10,... | collective-permute-start | bytes 786440 | tf_op jit(solution)/shard_map/ppermute | solution.py:928
  39.9 9.5 %collective-permute-start.22 = (bf16[256,512]{1,0:T(8,128)(2,1)}, bf16[256,512]{1,0:T(8,128)(2,1)}, u32[]{:S(2)}, u32[]{:S(2)}) collective-permute-start(bf16[256,512]{1,0:T(8,128)(2,1)} %join_d.1.refs_8_.refs_0_), channel_id=1, source_target_pairs={{0,6},{1,7},{2,0},{3,1},{4,2},{5,3},{6,4},{7,5},{8,14},{9,15},{10,... | collective-permute-start | bytes 786440 | tf_op jit(solution)/shard_map/ppermute | solution.py:928
  43.5 11.5 %collective-permute-start.14 = (bf16[512,256]{1,0:T(8,128)(2,1)}, bf16[512,256]{1,0:T(8,128)(2,1)}, u32[]{:S(2)}, u32[]{:S(2)}) collective-permute-start(bf16[512,256]{1,0:T(8,128)(2,1)} %join_u.1.refs_0_.refs_8_), channel_id=1, source_target_pairs={{0,6},{1,7},{2,0},{3,1},{4,2},{5,3},{6,4},{7,5},{8,14},{9,15},{10,... | collective-permute-start | bytes 786440 | tf_op jit(solution)/shard_map/ppermute | solution.py:928
  44.0 15.5 %collective-permute-start.5 = (bf16[256,512]{1,0:T(8,128)(2,1)S(1)}, bf16[256,512]{1,0:T(8,128)(2,1)S(1)}, u32[]{:S(2)}, u32[]{:S(2)}) collective-permute-start(bf16[256,512]{1,0:T(8,128)(2,1)S(1)} %collective-permute-done.4.refs_1_), channel_id=1, source_target_pairs={{0,6},{1,7},{2,0},{3,1},{4,2},{5,3},{6,4},{7,5},{8,14},{9,15},{10,... | collective-permute-start | bytes 786440 | tf_op jit(solution)/shard_map/ppermute | solution.py:928
  49.4 14.8 %collective-permute-start.7 = (bf16[256,512]{1,0:T(8,128)(2,1)}, bf16[256,512]{1,0:T(8,128)(2,1)S(1)}, u32[]{:S(2)}, u32[]{:S(2)}) collective-permute-start(bf16[256,512]{1,0:T(8,128)(2,1)} %join_a.1.refs_0_), channel_id=1, source_target_pairs={{0,16},{1,17},{2,18},{3,19},{4,20},{5,21},{6,22},{7,23},{8,24},{9,... | collective-permute-start | bytes 786440 | tf_op jit(solution)/shard_map/ppermute | solution.py:928
  55.0 17.3 %collective-permute-start.8 = (bf16[256,512]{1,0:T(8,128)(2,1)S(1)}, bf16[256,512]{1,0:T(8,128)(2,1)S(1)}, u32[]{:S(2)}, u32[]{:S(2)}) collective-permute-start(bf16[256,512]{1,0:T(8,128)(2,1)S(1)} %collective-permute-done.4.refs_1_), channel_id=1, source_target_pairs={{0,16},{1,17},{2,18},{3,19},{4,20},{5,21},{6,22},{7,23},{8,24},{9,... | collective-permute-start | bytes 786440 | tf_op jit(solution)/shard_map/ppermute | solution.py:928
  59.5 11.3 %collective-permute-start.15 = (bf16[512,256]{1,0:T(8,128)(2,1)}, bf16[512,256]{1,0:T(8,128)(2,1)}, u32[]{:S(2)}, u32[]{:S(2)}) collective-permute-start(bf16[512,256]{1,0:T(8,128)(2,1)} %collective-permute-done.14.refs_1_.refs_9_), channel_id=1, source_target_pairs={{0,6},{1,7},{2,0},{3,1},{4,2},{5,3},{6,4},{7,5},{8,14},{9,15},{10,... | collective-permute-start | bytes 786440 | tf_op jit(solution)/shard_map/ppermute | solution.py:928
  63.8 10.7 %collective-permute-start.6 = (bf16[256,512]{1,0:T(8,128)(2,1)S(1)}, bf16[256,512]{1,0:T(8,128)(2,1)}, u32[]{:S(2)}, u32[]{:S(2)}) collective-permute-start(bf16[256,512]{1,0:T(8,128)(2,1)S(1)} %collective-permute-done.5.refs_2_), channel_id=1, source_target_pairs={{0,6},{1,7},{2,0},{3,1},{4,2},{5,3},{6,4},{7,5},{8,14},{9,15},{10,... | collective-permute-start | bytes 786440 | tf_op jit(solution)/shard_map/ppermute | solution.py:928
  64.2 104.5 %collective-permute-start.32 = (bf16[2,384,1024]{2,1,0:T(8,128)(2,1)S(1)}, bf16[2,384,1024]{2,1,0:T(8,128)(2,1)S(1)}, u32[]{:S(2)}, u32[]{:S(2)}) collective-permute-start(bf16[2,384,1024]{2,1,0:T(8,128)(2,1)S(1)} %bitcast.34), channel_id=1, source_target_pairs={{0,8},{1,9},{2,10},{3,11},{4,12},{5,13},{6,14},{7,15},{8,0},{9,1},... | collective-permute-start | bytes 4718600 | tf_op jit(solution)/shard_map/ppermute | solution.py:928
  70.8 45.0 %collective-permute-start.17 = (bf16[512,256]{1,0:T(8,128)(2,1)}, bf16[512,256]{1,0:T(8,128)(2,1)}, u32[]{:S(2)}, u32[]{:S(2)}) collective-permute-start(bf16[512,256]{1,0:T(8,128)(2,1)} %join_u.1.refs_0_.refs_8_), channel_id=1, source_target_pairs={{0,16},{1,17},{2,18},{3,19},{4,20},{5,21},{6,22},{7,23},{8,24},{9,... | collective-permute-start | bytes 786440 | tf_op jit(solution)/shard_map/ppermute | solution.py:928
  72.3 11.8 %collective-permute-start.9 = (bf16[256,512]{1,0:T(8,128)(2,1)S(1)}, bf16[256,512]{1,0:T(8,128)(2,1)S(1)}, u32[]{:S(2)}, u32[]{:S(2)}) collective-permute-start(bf16[256,512]{1,0:T(8,128)(2,1)S(1)} %collective-permute-done.5.refs_2_), channel_id=1, source_target_pairs={{0,16},{1,17},{2,18},{3,19},{4,20},{5,21},{6,22},{7,23},{8,24},{9,... | collective-permute-start | bytes 786440 | tf_op jit(solution)/shard_map/ppermute | solution.py:928
  74.5 21.9 %collective-permute-start.10 = (bf16[256,512]{1,0:T(8,128)(2,1)}, bf16[256,512]{1,0:T(8,128)(2,1)}, u32[]{:S(2)}, u32[]{:S(2)}) collective-permute-start(bf16[256,512]{1,0:T(8,128)(2,1)} %collective-permute-done.6.refs_3_), channel_id=1, source_target_pairs={{0,16},{1,17},{2,18},{3,19},{4,20},{5,21},{6,22},{7,23},{8,24},{9,... | collective-permute-start | bytes 786440 | tf_op jit(solution)/shard_map/ppermute | solution.py:928
  84.2 33.2 %collective-permute-start.23 = (bf16[256,512]{1,0:T(8,128)(2,1)}, bf16[256,512]{1,0:T(8,128)(2,1)}, u32[]{:S(2)}, u32[]{:S(2)}) collective-permute-start(bf16[256,512]{1,0:T(8,128)(2,1)} %collective-permute-done.22.refs_9_.refs_1_), channel_id=1, source_target_pairs={{0,6},{1,7},{2,0},{3,1},{4,2},{5,3},{6,4},{7,5},{8,14},{9,15},{10,... | collective-permute-start | bytes 786440 | tf_op jit(solution)/shard_map/ppermute | solution.py:928
  88.4 29.5 %collective-permute-start.16 = (bf16[512,256]{1,0:T(8,128)(2,1)}, bf16[512,256]{1,0:T(8,128)(2,1)}, u32[]{:S(2)}, u32[]{:S(2)}) collective-permute-start(bf16[512,256]{1,0:T(8,128)(2,1)} %collective-permute-done.15.refs_2_.refs_10_), channel_id=1, source_target_pairs={{0,6},{1,7},{2,0},{3,1},{4,2},{5,3},{6,4},{7,5},{8,14},{9,15},{10,... | collective-permute-start | bytes 786440 | tf_op jit(solution)/shard_map/ppermute | solution.py:928
  115.9 9.5 %collective-permute-start.18 = (bf16[512,256]{1,0:T(8,128)(2,1)}, bf16[512,256]{1,0:T(8,128)(2,1)}, u32[]{:S(2)}, u32[]{:S(2)}) collective-permute-start(bf16[512,256]{1,0:T(8,128)(2,1)} %collective-permute-done.14.refs_1_.refs_9_), channel_id=1, source_target_pairs={{0,16},{1,17},{2,18},{3,19},{4,20},{5,21},{6,22},{7,23},{8,24},{9,... | collective-permute-start | bytes 786440 | tf_op jit(solution)/shard_map/ppermute | solution.py:928
  117.4 13.6 %collective-permute-start.19 = (bf16[512,256]{1,0:T(8,128)(2,1)}, bf16[512,256]{1,0:T(8,128)(2,1)}, u32[]{:S(2)}, u32[]{:S(2)}) collective-permute-start(bf16[512,256]{1,0:T(8,128)(2,1)} %collective-permute-done.15.refs_2_.refs_10_), channel_id=1, source_target_pairs={{0,16},{1,17},{2,18},{3,19},{4,20},{5,21},{6,22},{7,23},{8,24},{9,... | collective-permute-start | bytes 786440 | tf_op jit(solution)/shard_map/ppermute | solution.py:928
  117.9 9.4 %collective-permute-start.24 = (bf16[256,512]{1,0:T(8,128)(2,1)}, bf16[256,512]{1,0:T(8,128)(2,1)}, u32[]{:S(2)}, u32[]{:S(2)}) collective-permute-start(bf16[256,512]{1,0:T(8,128)(2,1)} %collective-permute-done.23.refs_10_.refs_2_), channel_id=1, source_target_pairs={{0,6},{1,7},{2,0},{3,1},{4,2},{5,3},{6,4},{7,5},{8,14},{9,15},{10,... | collective-permute-start | bytes 786440 | tf_op jit(solution)/shard_map/ppermute | solution.py:928
  120.4 16.2 %collective-permute-start.20 = (bf16[512,256]{1,0:T(8,128)(2,1)}, bf16[512,256]{1,0:T(8,128)(2,1)}, u32[]{:S(2)}, u32[]{:S(2)}) collective-permute-start(bf16[512,256]{1,0:T(8,128)(2,1)} %collective-permute-done.16.refs_3_.refs_11_), channel_id=1, source_target_pairs={{0,16},{1,17},{2,18},{3,19},{4,20},{5,21},{6,22},{7,23},{8,24},{9,... | collective-permute-start | bytes 786440 | tf_op jit(solution)/shard_map/ppermute | solution.py:928
  125.4 12.7 %collective-permute-start.12 = (bf16[4,80,256]{2,1,0:T(8,128)(2,1)}, bf16[4,80,256]{2,1,0:T(8,128)(2,1)}, u32[]{:S(2)}, u32[]{:S(2)}) collective-permute-start(bf16[4,80,256]{2,1,0:T(8,128)(2,1)} %fusion.5), channel_id=1, source_target_pairs={{0,4},{1,5},{2,6},{3,7},{8,12},{9,13},{10,14},{11,15},{16,20},{17,... | collective-permute-start | bytes 491528 | tf_op jit(solution)/shard_map/ppermute | solution.py:928
  127.3 23.2 %collective-permute-start.25 = (bf16[256,512]{1,0:T(8,128)(2,1)S(1)}, bf16[256,512]{1,0:T(8,128)(2,1)S(1)}, u32[]{:S(2)}, u32[]{:S(2)}) collective-permute-start(bf16[256,512]{1,0:T(8,128)(2,1)S(1)} %copy-done.9), channel_id=1, source_target_pairs={{0,16},{1,17},{2,18},{3,19},{4,20},{5,21},{6,22},{7,23},{8,24},{9,... | collective-permute-start | bytes 786440 | tf_op jit(solution)/shard_map/ppermute | solution.py:928
  131.0 19.5 %collective-permute-start.26 = (bf16[256,512]{1,0:T(8,128)(2,1)}, bf16[256,512]{1,0:T(8,128)(2,1)S(1)}, u32[]{:S(2)}, u32[]{:S(2)}) collective-permute-start(bf16[256,512]{1,0:T(8,128)(2,1)} %collective-permute-done.22.refs_9_.refs_1_), channel_id=1, source_target_pairs={{0,16},{1,17},{2,18},{3,19},{4,20},{5,21},{6,22},{7,23},{8,24},{9,... | collective-permute-start | bytes 786440 | tf_op jit(solution)/shard_map/ppermute | solution.py:928
  136.6 13.9 %collective-permute-start.27 = (bf16[256,512]{1,0:T(8,128)(2,1)}, bf16[256,512]{1,0:T(8,128)(2,1)S(1)}, u32[]{:S(2)}, u32[]{:S(2)}) collective-permute-start(bf16[256,512]{1,0:T(8,128)(2,1)} %collective-permute-done.23.refs_10_.refs_2_), channel_id=1, source_target_pairs={{0,16},{1,17},{2,18},{3,19},{4,20},{5,21},{6,22},{7,23},{8,24},{9,... | collective-permute-start | bytes 786440 | tf_op jit(solution)/shard_map/ppermute | solution.py:928
  138.1 13.4 %collective-permute-start.28 = (bf16[256,512]{1,0:T(8,128)(2,1)}, bf16[256,512]{1,0:T(8,128)(2,1)S(1)}, u32[]{:S(2)}, u32[]{:S(2)}) collective-permute-start(bf16[256,512]{1,0:T(8,128)(2,1)} %collective-permute-done.24.refs_11_.refs_3_), channel_id=1, source_target_pairs={{0,16},{1,17},{2,18},{3,19},{4,20},{5,21},{6,22},{7,23},{8,24},{9,... | collective-permute-start | bytes 786440 | tf_op jit(solution)/shard_map/ppermute | solution.py:928
  190.5 16.2 %collective-permute-start.33 = (bf16[4,80,256]{2,1,0:T(8,128)(2,1)S(1)}, bf16[4,80,256]{2,1,0:T(8,128)(2,1)S(1)}, u32[]{:S(2)}, u32[]{:S(2)}) collective-permute-start(bf16[4,80,256]{2,1,0:T(8,128)(2,1)S(1)} %convert_element_type.164), channel_id=1, source_target_pairs={{0,2},{1,3},{2,0},{3,1},{4,6},{5,7},{6,4},{7,5},{8,10},{9,11},{10,... | collective-permute-start | bytes 491528 | tf_op jit(solution)/shard_map/ppermute | solution.py:928
  206.1 50.3 %collective-permute-start.52 = (bf16[4,512,256]{2,1,0:T(8,128)(2,1)}, bf16[4,512,256]{2,1,0:T(8,128)(2,1)S(1)}, u32[]{:S(2)}, u32[]{:S(2)}) collective-permute-start(bf16[4,512,256]{2,1,0:T(8,128)(2,1)} %up_grad1.1), channel_id=1, source_target_pairs={{0,16},{1,17},{2,18},{3,19},{4,20},{5,21},{6,22},{7,23},{8,24},{9,... | collective-permute-start | bytes 3145736 | tf_op jit(solution)/shard_map/ppermute | solution.py:928
  206.8 9.9 %collective-permute-start.34 = (bf16[4,80,256]{2,1,0:T(8,128)(2,1)S(1)}, bf16[4,80,256]{2,1,0:T(8,128)(2,1)S(1)}, u32[]{:S(2)}, u32[]{:S(2)}) collective-permute-start(bf16[4,80,256]{2,1,0:T(8,128)(2,1)S(1)} %fusion.9), channel_id=1, source_target_pairs={{4,0},{5,1},{6,2},{7,3},{12,8},{13,9},{14,10},{15,11},{20,16},{21,... | collective-permute-start | bytes 491528 | tf_op jit(solution)/shard_map/ppermute | solution.py:928
  230.0 41.8 %collective-permute-start.42 = (bf16[4,192,512]{2,1,0:T(8,128)(2,1)}, bf16[4,192,512]{2,1,0:T(8,128)(2,1)S(1)}, u32[]{:S(2)}, u32[]{:S(2)}) collective-permute-start(bf16[4,192,512]{2,1,0:T(8,128)(2,1)} %qkv_grad1.1), channel_id=1, source_target_pairs={{0,16},{1,17},{2,18},{3,19},{4,20},{5,21},{6,22},{7,23},{8,24},{9,... | collective-permute-start | bytes 2359304 | tf_op jit(solution)/shard_map/ppermute | solution.py:928
  231.5 74.4 %collective-permute-start.29 = (bf16[2,384,1024]{2,1,0:T(8,128)(2,1)}, bf16[2,384,1024]{2,1,0:T(8,128)(2,1)S(1)}, u32[]{:S(2)}, u32[]{:S(2)}) collective-permute-start(bf16[2,384,1024]{2,1,0:T(8,128)(2,1)} %get-tuple-element.74), channel_id=1, source_target_pairs={{0,8},{1,9},{2,10},{3,11},{4,12},{5,13},{6,14},{7,15},{8,0},{9,1},... | collective-permute-start | bytes 4718600 | tf_op jit(solution)/shard_map/ppermute | solution.py:928
  238.8 55.2 %collective-permute-start.47 = (bf16[4,320,512]{2,1,0:T(8,128)(2,1)}, bf16[4,320,512]{2,1,0:T(8,128)(2,1)S(1)}, u32[]{:S(2)}, u32[]{:S(2)}) collective-permute-start(bf16[4,320,512]{2,1,0:T(8,128)(2,1)} %down_grad1.1), channel_id=1, source_target_pairs={{0,16},{1,17},{2,18},{3,19},{4,20},{5,21},{6,22},{7,23},{8,24},{9,... | collective-permute-start | bytes 3932168 | tf_op jit(solution)/shard_map/ppermute | solution.py:928
  256.1 8.1 %collective-permute-start.37 = (f32[4,1024]{1,0:T(4,128)S(1)}, f32[4,1024]{1,0:T(4,128)S(1)}, u32[]{:S(2)}, u32[]{:S(2)}) collective-permute-start(f32[4,1024]{1,0:T(4,128)S(1)} %slice.54), channel_id=1, source_target_pairs={{0,8},{1,9},{2,10},{3,11},{4,12},{5,13},{6,14},{7,15},{8,0},{9,1},... | collective-permute-start | bytes 49160 | tf_op jit(solution)/shard_map/ppermute | solution.py:928
  264.0 14.0 %collective-permute-start.53 = (bf16[512,256]{1,0:T(8,128)(2,1)}, bf16[512,256]{1,0:T(8,128)(2,1)S(1)}, u32[]{:S(2)}, u32[]{:S(2)}) collective-permute-start(bf16[512,256]{1,0:T(8,128)(2,1)} %get-tuple-element.105), channel_id=1, source_target_pairs={{0,2},{1,3},{2,4},{3,5},{4,6},{5,7},{6,0},{7,1},{8,10},{9,11},{10,... | collective-permute-start | bytes 786440 | tf_op jit(solution)/shard_map/ppermute | solution.py:928
  271.8 46.8 %collective-permute-start.35 = (bf16[2,384,1024]{2,1,0:T(8,128)(2,1)}, bf16[2,384,1024]{2,1,0:T(8,128)(2,1)S(1)}, u32[]{:S(2)}, u32[]{:S(2)}) collective-permute-start(bf16[2,384,1024]{2,1,0:T(8,128)(2,1)} %get-tuple-element.87), channel_id=1, source_target_pairs={{0,8},{1,9},{2,10},{3,11},{4,12},{5,13},{6,14},{7,15},{8,0},{9,1},... | collective-permute-start | bytes 4718600 | tf_op jit(solution)/shard_map/ppermute | solution.py:928
  271.8 7.5 %collective-permute-start.40 = (f32[4,1024]{1,0:T(4,128)S(1)}, f32[4,1024]{1,0:T(4,128)S(1)}, u32[]{:S(2)}, u32[]{:S(2)}) collective-permute-start(f32[4,1024]{1,0:T(4,128)S(1)} %add.131), channel_id=1, source_target_pairs={{0,2},{1,3},{2,0},{3,1},{4,6},{5,7},{6,4},{7,5},{8,10},{9,11},{10,... | collective-permute-start | bytes 49160 | tf_op jit(solution)/shard_map/ppermute | solution.py:928
  277.9 9.8 %collective-permute-start.43 = (bf16[192,512]{1,0:T(8,128)(2,1)}, bf16[192,512]{1,0:T(8,128)(2,1)S(1)}, u32[]{:S(2)}, u32[]{:S(2)}) collective-permute-start(bf16[192,512]{1,0:T(8,128)(2,1)} %get-tuple-element.89), channel_id=1, source_target_pairs={{0,2},{1,3},{2,4},{3,5},{4,6},{5,7},{6,0},{7,1},{8,10},{9,11},{10,... | collective-permute-start | bytes 589832 | tf_op jit(solution)/shard_map/ppermute | solution.py:928
  279.3 13.9 %collective-permute-start.54 = (bf16[512,256]{1,0:T(8,128)(2,1)S(1)}, bf16[512,256]{1,0:T(8,128)(2,1)S(1)}, u32[]{:S(2)}, u32[]{:S(2)}) collective-permute-start(bf16[512,256]{1,0:T(8,128)(2,1)S(1)} %add_convert_fusion.3), channel_id=1, source_target_pairs={{0,2},{1,3},{2,4},{3,5},{4,6},{5,7},{6,0},{7,1},{8,10},{9,11},{10,... | collective-permute-start | bytes 786440 | tf_op jit(solution)/shard_map/ppermute | solution.py:928
  287.8 40.7 %collective-permute-start.41 = (f32[4,1024]{1,0:T(4,128)S(1)}, f32[4,1024]{1,0:T(4,128)S(1)}, u32[]{:S(2)}, u32[]{:S(2)}) collective-permute-start(f32[4,1024]{1,0:T(4,128)S(1)} %add.132), channel_id=1, source_target_pairs={{0,4},{1,5},{2,6},{3,7},{4,0},{5,1},{6,2},{7,3},{8,12},{9,13},{10,... | collective-permute-start | bytes 49160 | tf_op jit(solution)/shard_map/ppermute | solution.py:928
  293.2 10.9 %collective-permute-start.44 = (bf16[192,512]{1,0:T(8,128)(2,1)S(1)}, bf16[192,512]{1,0:T(8,128)(2,1)S(1)}, u32[]{:S(2)}, u32[]{:S(2)}) collective-permute-start(bf16[192,512]{1,0:T(8,128)(2,1)S(1)} %add_convert_fusion.5), channel_id=1, source_target_pairs={{0,2},{1,3},{2,4},{3,5},{4,6},{5,7},{6,0},{7,1},{8,10},{9,11},{10,... | collective-permute-start | bytes 589832 | tf_op jit(solution)/shard_map/ppermute | solution.py:928
  294.0 34.4 %collective-permute-start.55 = (bf16[512,256]{1,0:T(8,128)(2,1)}, bf16[512,256]{1,0:T(8,128)(2,1)}, u32[]{:S(2)}, u32[]{:S(2)}) collective-permute-start(bf16[512,256]{1,0:T(8,128)(2,1)} %add_convert_fusion.2), channel_id=1, source_target_pairs={{0,2},{1,3},{2,4},{3,5},{4,6},{5,7},{6,0},{7,1},{8,10},{9,11},{10,... | collective-permute-start | bytes 786440 | tf_op jit(solution)/shard_map/ppermute | solution.py:928
  304.1 12.2 %collective-permute-start.48 = (bf16[320,512]{1,0:T(8,128)(2,1)}, bf16[320,512]{1,0:T(8,128)(2,1)S(1)}, u32[]{:S(2)}, u32[]{:S(2)}) collective-permute-start(bf16[320,512]{1,0:T(8,128)(2,1)} %get-tuple-element.98), channel_id=1, source_target_pairs={{0,2},{1,3},{2,4},{3,5},{4,6},{5,7},{6,0},{7,1},{8,10},{9,11},{10,... | collective-permute-start | bytes 983048 | tf_op jit(solution)/shard_map/ppermute | solution.py:928
  305.9 25.0 %collective-permute-start.45 = (bf16[192,512]{1,0:T(8,128)(2,1)}, bf16[192,512]{1,0:T(8,128)(2,1)}, u32[]{:S(2)}, u32[]{:S(2)}) collective-permute-start(bf16[192,512]{1,0:T(8,128)(2,1)} %add_convert_fusion.4), channel_id=1, source_target_pairs={{0,2},{1,3},{2,4},{3,5},{4,6},{5,7},{6,0},{7,1},{8,10},{9,11},{10,... | collective-permute-start | bytes 589832 | tf_op jit(solution)/shard_map/ppermute | solution.py:928
  316.3 29.0 %collective-permute-start.30 = (bf16[2,192,1024]{2,1,0:T(8,128)(2,1)}, bf16[2,192,1024]{2,1,0:T(8,128)(2,1)}, u32[]{:S(2)}, u32[]{:S(2)}) collective-permute-start(bf16[2,192,1024]{2,1,0:T(8,128)(2,1)} %slice.79), channel_id=1, source_target_pairs={{0,1},{1,0},{2,3},{3,2},{4,5},{5,4},{6,7},{7,6},{8,9},{9,8},{10,11... | collective-permute-start | bytes 2359304 | tf_op jit(solution)/shard_map/ppermute | solution.py:928
  318.6 8.9 %collective-permute-start.49 = (bf16[320,512]{1,0:T(8,128)(2,1)S(1)}, bf16[320,512]{1,0:T(8,128)(2,1)S(1)}, u32[]{:S(2)}, u32[]{:S(2)}) collective-permute-start(bf16[320,512]{1,0:T(8,128)(2,1)S(1)} %add_convert_fusion.1), channel_id=1, source_target_pairs={{0,2},{1,3},{2,4},{3,5},{4,6},{5,7},{6,0},{7,1},{8,10},{9,11},{10,... | collective-permute-start | bytes 983048 | tf_op jit(solution)/shard_map/ppermute | solution.py:928
  327.5 23.4 %collective-permute-start.36 = (bf16[2,192,1024]{2,1,0:T(8,128)(2,1)S(1)}, bf16[2,192,1024]{2,1,0:T(8,128)(2,1)}, u32[]{:S(2)}, u32[]{:S(2)}) collective-permute-start(bf16[2,192,1024]{2,1,0:T(8,128)(2,1)S(1)} %slice.78), channel_id=1, source_target_pairs={{0,1},{1,0},{2,3},{3,2},{4,5},{5,4},{6,7},{7,6},{8,9},{9,8},{10,11... | collective-permute-start | bytes 2359304 | tf_op jit(solution)/shard_map/ppermute | solution.py:928
  328.5 13.6 %collective-permute-start.50 = (bf16[320,512]{1,0:T(8,128)(2,1)}, bf16[320,512]{1,0:T(8,128)(2,1)S(1)}, u32[]{:S(2)}, u32[]{:S(2)}) collective-permute-start(bf16[320,512]{1,0:T(8,128)(2,1)} %add_convert_fusion), channel_id=1, source_target_pairs={{0,2},{1,3},{2,4},{3,5},{4,6},{5,7},{6,0},{7,1},{8,10},{9,11},{10,... | collective-permute-start | bytes 983048 | tf_op jit(solution)/shard_map/ppermute | solution.py:928
  (45 other events, 332.8 us)

commit v2 on v1

--- a/solution.py
+++ b/solution.py
@@ -420,9 +420,10 @@
 class Rows:
     def __init__(self, scal, seq, chunk, docs):
         rows = chunk // 2
-        self.here = scal[1] * chunk
-        low = self.here + scal[2] * rows
-        high = self.here + (1 - scal[2]) * rows - rows
+        self.here = (scal[1] * 2 + (scal[2] // 2 + seq) % 2) * chunk
+        side = scal[2] % 2
+        low = self.here + side * rows
+        high = self.here + (1 - side) * rows - rows
 
         def places(shape, axis):
             count = lax.broadcasted_iota(jnp.int32, shape, axis)
@@ -471,18 +472,22 @@
     return jax.ShapeDtypeStruct(shape, kind)
 
 
-def call(name, body, scal, grid, ins, outs, scratch=()):
+def call(name, body, scal, grid, ins, outs, scratch=(), aliases=None):
     return pl.pallas_call(
         body,
         name=name,
         grid_spec=pltpu.PrefetchScalarGridSpec(
             num_scalar_prefetch=1,
             grid=grid or (1,),
-            in_specs=[pl.BlockSpec(block, index) for _, block, index in ins],
+            in_specs=[
+                pl.BlockSpec(block, index) if index else pl.BlockSpec(memory_space=pl.ANY)
+                for _, block, index in ins
+            ],
             out_specs=[pl.BlockSpec(block, index) for _, block, index in outs],
             scratch_shapes=list(scratch),
         ),
         out_shape=[array for array, _, _ in outs],
+        input_output_aliases=aliases or {},
         compiler_params=pltpu.CompilerParams(
             dimension_semantics=("arbitrary",) * max(len(grid), 1), vmem_limit_bytes=VMEM_LIMIT
         ),
@@ -528,33 +533,9 @@
     send_d[...] = jnp.where(low, down[half:, :], down[:half, :])
 
 
-def join_a_body(scal, keep, got, block):
-    low = scal[3] == 0
-    size = keep.shape[1]
-    block[:, :size] = jnp.where(low, keep[...], got[...])
-    block[:, size:] = jnp.where(low, got[...], keep[...])
-
-
-def join_u_body(scal, up, got, block):
-    low = scal[3] == 0
-    rows, half = up.shape[0], up.shape[1] // 2
-    keep = jnp.where(low, up[:, :half], up[:, half:])
-    block[:rows, :] = jnp.where(low, keep, got[...])
-    block[rows:, :] = jnp.where(low, got[...], keep)
-
-
-def join_d_body(scal, down, got, block):
-    low = scal[3] == 0
-    cols, half = down.shape[1], down.shape[0] // 2
-    keep = jnp.where(low, down[:half, :], down[half:, :])
-    block[:, :cols] = jnp.where(low, keep, got[...])
-    block[:, cols:] = jnp.where(low, got[...], keep)
-
-
-def norm_body(scal, own, away, g1, b1, g2, b2, one, two):
-    own_turn = pl.program_id(0) < pl.num_programs(0) // 2
-    x = jnp.where(own_turn, own[0], away[0]).astype(F32)
-    n, _ = normalize(x)
+def norm_body(scal, rows, g1, b1, g2, b2, *refs):
+    one, two = refs[-2:]
+    n, _ = normalize(rows[0].astype(F32))
     one[0] = (n * g1[...] + b1[...]).astype(BF16)
     two[0] = (n * g2[...] + b2[...]).astype(BF16)
 
@@ -607,7 +588,7 @@
         jnp.sum(totals, axis=0, keepdims=True), (STATE_ROWS - HEAD_DIM, sh.width)
     )
     state = jnp.concatenate([diag_blocks(sums), tail], axis=0)
-    st_out[0] = pltpu.roll(state, scal[1] * sh.hu, 1)
+    st_out[0] = pltpu.roll(state, scal[1] * sh.hu, 1).astype(BF16)
 
 
 def load_state(sh, scal, carry):
@@ -634,31 +615,29 @@
     slope_out[0] = (cdf + hidden * bell).astype(BF16)
 
 
-def fill_out(sh, blocks_a, blocks_d, wo, wd):
-    fill_rows(sh, wo, blocks_a, 3 * sh.hu, sh.hu, 0)
-    fill_rows(sh, wd, blocks_d, 0, sh.hf, 0)
-
-
-def branch_body(sh, scal, num, den, fq, carry, act, *refs):
-    count = sh.pairs * sh.chunks
-    blocks_a, blocks_d = refs[:count], refs[count : 2 * count]
-    ctx_out, rden_out, own_out, away_out, wo, wd = refs[2 * count :]
-    seq = pl.program_id(0)
-
-    @pl.when(seq == 0)
-    def _():
-        fill_out(sh, blocks_a, blocks_d, wo, wd)
-
+def finish_body(sh, scal, num, den, fq, carry, ctx_out, rden_out):
     fqb = fq[0]
     sums, totals = load_state(sh, scal, carry)
     more_num = mm(fqb, block_diag(sums).astype(BF16))
     more_den = head_sums(fqb.astype(F32) * totals)
-    came = Rows(scal, seq, sh.chunk, sh.docs).came
+    came = Rows(scal, pl.program_id(0), sh.chunk, sh.docs).came
     inverse = 1.0 / (den[0] + jnp.where(came, more_den, 0.0))
-    ctx = (num[0] + jnp.where(came, more_num, 0.0)) * inverse
-    ctx_out[0] = ctx
+    ctx_out[0] = (num[0] + jnp.where(came, more_num, 0.0)) * inverse
     rden_out[0] = inverse
-    ctxb = ctx.astype(BF16)
+
+
+def branch_body(sh, scal, ctx, act, *refs):
+    count = sh.pairs * sh.chunks
+    blocks_a, blocks_d = refs[:count], refs[count : 2 * count]
+    own_out, away_out, wo, wd = refs[2 * count :]
+    seq = pl.program_id(0)
+
+    @pl.when(seq == 0)
+    def _():
+        fill_rows(sh, wo, blocks_a, 3 * sh.hu, sh.hu, 0)
+        fill_rows(sh, wd, blocks_d, 0, sh.hf, 0)
+
+    ctxb = ctx[0].astype(BF16)
     half = pl.num_programs(0) // 2
     for slot in range(sh.pairs):
         part = (mm(act[0], wd[slot]) + mm(ctxb, wo[slot])).astype(BF16)
@@ -715,33 +694,20 @@
     dn_high, dn_low = split(dnum)
     v_high, v_low = split(v)
     dd_high = dden.astype(BF16).astype(F32)
-    roll = lambda values, steps: pltpu.roll(values, steps * HEAD_DIM, 1)
+    roll = lambda values: pltpu.roll(values.astype(F32), HEAD_DIM, 1).astype(BF16)
     den_part = jnp.where(lane == 0, dd_high, jnp.where(lane == 1, dden - dd_high, 0.0))
-    left = [
-        dn_high,
-        roll(dn_low.astype(F32), 1).astype(BF16),
-        roll(den_part, 2).astype(BF16),
-        roll(dn_high.astype(F32), 3).astype(BF16),
-    ]
-    right = [
-        v_high,
-        roll(v_high.astype(F32), 1).astype(BF16),
-        jnp.ones(v.shape, BF16),
-        roll(v_low.astype(F32), 3).astype(BF16),
-    ]
-
-    def lay_out(parts, head):
-        group = (lanes - head) & 3
-        low = jnp.where(group == 0, parts[0], parts[1])
-        high = jnp.where(group == 2, parts[2], parts[3])
-        return jnp.where(group < 2, low, high)
+    den_part = den_part.astype(BF16)
+    dn_high_beside, dn_low_beside = roll(dn_high), roll(dn_low)
+    v_high_beside, v_low_beside = roll(v_high), roll(v_low)
 
     dfq = jnp.zeros(v.shape, F32)
     dfk = jnp.zeros(v.shape, F32)
     dv = jnp.zeros(v.shape, F32)
     for head in range(width // HEAD_DIM):
         mine = lanes == head
-        dscores = mm(lay_out(left, head), lay_out(right, head), NT)
+        left = [jnp.where(mine, dn_high, dn_low_beside), jnp.where(mine, den_part, dn_high_beside)]
+        right = [jnp.where(mine, v_high, v_high_beside), jnp.where(mine, 1, v_low_beside)]
+        dscores = mm(jnp.concatenate(left, axis=1), jnp.concatenate(right, axis=1), NT)
         dscores = jnp.where(mask, dscores, 0.0).astype(BF16)
         scores = mm(jnp.where(mine, fqb, 0), fkb, NT)
         scores = jnp.where(mask, scores, 0.0).astype(BF16)
@@ -772,48 +738,37 @@
     dk_out[0] = turn(turned, cos[0], -sin[0]).astype(BF16)
 
 
-def down_grad_body(sh, with_got, scal, act, ctx, own, away, *refs):
+def unit_grad_body(with_got, scal, left, *refs):
+    many, with_got = with_got
+    rights, refs = refs[:many], refs[many:]
+    at, grad = 0, None
+    for right in rights:
+        part = mm(left[at : at + right.shape[0], :], right[...], TN)
+        at += right.shape[0]
+        grad = part if grad is None else grad + part
+    if not with_got:
+        refs[0][0] = grad.astype(BF16)
+        return
+    value = (grad + refs[0][0].astype(F32)).astype(BF16)
+    j = pl.program_id(0)
+    for step, out in enumerate(refs[1:]):
+
+        @pl.when(j == step)
+        def _():
+            out[...] = value
+
+
+def head_grad_body(sh, with_got, scal, dq, dk, dv, ctx, normed, own, away, *refs):
+    scratch = refs[-1]
+    for kind, ref in enumerate((dq, dk, dv)):
+        scratch[kind] = mm(ref[...], normed[...], TN)
     half = own.shape[0]
-    scratch = refs[-1]
-    j = pl.program_id(0)
-
-    @pl.when(j == 0)
-    def _():
-        scratch[...] = mm(ctx[:half, :].astype(BF16), own[...], TN) + mm(
-            ctx[half:, :].astype(BF16), away[...], TN
-        )
-
-    grad = mm(act[:half, :], own[...], TN) + mm(act[half:, :], away[...], TN)
-    low = scratch[pl.ds(pl.multiple_of(j * sh.hu, 8), sh.hu), :]
-    store_block(with_got, refs[:-1], (grad, low), j)
-
-
-def store_block(with_got, refs, parts, j):
-    at = 0
-    for part in parts:
-        rows = slice(at, at + part.shape[0])
-        at += part.shape[0]
-        if not with_got:
-            refs[0][0, rows, :] = part.astype(BF16)
-            continue
-        value = (part + refs[0][0, rows, :].astype(F32)).astype(BF16)
-        for step, out in enumerate(refs[1:]):
-
-            @pl.when(j == step)
-            def _():
-                out[rows, :] = value
-
-
-def up_grad_body(sh, with_got, scal, normed, grad, *refs):
-    store_block(with_got, refs, (mm(normed[...], grad[...], TN),), pl.program_id(0))
-
-
-def qkv_grad_body(sh, with_got, scal, dq, dk, dv, normed, *refs):
-    for kind, ref in enumerate((dq, dk, dv)):
-        refs[-1][kind] = mm(ref[...], normed[...], TN)
+    scratch[3] = mm(ctx[:half, :].astype(BF16), own[...], TN) + mm(
+        ctx[half:, :].astype(BF16), away[...], TN
+    )
     for j in range(sh.chunks):
         rows = slice(j * sh.hu, (j + 1) * sh.hu)
-        value = jnp.concatenate([refs[-1][kind, rows, :] for kind in range(3)], axis=0)
+        value = jnp.concatenate([scratch[kind, rows, :] for kind in range(4)], axis=0)
         if with_got:
             refs[1 + j][...] = (value + refs[0][j].astype(F32)).astype(BF16)
         else:
@@ -866,72 +821,53 @@
     out[0] = cot[0].astype(F32) + scale * (e - shift)
 
 
-def cut_cols_body(scal, first, second, keep, send):
-    total = (first[...].astype(F32) + second[...].astype(F32)).astype(BF16)
-    half = total.shape[1] // 2
-    low = scal[3] == 0
-    keep[...] = jnp.where(low, total[:, :half], total[:, half:])
-    send[...] = jnp.where(low, total[:, half:], total[:, :half])
-
-
-def cut_rows_body(scal, first, second, keep, send):
-    total = (first[...].astype(F32) + second[...].astype(F32)).astype(BF16)
-    half = total.shape[0] // 2
-    low = scal[3] == 0
-    keep[...] = jnp.where(low, total[:half], total[half:])
-    send[...] = jnp.where(low, total[half:], total[:half])
-
-
-def end_down_body(sh, scal, keep, got, down, out):
+def join_units(scal, keep, got):
     low = scal[3] == 0
     mine, other = keep[...].astype(F32), got[...].astype(F32)
-    first, second = jnp.where(low, mine, other), jnp.where(low, other, mine)
-    down[: sh.hf, :] = first[: sh.hf]
-    down[sh.hf :, :] = second[: sh.hf]
-    out[: sh.hu, :] = first[sh.hf :]
-    out[sh.hu :, :] = second[sh.hf :]
-
-
-def end_up_body(sh, scal, keep, got, up):
-    low = scal[3] == 0
-    mine, other = keep[...].astype(F32), got[...].astype(F32)
-    up[:, : sh.hf] = jnp.where(low, mine, other)
-    up[:, sh.hf :] = jnp.where(low, other, mine)
-
-
-def end_qkv_body(sh, scal, keep, got, *outs):
-    low = scal[3] == 0
-    mine, other = keep[...].astype(F32), got[...].astype(F32)
-    first, second = jnp.where(low, mine, other), jnp.where(low, other, mine)
-    for kind, out in enumerate(outs):
+    return jnp.where(low, mine, other), jnp.where(low, other, mine)
+
+
+def end_units_body(sh, scal, keep_u, got_u, keep_d, got_d, up, down):
+    first, second = join_units(scal, keep_u, got_u)
+    up[:, : sh.hf] = jnp.transpose(first)
+    up[:, sh.hf :] = jnp.transpose(second)
+    first, second = join_units(scal, keep_d, got_d)
+    down[: sh.hf, :] = first
+    down[sh.hf :, :] = second
+
+
+def end_heads_body(sh, scal, keep, got, *outs):
+    first, second = join_units(scal, keep, got)
+    for kind in range(4):
         rows = slice(kind * sh.hu, (kind + 1) * sh.hu)
-        out[...] = jnp.transpose(jnp.concatenate([first[rows], second[rows]], axis=0))
+        both = jnp.concatenate([first[rows], second[rows]], axis=0)
+        outs[kind][...] = both if kind == 3 else jnp.transpose(both)
 
 
 class Layout:
     def __init__(self):
         self.seqs, self.parts = lax.axis_size("seq"), lax.axis_size("mp")
-        self.pairs, self.chunks = self.seqs // 2, self.parts // 2
+        self.pairs, self.chunks = self.seqs // 2, self.parts // 4
         seq, part = lax.axis_index("seq"), lax.axis_index("mp")
         self.pair, self.core = seq // 2, seq % 2
-        self.hi, self.lo = part // 2, part % 2
+        self.hi, self.lo = part // 4, part % 4
 
     def move(self, values, rule):
         links = []
         for seq in range(self.seqs):
             for part in range(self.parts):
-                there = rule(seq // 2, seq % 2, part // 2, part % 2)
+                there = rule(seq // 2, seq % 2, part // 4, part % 4)
                 if there is not None:
                     pair, core, hi, lo = there
-                    goal = (pair * 2 + core) * self.parts + hi * 2 + lo
+                    goal = (pair * 2 + core) * self.parts + hi * 4 + lo
                     links.append((seq * self.parts + part, goal))
         return lax.ppermute(values, AXES, links)
 
     def core_swap(self, values):
         return self.move(values, lambda p, c, h, l: (p, 1 - c, h, l))
 
-    def lo_swap(self, values):
-        return self.move(values, lambda p, c, h, l: (p, c, h, 1 - l))
+    def lo_swap(self, values, bit):
+        return self.move(values, lambda p, c, h, l: (p, c, h, l ^ bit))
 
     def pair_step(self, values, way):
         return self.move(values, lambda p, c, h, l: ((p + way) % self.pairs, c, h, l))
@@ -940,48 +876,40 @@
         return self.move(values, lambda p, c, h, l: (p, c, (h + way) % self.chunks, l))
 
 
-def gather_blocks(lay, block):
-    ring = [block]
-    for _ in range(lay.chunks - 1):
-        ring.append(lay.hi_step(ring[-1], -1))
-    blocks = list(ring)
-    for _ in range(lay.pairs - 1):
-        ring = [lay.pair_step(part, -1) for part in ring]
-        blocks += ring
-    return blocks
-
-
-def combine_states(lay, local, straddles, size, backward):
-    reach = local
-    found = jnp.zeros_like(local)
-    step = 1
-    while step < lay.chunks:
-        base = (lay.hi // (2 * step)) * (2 * step)
-        upper = (lay.hi & step) > 0
-        middle = (base + step) * size
-        last = step * 2 >= lay.chunks
-
-        def rule(p, c, h, l, step=step, last=last):
-            sender = ((h & step) == 0) != backward
-            return (p, c, h ^ step, l) if sender or not last else None
-
-        got = lay.move(reach.astype(BF16), rule).astype(F32)
-        scale = lambda edge: straddles(middle, edge)[:, None, None]
-        if backward:
-            here = (lay.hi + 1) * size
-            keeps = jnp.where(upper, 0.0, scale(here))
-            edge = base * size
-        else:
-            here = lay.hi * size
-            keeps = jnp.where(upper, scale(here), 0.0)
-            edge = (base + 2 * step) * size
-        found = found + keeps * got
-        if not last:
-            far = scale(edge)
-            mine_far = upper if backward else jnp.logical_not(upper)
-            reach = jnp.where(mine_far, far * reach + got, reach + far * got)
-        step *= 2
-    return found
+def after(value, *others):
+    return lax.optimization_barrier((value,) + others)[0]
+
+
+def hold(values, *others):
+    return lax.optimization_barrier(tuple(values) + others)[: len(values)]
+
+
+def in_order(lay, one, two):
+    flip = lay.lo >= 2
+    return jnp.where(flip, two, one), jnp.where(flip, one, two)
+
+
+def send_states(lay, local, scale, backward):
+    states = local.astype(F32).reshape((-1, 2) + local.shape[1:])
+    first, second = in_order(lay, states[:, 0], states[:, 1])
+    if backward:
+        out, goal = first + second * scale(0, 1), 0
+    else:
+        out, goal = second + first * scale(1, 2), 1
+    return lay.move(
+        out.astype(BF16), lambda p, c, h, l: (p, c, goal, l) if h != goal else None
+    )
+
+
+def combine_states(lay, local, got, scale, backward):
+    states = local.astype(F32).reshape((-1, 2) + local.shape[1:])
+    first, second = in_order(lay, states[:, 0], states[:, 1])
+    got = got.astype(F32)
+    if backward:
+        first, second = second + got * scale(1, 2), got
+    else:
+        first, second = got, first + got * scale(0, 1)
+    return jnp.stack(in_order(lay, first, second), 1).reshape(local.shape)
 
 
 def erf_inverse(target):
@@ -1039,16 +967,18 @@
     half_units, half_ff = units // 2, up_weight.shape[1] // 2
     sh = Shape(lay.pairs, lay.chunks, dim, half_units, half_ff, chunk, docs)
     width, ff, dp = sh.width, sh.ff, sh.dp
-    count = 2 * micro
+    half = 2 * micro
+    count = 2 * half
     total = count * chunk
     whole_rows = lambda array: array.reshape(total, array.shape[-1])
     bind = lambda body, *first: functools.partial(body, *first)
     gains = [vec.reshape(1, dim) for vec in (ln1_gain, ln1_bias, ln2_gain, ln2_bias)]
 
     own_lengths = lengths[:, 0]
-    table = jnp.stack([own_lengths, lay.core_swap(own_lengths)]).reshape(count, docs)
-    ends = jnp.cumsum(table, axis=1)
-    starts = ends - table
+    table = jnp.stack([own_lengths, lay.core_swap(own_lengths)]).reshape(half, docs)
+    seq_ends = jnp.cumsum(table, axis=1)
+    seq_starts = seq_ends - table
+    starts, ends = jnp.repeat(seq_starts, 2, axis=0), jnp.repeat(seq_ends, 2, axis=0)
     scal = jnp.concatenate(
         [
             jnp.stack([lay.pair, lay.hi, lay.lo, lay.core]).astype(jnp.int32),
@@ -1064,42 +994,55 @@
         [whole(w) for w in (q_weight, k_weight, value_weight, out_weight, up_weight, down_weight)],
         [whole(new(shape, BF16)) for shape in [block_shape[0]] + block_shape],
     )
-    got_a = lay.core_swap(send_a)
-    tokens_beside = lay.lo_swap(tokens)
-    (block,) = call(
-        "join_a", join_a_body, core_only, (), [whole(keep_a), whole(got_a)],
-        [whole(new((4 * half_units, 2 * drows), BF16))],
-    )
-    blocks_a = gather_blocks(lay, block)
-    got_u = lay.core_swap(send_u)
-    (block,) = call(
-        "join_u", join_u_body, core_only, (), [whole(up_weight), whole(got_u)],
-        [whole(new((2 * drows, half_ff), BF16))],
-    )
-    blocks_u = gather_blocks(lay, block)
-    got_d = lay.core_swap(send_d)
-    (block,) = call(
-        "join_d", join_d_body, core_only, (), [whole(down_weight), whole(got_d)],
-        [whole(new((half_ff, 2 * drows), BF16))],
-    )
-    blocks_d = gather_blocks(lay, block)
-    in_a, in_u, in_d = ([whole(b) for b in blocks] for blocks in (blocks_a, blocks_u, blocks_d))
-
-    def pair_rows(values, beside):
-        own = jnp.stack([values, beside], 1).reshape(micro, chunk, dim)
+    first_core = lay.core == 0
+
+    def join(keep, got, axis):
+        return jnp.where(
+            first_core, jnp.concatenate([keep, got], axis), jnp.concatenate([got, keep], axis)
+        )
+
+    got_a, got_u, got_d = lax.optimization_barrier(
+        tuple(lay.core_swap(send) for send in (send_a, send_u, send_d))
+    )
+    block_a = join(keep_a, got_a, 1)
+    split_at = micro // 2
+
+    def first_swaps(values):
+        return lay.lo_swap(values, 1), lay.lo_swap(values, 2)
+
+    def second_swaps(by_y, by_z):
+        return lay.lo_swap(by_z[:split_at], 1), lay.lo_swap(by_y[split_at:], 2)
+
+    def team_rows(values, by_y, by_z, both):
+        both = jnp.concatenate(both, 0)
+        own = jnp.stack([jnp.stack([values, by_y], 1), jnp.stack([by_z, both], 1)], 1)
+        own = own.reshape(half, chunk, dim)
         return own, lay.core_swap(own)
 
-    x_own, x_away = pair_rows(tokens, tokens_beside)
-    g_own, g_away = pair_rows(cotangent, lay.lo_swap(cotangent))
-
-    here = lay.hi * chunk
+    def cross(values):
+        return lay.pair_step(values, -1)
+
+    def beside(values):
+        return lay.hi_step(values, -1)
+
+    block_a, own_tokens = hold((block_a, tokens), got_a)
+    by_y, by_z = first_swaps(own_tokens)
+    beside_a, cross_a = beside(block_a), cross(block_a)
+    late_up, late_down = hold((up_weight, down_weight), block_a)
+    keep_u = jnp.where(first_core, late_up[:, :half_ff], late_up[:, half_ff:])
+    keep_d = jnp.where(first_core, late_down[:half_ff], late_down[half_ff:])
+    block_u, block_d = join(keep_u, got_u, 0), join(keep_d, got_d, 1)
+    cross_u = cross(block_u)
+
+    here = (2 * lay.hi + (lay.lo // 2 + jnp.arange(count, dtype=jnp.int32)) % 2) * chunk
     step = jnp.arange(rows, dtype=jnp.int32)
-    places = jnp.concatenate([here + lay.lo * rows + step, here + (1 - lay.lo) * rows + step])
+    side = (lay.lo % 2) * rows
+    places = here[:, None] + jnp.concatenate([side + step, rows - side + step])[None, :]
     start = jnp.zeros((count, chunk), jnp.int32)
     for doc in range(docs):
         first = starts[:, doc : doc + 1]
-        start = jnp.where(places[None, :] >= first, first, start)
-    offset = (places[None, :] - start).astype(F32)
+        start = jnp.where(places >= first, first, start)
+    offset = after((places - start).astype(F32), block_a)
     lane = np.arange(128) % HEAD_DIM
     turned = lane < ROT
     inverse = np.where(turned, 10000.0 ** (-(lane % (ROT // 2)) * 2.0 / ROT), 0.0)
@@ -1107,70 +1050,75 @@
     angles = offset[:, :, None] * jnp.asarray(inverse, F32)[None, None, :]
     cos = jnp.cos(angles)
     sin = jnp.sin(angles) * jnp.asarray(side, F32)[None, None, :]
+    cos, sin = lax.optimization_barrier((cos, sin))
+
+    by_y, by_z, beside_a, cross_a, cross_u, block_d, cos, sin = hold(
+        (by_y, by_z, beside_a, cross_a, cross_u, block_d, cos, sin)
+    )
+    both = second_swaps(by_y, by_z)
+    across_a, cross_d = cross(beside_a), cross(block_d)
+    both = hold(both, across_a)
+    x_own, x_away = team_rows(tokens, by_y, by_z, both)
+
     high, low, weighting = tables(width // HEAD_DIM)
     maps = [whole(jnp.asarray(high)), whole(jnp.asarray(low))]
     turns = [by_seq(cos), by_seq(sin)]
 
     def straddles(first, second):
         lower, higher = jnp.minimum(first, second), jnp.maximum(first, second)
-        return jnp.any((starts < lower) & (ends > higher), axis=1).astype(F32)
+        return jnp.any((seq_starts < lower) & (seq_ends > higher), axis=1).astype(F32)
+
+    edges = [(2 * lay.hi + step) * chunk for step in range(3)]
+    scale = lambda a, b: straddles(edges[a], edges[b])[:, None, None]
 
     rows_new = lambda size, kind: by_seq(new((count, chunk, size), kind))
-    state_new = by_seq(new((count, STATE_ROWS, width), F32))
+    state_new = by_seq(new((count, STATE_ROWS, width), BF16))
+    norm_ins = [whole(vec) for vec in gains]
+    norm_outs = [rows_new(dim, BF16), rows_new(dim, BF16)]
     n_one, n_two = call(
-        "norms", norm_body, scal, (count,),
-        [own_seq(x_own), away_seq(x_away)] + [whole(vec) for vec in gains],
-        [rows_new(dim, BF16), rows_new(dim, BF16)],
-    )
+        "norms_own", norm_body, core_only, (half,), [by_seq(x_own)] + norm_ins, norm_outs
+    )
+    n_one, n_two, x_away, block_u, cross_u, block_d, cross_d, cot = hold(
+        (n_one, n_two, x_away, block_u, cross_u, block_d, cross_d, cotangent)
+    )
+    beside_u, across_u = beside(block_u), beside(cross_u)
+    cot_y, cot_z = first_swaps(cot)
+    beside_d = beside(block_d)
+    rest = lambda i, s: (i + half, 0, 0)
+    n_one, n_two = call(
+        "norms_away", norm_body, core_only, (half,),
+        [by_seq(x_away)] + norm_ins + [(n_one, None, None), (n_two, None, None)],
+        [(array, block, rest) for array, block, _ in norm_outs], aliases={6: 0, 7: 1},
+    )
+    in_a = [whole(block) for block in (block_a, beside_a, cross_a, across_a)]
     fq, fk, vals, num, den, state = call(
         "attend", bind(attend_body, sh), scal, (count,),
         [by_seq(n_one)] + turns + maps + [whole(jnp.asarray(weighting))] + in_a,
         [rows_new(width, BF16)] * 2 + [rows_new(width, F32)] * 3 + [state_new],
         [pltpu.VMEM((sh.pairs, 3 * width, dp), BF16)],
     )
-    carry = combine_states(lay, state, straddles, chunk, False)
+    n_two, fq, state, beside_u, across_u, cot_y, cot_z = hold(
+        (n_two, fq, state, beside_u, across_u, cot_y, cot_z)
+    )
+    in_u = [whole(block) for block in (block_u, beside_u, cross_u, across_u)]
+    state_got = send_states(lay, state, scale, False)
+    cot_both = second_swaps(cot_y, cot_z)
     act, slope = call(
         "up", bind(up_body, sh), scal, (count,), [by_seq(n_two)] + in_u,
         [rows_new(ff, BF16)] * 2, [pltpu.VMEM((sh.pairs, dp, ff), BF16)],
     )
-    out_scratch = [
-        pltpu.VMEM((sh.pairs, width, dp), BF16), pltpu.VMEM((sh.pairs, ff, dp), BF16)
-    ]
-    halves_new = [
-        own_seq(new((micro, chunk, dim), BF16)), away_seq(new((micro, chunk, dim), BF16))
-    ]
-    ctx, rden, own, away = call(
-        "branch", bind(branch_body, sh), scal, (count,),
-        [by_seq(a) for a in (num, den, fq, carry, act)] + in_a + in_d,
-        [rows_new(width, F32)] * 2 + halves_new, out_scratch,
-    )
-
-    def team_sum(own, away):
-        got = lay.core_swap(away)
-        both = own.astype(F32) + got.astype(F32)
-        return both[:, :rows], lay.lo_swap(both[:, rows:].astype(BF16))
-
-    mine, got = team_sum(own, away)
-    mixed = (tokens.astype(F32) + mine + got.astype(F32)).astype(BF16)
-
-    (grad_hidden,) = call(
-        "hidden_grad", bind(hidden_body, sh), scal, (count,),
-        [own_seq(g_own), away_seq(g_away), by_seq(slope)] + in_d,
-        [rows_new(ff, BF16)], [pltpu.VMEM((sh.pairs, ff, dp), BF16)],
-    )
-    dq, dk_part, dv_part, dstate = call(
-        "attend_back", bind(back_body, sh), scal, (count,),
-        [own_seq(g_own), away_seq(g_away)]
-        + [by_seq(a) for a in (fq, fk, vals, ctx, rden, carry)] + turns + maps + in_a,
-        [rows_new(width, BF16), rows_new(width, F32), rows_new(width, F32), state_new],
-        [pltpu.VMEM((sh.pairs, width, dp), BF16)],
-    )
-    dcarry = combine_states(lay, dstate, straddles, chunk, True)
-    dk, dv = call(
-        "keys_back", bind(last_body, sh), scal, (count,),
-        [by_seq(a) for a in (dk_part, dv_part, fk, vals, dcarry)] + turns + maps,
-        [rows_new(width, BF16)] * 2,
-    )
+    act, num, state_got, beside_d, cot_both0, cot_both1 = hold(
+        (act, num, state_got, beside_d) + cot_both
+    )
+    across_d = cross(beside_d)
+    g_own, g_away = team_rows(cotangent, cot_y, cot_z, (cot_both0, cot_both1))
+    carry = combine_states(lay, state, state_got, scale, False)
+    ctx, rden = call(
+        "finish", bind(finish_body, sh), scal, (count,),
+        [by_seq(a) for a in (after(num, g_own), den, fq, carry)], [rows_new(width, F32)] * 2,
+    )
+    g_own, g_away, ctx, across_d = hold((g_own, g_away, ctx, across_d))
+    in_d = [whole(block) for block in (block_d, beside_d, cross_d, across_d)]
 
     def cols_of(array, slot):
         pairs = sh.pairs
@@ -1184,20 +1132,42 @@
         rest = tuple(array.shape[1:])
         return (array, (1,) + rest, lambda j, s: (j,) + (0,) * len(rest))
 
-    def scatter(name, body, shape, ins, scratch, grid):
+    g_rows = [g.reshape(total // 2, dim) for g in (g_own, g_away)]
+    unit_shape, head_shape = (half_ff, dp), (4 * half_units, dp)
+
+    def unit_grads(name, left, rights, slot, got=None):
+        final = slot == 0
+        outs = [whole(new(unit_shape, BF16))] * sh.chunks
+        if not final:
+            outs = [block_of(new((sh.chunks,) + unit_shape, BF16))]
+        return call(
+            name + str(slot), bind(unit_grad_body, (len(rights), got is not None)), scal,
+            (sh.chunks,),
+            [lanes_of(left, half_ff)] + [cols_of(right, slot) for right in rights]
+            + ([] if got is None else [block_of(got)]),
+            outs,
+        )
+
+    def head_grads(parts, slot, got=None):
+        final = slot == 0
+        outs = [whole(new(head_shape, BF16))] * sh.chunks
+        if not final:
+            outs = [whole(new((sh.chunks,) + head_shape, BF16))]
+        return call(
+            "head_grad" + str(slot), bind(head_grad_body, sh, got is not None), scal, (),
+            [whole(whole_rows(a)) for a in parts] + [cols_of(whole_rows(n_one), slot)]
+            + [cols_of(g, slot) for g in g_rows] + ([] if got is None else [whole(got)]),
+            outs, [pltpu.VMEM((4, width, dp), F32)],
+        )
+
+    def pair_sums(make):
         got = None
-        for slot in range(sh.pairs - 1, -1, -1):
-            stacked = new((sh.chunks,) + shape, BF16)
-            take = block_of if grid else whole
-            extra = [] if got is None else [take(got)]
-            final = slot == 0
-            outs = [whole(new(shape, BF16))] * sh.chunks if final else [take(stacked)]
-            parts = call(
-                name + str(slot), bind(body, sh, got is not None), scal, grid,
-                ins(slot) + extra, outs, scratch,
-            )
-            if not final:
-                got = lay.pair_step(parts[0], 1)
+        for slot in range(sh.pairs - 1, 0, -1):
+            part = make(slot, got)[0]
+            got = lay.pair_step(part, 1)
+        return part, got
+
+    def hi_sums(parts):
         term = parts[sh.chunks - 1]
         for j in range(sh.chunks - 2, -1, -1):
             term = lay.hi_step(term, 1)
@@ -1205,29 +1175,90 @@
                 term = (term.astype(F32) + parts[j].astype(F32)).astype(BF16)
         return term, parts[0]
 
-    g_rows = [g.reshape(total // 2, dim) for g in (g_own, g_away)]
-    grid = (sh.chunks,)
-    down_ends = scatter(
-        "down_grad", down_grad_body, (half_ff + half_units, dp),
-        lambda slot: [lanes_of(whole_rows(act), half_ff), whole(whole_rows(ctx))]
-        + [cols_of(g, slot) for g in g_rows],
-        [pltpu.VMEM((width, dp), F32)], grid,
-    )
-    up_ends = scatter(
-        "up_grad", up_grad_body, (dp, half_ff),
-        lambda slot: [cols_of(whole_rows(n_two), slot), lanes_of(whole_rows(grad_hidden), half_ff)],
-        [], grid,
-    )
-    qkv_ends = scatter(
-        "qkv_grad", qkv_grad_body, (3 * half_units, dp),
-        lambda slot: [whole(whole_rows(a)) for a in (dq, dk, dv)]
-        + [cols_of(whole_rows(n_one), slot)],
-        [pltpu.VMEM((3, width, dp), F32)], (),
-    )
-
+    def trade(ends, *others):
+        sums = (ends[0].astype(F32) + ends[1].astype(F32)).astype(BF16)
+        first, second = sums[:, :drows], sums[:, drows:]
+        keep = jnp.where(first_core, first, second)
+        send = jnp.where(first_core, second, first)
+        return [whole(keep), whole(lay.core_swap(send))]
+
+    down_make = lambda slot, got: unit_grads("down_grad", whole_rows(act), g_rows, slot, got)
+    down_part, down_got = pair_sums(down_make)
+
+    ctx = after(ctx, down_part)
+    halves_new = [
+        own_seq(new((half, chunk, dim), BF16)), away_seq(new((half, chunk, dim), BF16))
+    ]
+    branch_own, branch_away = call(
+        "branch", bind(branch_body, sh), scal, (count,),
+        [by_seq(ctx), by_seq(act)] + in_a + in_d, halves_new,
+        [pltpu.VMEM((sh.pairs, width, dp), BF16), pltpu.VMEM((sh.pairs, ff, dp), BF16)],
+    )
+
+    def first_sums(own, away_got):
+        both = (own.astype(F32) + away_got.astype(F32)).reshape(micro, 2, 2, rows, dim)
+        by_z, by_y = both[:split_at], both[split_at:]
+        sends = by_z[:, 1].astype(BF16), by_y[:, :, 1].astype(BF16)
+        return (by_z[:, 0].astype(BF16), by_y[:, :, 0].astype(BF16)), sends
+
+    def second_sums(keeps, gots):
+        by_z = keeps[0].astype(F32) + gots[0].astype(F32)
+        by_y = keeps[1].astype(F32) + gots[1].astype(F32)
+        sends = by_z[:, 1].astype(BF16), by_y[:, 1].astype(BF16)
+        return (by_z[:, 0].astype(BF16), by_y[:, 0].astype(BF16)), sends
+
+    def round_one(sends):
+        return lay.lo_swap(sends[0], 2), lay.lo_swap(sends[1], 1)
+
+    def round_two(sends):
+        return lay.lo_swap(sends[0], 1), lay.lo_swap(sends[1], 2)
+
+    join_micro = lambda parts: jnp.concatenate(parts, 0)
+    down_got, branch_own, branch_away, ctx = hold((down_got, branch_own, branch_away, ctx))
+    m_got = lay.core_swap(branch_away)
+
+    dq, dk_part, dv_part, dstate = call(
+        "attend_back", bind(back_body, sh), scal, (count,),
+        [own_seq(g_own), away_seq(g_away)]
+        + [by_seq(a) for a in (fq, fk, vals, ctx, rden, carry)]
+        + turns + maps + in_a,
+        [rows_new(width, BF16), rows_new(width, F32), rows_new(width, F32), state_new],
+        [pltpu.VMEM((sh.pairs, width, dp), BF16)],
+    )
+    branch_own, m_got, dq, dstate = hold((branch_own, m_got, dq, dstate))
+    m_keeps, m_sends = first_sums(branch_own, m_got)
+    m_gots = round_one(m_sends)
+    state_got = send_states(lay, dstate, scale, True)
+    (grad_hidden,) = call(
+        "hidden_grad", bind(hidden_body, sh), scal, (count,),
+        [own_seq(g_own), away_seq(g_away), by_seq(after(slope, *m_sends))] + in_d,
+        [rows_new(ff, BF16)], [pltpu.VMEM((sh.pairs, ff, dp), BF16)],
+    )
+    grad_hidden, state_got = hold((grad_hidden, state_got))
+    dcarry = combine_states(lay, dstate, state_got, scale, True)
+    up_make = lambda slot, got: unit_grads(
+        "up_grad", whole_rows(grad_hidden), [whole_rows(n_two)], slot, got
+    )
+    up_part, up_got = pair_sums(up_make)
+    dk_part, *m_parts = hold((dk_part,) + m_keeps + m_gots, up_part)
+    m_keeps, m_sends = second_sums(m_parts[:2], m_parts[2:])
+    m_gots = round_two(m_sends)
+    dk, dv = call(
+        "keys_back", bind(last_body, sh), scal, (count,),
+        [by_seq(a) for a in (after(dk_part, *m_sends), dv_part, fk, vals, dcarry)]
+        + turns + maps,
+        [rows_new(width, BF16)] * 2,
+    )
+    dk, up_got, *m_parts = hold((dk, up_got) + m_keeps + m_gots)
+    up_parts = up_make(0, up_got)
+    dk, *up_parts = hold((dk,) + tuple(up_parts))
+    up_ends = hi_sums(up_parts)
+    mixed = tokens.astype(F32) + join_micro(m_parts[:2]).astype(F32)
+    mixed = (mixed + join_micro(m_parts[2:]).astype(F32)).astype(BF16)
     own, away, sums = call(
         "rows_grad", bind(rows_grad_body, sh), scal, (count,),
-        [by_seq(a) for a in (dq, dk, dv, grad_hidden)] + [own_seq(x_own), away_seq(x_away)]
+        [by_seq(a) for a in (after(dq, mixed), dk, dv, grad_hidden)]
+        + [own_seq(x_own), away_seq(x_away)]
         + [whole(gains[0]), whole(gains[2])] + in_a + in_u,
         halves_new + [whole(new((8, dim), F32))],
         [
@@ -1236,45 +1267,50 @@
             pltpu.VMEM((chunk, dim), F32),
         ],
     )
-    mine, got = team_sum(own, away)
+    own, away, sums, dq, up_ends = hold((own, away, sums, dq, up_ends))
+    e_got = lay.core_swap(away)
+    sums = sums[:4]
+    sums_got = lay.lo_swap(sums, 1)
+    head_make = lambda slot, got: head_grads((dq, dk, dv, ctx), slot, got)
+    head_part, head_got = pair_sums(head_make)
+    own, e_got, sums_got = hold((own, e_got, sums_got), head_part)
+    sums = sums + sums_got
+    sums_got = lay.core_swap(sums)
+    e_keeps, e_sends = first_sums(own, e_got)
+    e_gots = round_one(e_sends)
+    down_parts = down_make(0, after(down_got, *e_sends))
+    head_got, sums_got, *down_parts = hold((head_got, sums_got) + tuple(down_parts))
+    down_ends = hi_sums(down_parts)
+    sums = sums + sums_got
+    sums_got = lay.move(sums, lambda p, c, h, l: (1 - p, c, h, l))
+    head_parts = head_make(0, after(head_got, sums))
+    e_keep0, e_keep1, e_got0, e_got1, sums_got, down_end0, down_end1, *head_parts = hold(
+        e_keeps + e_gots + (sums_got,) + down_ends + tuple(head_parts)
+    )
+    down_ends = (down_end0, down_end1)
+    sums = sums + sums_got
+    sums_got = lay.lo_swap(sums, 2)
+    head_ends = hi_sums(head_parts)
+    e_keeps, e_sends = second_sums((e_keep0, e_keep1), (e_got0, e_got1))
+    sums_got, *e_sends = hold((sums_got,) + e_sends)
+    e_gots = round_two(e_sends)
+    sums = sums + sums_got
+    units_ends = trade(hold(up_ends, *e_sends)) + trade(hold(down_ends, *e_sends))
+    grads_units = call(
+        "end_units", bind(end_units_body, sh), core_only, (), units_ends,
+        [whole(new(w.shape, F32)) for w in (up_weight, down_weight)],
+    )
+    e_gots = hold(e_gots, grads_units[0])
+    mine, got = join_micro(e_keeps), join_micro(e_gots)
     (grad_tokens,) = call(
         "tokens_grad", tokens_grad_body, scal, (micro,),
         [by_seq(a) for a in (mine, got, tokens, cotangent)],
         [by_seq(new((micro, rows, dim), F32))],
     )
-    sums = sums[:4]
-    sums = sums + lay.core_swap(sums)
-    sums = sums + lay.lo_swap(sums)
-    step = 1
-    while step < lay.pairs:
-        sums = sums + lay.move(sums, lambda p, c, h, l, step=step: (p ^ step, c, h, l))
-        step *= 2
-    step = 1
-    while step < lay.chunks:
-        sums = sums + lay.move(sums, lambda p, c, h, l, step=step: (p, c, h ^ step, l))
-        step *= 2
-
-    def trade(name, body, ends, shape):
-        keep, send = call(
-            name, body, core_only, (), [whole(part) for part in ends],
-            [whole(new(shape, BF16))] * 2,
-        )
-        return [whole(keep), whole(lay.core_swap(send))]
-
-    grad_down, grad_out = call(
-        "end_down", bind(end_down_body, sh), core_only, (),
-        trade("cut_down", cut_cols_body, down_ends, (half_ff + half_units, drows)),
-        [whole(new(down_weight.shape, F32)), whole(new(out_weight.shape, F32))],
-    )
-    (grad_up,) = call(
-        "end_up", bind(end_up_body, sh), core_only, (),
-        trade("cut_up", cut_rows_body, up_ends, (drows, half_ff)),
-        [whole(new(up_weight.shape, F32))],
-    )
+    sums = sums + lay.move(sums, lambda p, c, h, l: (p, c, 1 - h, l))
     grads = call(
-        "end_qkv", bind(end_qkv_body, sh), core_only, (),
-        trade("cut_qkv", cut_cols_body, qkv_ends, (3 * half_units, drows)),
-        [whole(new(q_weight.shape, F32))] * 3,
+        "end_heads", bind(end_heads_body, sh), core_only, (), trade(head_ends),
+        [whole(new(w.shape, F32)) for w in (q_weight, k_weight, value_weight, out_weight)],
     )
     return (
         mixed,
@@ -1286,9 +1322,9 @@
         grads[0],
         grads[1],
         grads[2],
-        grad_out,
-        grad_up,
-        grad_down,
+        grads[3],
+        grads_units[0],
+        grads_units[1],
     )
 
 
@@ -1297,9 +1333,7 @@
 
     def body(*args):
         units = args[5].shape[1]
-        teams = seqs % 2 == 0 and parts % 2 == 0 and (units // HEAD_DIM) % 2 == 0
-        chunks = parts // 2
-        if teams and chunks & (chunks - 1) == 0 and parts * units == 16 * HEAD_DIM:
+        if parts == 8 and seqs == 4 and units == 2 * HEAD_DIM and args[0].shape[0] % 2 == 0:
             return team_local(*args)
         return plain_local(*args)
 

time: 357 us -> 312 us (0.87)
  waiting for transfers between devices: 85.7 us -> 35.7 us
  Pallas kernels: 169 us -> 179 us
  starting transfers between devices: 63.6 us -> 56.4 us
  other arithmetic: 20.8 us -> 25.1 us
    ppermute x57 -> x49, waiting for transfers between devices: 85.7 us -> 35.7 us  [move(): return lax.ppermute(values, AXES, links)]
    pallas_call x25 -> x20, Pallas kernels: 169 us -> 179 us  [call(): pl.pallas_call(body, name=name, grid_spec=pltpu.PrefetchScalarGridSpec(nu...]
    convert_element_type x14 -> x9, other arithmetic: 10.6 us -> 1.78 us  [the longest x1 1.32 us: team_local(): mixed = (mixed + join_micro(m_parts[2:]).astype(F32)).astype(BF16)]
    ppermute x57 -> x49, starting transfers between devices: 63.6 us -> 56.4 us  [move(): return lax.ppermute(values, AXES, links)]
    another operation x4 -> x18, other arithmetic: 1.61 us -> 6.87 us  [the longest x6 3.67 us: team_rows(): jnp.stack([jnp.stack([values, by_y], 1), jnp.stack([by_z, both], 1)], 1)]
    select_n x2 -> x8, other arithmetic: 0.01 us -> 4.05 us  [the longest x3 2.03 us: trade(): send = jnp.where(first_core, second, first)]
    unnamed x72 -> x68, local copies, waits for them, and re-layouts: 8.35 us -> 4.92 us
  transfers between devices with their start and end apart: 57 -> 49, of which waited for: 19 -> 16; matrix products, arithmetic and copies ran while one was open for 7% -> 8% of each run, Pallas kernels for 41% -> 52%
where the time goes in v2:
time: 312 us; the launch traced here: 310 us
  Pallas kernels  179 us (57%)
  starting transfers between devices  56.4 us (18%)
  waiting for transfers between devices  35.7 us (11%)
  other arithmetic  25.1 us (8%)
  local copies, waits for them, and re-layouts  12.6 us (4%)
    pallas_call x20, Pallas kernels, call(): pl.pallas_call(body, name=name, grid_spec=pltpu.PrefetchScalarGridSpec(nu...  179 us
    ppermute x49, starting transfers between devices, move(): return lax.ppermute(values, AXES, links)  56.4 us
    ppermute x49, waiting for transfers between devices, move(): return lax.ppermute(values, AXES, links)  35.7 us
    mul x1, other arithmetic, team_local(): sin = jnp.sin(angles) * jnp.asarray(side, F32)[None, None, :]  6.98 us
  transfers between devices with their start and end apart: 49, of which 16 were waited for; matrix products, arithmetic and copies ran while one was open for 8% of the time, Pallas kernels for 52%

profile of v2, /device:TPU:0, one launch (start us, length us, event | category | flops | bytes accessed | tf_op | source)
XLA Modules:
  0.0 309.7 jit_solution(6243690725363020827)
XLA Ops:
  1.8 2.7 pack.1
  7.6 2.9 collective-permute-start.7
  10.6 2.6 collective-permute-start.6
  13.2 1.6 collective-permute-start.5
  14.8 1.5 collective-permute-start.4
  17.7 7.0 %fusion = (f32[8,384,128]{2,1,0:T(8,128)}, f32[8,384,128]{2,1,0:T(8,128)}) fusion(f32[128]{0:T(128)S(1)} %copy-done.31, f32[128]{0:T(128)S(1)} %copy-done.32, f32[8,384]{1,0:T(8,128)S(1)} %fusion.13), kind=kLoop, calls=%fused_computation.10 | loop fusion | flops 786432 | bytes 3159040 | tf_op jit(solution)/shard_map/mul | solution.py:1052
  25.2 11.6 %collective-permute-done.5 = bf16[2,192,1024]{2,1,0:T(8,128)(2,1)S(1)} collective-permute-done((bf16[2,192,1024]{2,1,0:T(8,128)(2,1)}, bf16[2,192,1024]{2,1,0:T(8,128)(2,1)S(1)}, u32[]{:S(2)}, u32[]{:S(2)}) %collective-permute-start.5) | collective-permute-done | bytes 786464 | tf_op jit(solution)/shard_map/ppermute | solution.py:864
  37.0 1.6 collective-permute-start.9
  40.5 5.9 %collective-permute-done.11.refs_3_ = bf16[256,512]{1,0:T(8,128)(2,1)S(1)} collective-permute-done((bf16[256,512]{1,0:T(8,128)(2,1)S(1)}, bf16[256,512]{1,0:T(8,128)(2,1)S(1)}, u32[]{:S(2)}, u32[]{:S(2)}) %collective-permute-start.11) | collective-permute-done | bytes 262176 | tf_op jit(solution)/shard_map/ppermute | solution.py:864
  50.4 6.9 %norms_own.1 = (bf16[8,384,1024]{2,1,0:T(8,128)(2,1)}, bf16[8,384,1024]{2,1,0:T(8,128)(2,1)}) custom-call(s32[4]{0:T(128)} %stack.104.scal, bf16[4,384,1024]{2,1,0:T(8,128)(2,1)} %bitcast.196, f32[1,1024]{1,0:T(1,128)} %bitcast.220, f32[1,1024]{1,0:T(1,128)} %bitcast.229, f32[1,1024]{1,0:T(1,128)} %bitcast.223, f32[1,1024]{1,0:T(1,128)} %bitcast.231), custom_call_target="tpu_custom_call" | custom-call | tf_op jit(solution)/shard_map/norms_own/pallas_call | solution.py:476
  57.6 1.6 collective-permute-start.17
  59.7 1.6 collective-permute-start.14
  63.4 6.9 %norms_away.1 = (bf16[8,384,1024]{2,1,0:T(8,128)(2,1)}, bf16[8,384,1024]{2,1,0:T(8,128)(2,1)}) custom-call(s32[4]{0:T(128)} %stack.104.scal, bf16[4,384,1024]{2,1,0:T(8,128)(2,1)} %copy-done.3, f32[1,1024]{1,0:T(1,128)} %bitcast.221, f32[1,1024]{1,0:T(1,128)} %bitcast.230, f32[1,1024]{1,0:T(1,128)} %bitcast.224, ...), custom_call_target="tpu_custom_call", output_to_operand_aliasing={{0}: (6, {}), {1}: (7, {})} | custom-call | tf_op jit(solution)/shard_map/norms_away/pallas_call | solution.py:476
  70.3 16.7 %attend.1 = (bf16[8,384,128]{2,1,0:T(8,128)(2,1)}, bf16[8,384,128]{2,1,0:T(8,128)(2,1)}, f32[8,384,128]{2,1,0:T(8,128)}, f32[8,384,128]{2,1,0:T(8,128)}, f32[8,3...) custom-call(s32[52]{0:T(128)} %concatenate.46.scal, bf16[8,384,1024]{2,1,0:T(8,128)(2,1)} %get-tuple-element.187.normed, ...), custom_call_target="tpu_custom_call" | custom-call | tf_op jit(solution)/shard_map/attend/pallas_call | solution.py:476
  90.9 1.4 collective-permute-start.21
  92.3 1.7 collective-permute-start.19
  94.1 3.4 %collective-permute-start.18 = (bf16[4,80,128]{2,1,0:T(8,128)(2,1)S(1)}, bf16[4,80,128]{2,1,0:T(8,128)(2,1)S(1)}, u32[]{:S(2)}, u32[]{:S(2)}) collective-permute-start(bf16[4,80,128]{2,1,0:T(8,128)(2,1)S(1)} %fusion.10), channel_id=1, source_target_pairs={{0,4},{1,5},{2,6},{3,7},{8,12},{9,13},{10,14},{11,15},{16,20},{17,... | collective-permute-start | bytes 245768 | tf_op jit(solution)/shard_map/ppermute | solution.py:864
  97.5 11.6 %up.3 = (bf16[8,384,512]{2,1,0:T(8,128)(2,1)}, bf16[8,384,512]{2,1,0:T(8,128)(2,1)}) custom-call(s32[52]{0:T(128)} %concatenate.46.scal, bf16[8,384,1024]{2,1,0:T(8,128)(2,1)} %get-tuple-element.198.normed, bf16[512,256]{1,0:T(8,128)(2,1)} %maximum_select_fusion.1.refs_0_.refs_4_, bf16[512,256]{1,0:T(8,128)(2,1)} %collective-permute-done.14.refs_1_.refs_5_, ...), custom_call_target="tpu_custom_call" | custom-call | tf_op jit(solution)/shard_map/up/pallas_call | solution.py:476
  109.1 1.5 maximum_bitcast_fusion.2
  114.6 8.1 %finish.1 = (f32[8,384,128]{2,1,0:T(8,128)}, f32[8,384,128]{2,1,0:T(8,128)}) custom-call(s32[52]{0:T(128)} %concatenate.46.scal, f32[8,384,128]{2,1,0:T(8,128)} %get-tuple-element.208.num, f32[8,384,128]{2,1,0:T(8,128)} %get-tuple-element.209.den, bf16[8,384,128]{2,1,0:T(8,128)(2,1)} %get-tuple-element.210.fq, f32[8,80,128]{2,1,0:T(8,128)} %bitcast.211), custom_call_target="tpu_custom_call" | custom-call | tf_op jit(solution)/shard_map/finish/pallas_call | solution.py:476
  122.8 1.7 copy-done.1
  124.5 5.8 %down_grad1.1 = bf16[2,256,512]{2,1,0:T(8,128)(2,1)} custom-call(s32[52]{0:T(128)} %concatenate.46.scal, bf16[3072,512]{1,0:T(8,128)(2,1)} %bitcast.193, bf16[1536,1024]{1,0:T(8,128)(2,1)} %bitcast.177, bf16[1536,1024]{1,0:T(8,128)(2,1)} %bitcast.183), custom_call_target="tpu_custom_call" | custom-call | tf_op jit(solution)/shard_map/down_grad1/pallas_call | solution.py:476
  131.4 12.9 %branch.1 = (bf16[4,384,1024]{2,1,0:T(8,128)(2,1)}, bf16[4,384,1024]{2,1,0:T(8,128)(2,1)}) custom-call(s32[52]{0:T(128)} %concatenate.46.scal, f32[8,384,128]{2,1,0:T(8,128)} %get-tuple-element.225.ctx, bf16[8,384,512]{2,1,0:T(8,128)(2,1)} %get-tuple-element.218.act, bf16[256,512]{1,0:T(8,128)(2,1)} %copy-done.6, bf16[256,512]{1,0:T(8,128)(2,1)} %copy-done.8, ...), custom_call_target="tpu_custom_call" | custom-call | tf_op jit(solution)/shard_map/branch/pallas_call | solution.py:476
  144.5 23.0 %attend_back.1 = (bf16[8,384,128]{2,1,0:T(8,128)(2,1)}, f32[8,384,128]{2,1,0:T(8,128)}, f32[8,384,128]{2,1,0:T(8,128)}, bf16[8,80,128]{2,1,0:T(8,128)(2,1)}) custom-call(s32[52]{0:T(128)} %concatenate.46.scal, bf16[4,384,1024]{2,1,0:T(8,128)(2,1)} %bitcast.178, bf16[4,384,1024]{2,1,0:T(8,128)(2,1)} %copy-done.1, bf16[8,384,128]{2,1,0:T(8,128)(2,1)} %get-tuple-element.210.fq, ...), custom_call_target="tpu_custom_call" | custom-call | tf_op jit(solution)/shard_map/attend_back/pallas_call | solution.py:476
  167.5 1.5 convert_add_fusion.1
  169.7 1.6 collective-permute-start.27
  172.0 1.5 collective-permute-start.28
  173.5 10.8 %hidden_grad.1.gh = bf16[8,384,512]{2,1,0:T(8,128)(2,1)} custom-call(s32[52]{0:T(128)} %concatenate.46.scal, bf16[4,384,1024]{2,1,0:T(8,128)(2,1)} %bitcast.179, bf16[4,384,1024]{2,1,0:T(8,128)(2,1)} %copy-done.1, bf16[8,384,512]{2,1,0:T(8,128)(2,1)} %get-tuple-element.235.slope, bf16[256,512]{1,0:T(8,128)(2,1)} %copy-done.12, bf16[256,512]{1,0:T(8,128)(2,1)} %copy-done.15, ...), custom_call_target="tpu_custom_call" | custom-call | tf_op jit(solution)/shard_map/hidden_grad/pallas_call | solution.py:476
  184.2 5.8 %up_grad1.1 = bf16[2,256,512]{2,1,0:T(8,128)(2,1)} custom-call(s32[52]{0:T(128)} %concatenate.46.scal, bf16[3072,512]{1,0:T(8,128)(2,1)} %bitcast.191, bf16[3072,1024]{1,0:T(8,128)(2,1)} %bitcast.189), custom_call_target="tpu_custom_call" | custom-call | tf_op jit(solution)/shard_map/up_grad1/pallas_call | solution.py:476
  193.8 6.5 %collective-permute-start.31 = (bf16[1,192,1024]{2,1,0:T(8,128)(2,1)S(1)}, bf16[1,192,1024]{2,1,0:T(8,128)(2,1)S(1)}, u32[]{:S(2)}, u32[]{:S(2)}) collective-permute-start(bf16[1,192,1024]{2,1,0:T(8,128)(2,1)S(1)} %get-tuple-element.331), channel_id=1, source_target_pairs={{0,2},{1,3},{2,0},{3,1},{4,6},{5,7},{6,4},{7,5},{8,10},{9,11},{10,... | collective-permute-start | bytes 1179656 | tf_op jit(solution)/shard_map/ppermute | solution.py:864
  201.1 10.0 %keys_back.1 = (bf16[8,384,128]{2,1,0:T(8,128)(2,1)}, bf16[8,384,128]{2,1,0:T(8,128)(2,1)}) custom-call(s32[52]{0:T(128)} %concatenate.46.scal, f32[8,384,128]{2,1,0:T(8,128)} %get-tuple-element.243.dfk, f32[8,384,128]{2,1,0:T(8,128)} %get-tuple-element.244.dv, bf16[8,384,128]{2,1,0:T(8,128)(2,1)} %get-tuple-element.216.fk, ...), custom_call_target="tpu_custom_call" | custom-call | tf_op jit(solution)/shard_map/keys_back/pallas_call | solution.py:476
  212.0 6.1 %up_grad0.1 = (bf16[256,512]{1,0:T(8,128)(2,1)}, bf16[256,512]{1,0:T(8,128)(2,1)}) custom-call(s32[52]{0:T(128)} %concatenate.46.scal, bf16[3072,512]{1,0:T(8,128)(2,1)} %bitcast.192, bf16[3072,1024]{1,0:T(8,128)(2,1)} %bitcast.190, bf16[2,256,512]{2,1,0:T(8,128)(2,1)} %copy-done.20), custom_call_target="tpu_custom_call" | custom-call | tf_op jit(solution)/shard_map/up_grad0/pallas_call | solution.py:476
  219.4 20.9 %rows_grad.1 = (bf16[4,384,1024]{2,1,0:T(8,128)(2,1)}, bf16[4,384,1024]{2,1,0:T(8,128)(2,1)}, f32[8,1024]{1,0:T(8,128)}) custom-call(s32[52]{0:T(128)} %concatenate.46.scal, bf16[8,384,128]{2,1,0:T(8,128)(2,1)} %get-tuple-element.267.dq, bf16[8,384,128]{2,1,0:T(8,128)(2,1)} %get-tuple-element.257.dk, bf16[8,384,128]{2,1,0:T(8,128)(2,1)} %get-tuple-element.258.dv, ...), custom_call_target="tpu_custom_call" | custom-call | tf_op jit(solution)/shard_map/rows_grad/pallas_call | solution.py:476
  241.2 1.5 collective-permute-start.34
  242.7 7.5 %head_grad1.1 = bf16[2,256,512]{2,1,0:T(8,128)(2,1)} custom-call(s32[52]{0:T(128)} %concatenate.46.scal, bf16[3072,128]{1,0:T(8,128)(2,1)} %bitcast.200, bf16[3072,128]{1,0:T(8,128)(2,1)} %bitcast.202, bf16[3072,128]{1,0:T(8,128)(2,1)} %bitcast.204, f32[3072,128]{1,0:T(8,128)} %bitcast.198, bf16[3072,1024]{1,0:T(8,128)(2,1)} %bitcast.187, ...), custom_call_target="tpu_custom_call" | custom-call | tf_op jit(solution)/shard_map/head_grad1/pallas_call | solution.py:476
  251.5 1.5 convert_add_fusion
  254.3 6.0 %down_grad0.1 = (bf16[256,512]{1,0:T(8,128)(2,1)}, bf16[256,512]{1,0:T(8,128)(2,1)}) custom-call(s32[52]{0:T(128)} %concatenate.46.scal, bf16[3072,512]{1,0:T(8,128)(2,1)} %bitcast.194, bf16[1536,1024]{1,0:T(8,128)(2,1)} %bitcast.181, bf16[1536,1024]{1,0:T(8,128)(2,1)} %bitcast.185, bf16[2,256,512]{2,1,0:T(8,128)(2,1)} %copy-done.19), custom_call_target="tpu_custom_call" | custom-call | tf_op jit(solution)/shard_map/down_grad0/pallas_call | solution.py:476
  260.3 4.2 %collective-permute-done.37.refs_0_ = bf16[2,256,512]{2,1,0:T(8,128)(2,1)S(1)} collective-permute-done((bf16[2,256,512]{2,1,0:T(8,128)(2,1)}, bf16[2,256,512]{2,1,0:T(8,128)(2,1)S(1)}, u32[]{:S(2)}, u32[]{:S(2)}) %collective-permute-start.37) | collective-permute-done | bytes 524320 | tf_op jit(solution)/shard_map/ppermute | solution.py:864
  264.4 2.9 collective-permute-start.40
  268.6 7.3 %head_grad0.1 = (bf16[256,512]{1,0:T(8,128)(2,1)}, bf16[256,512]{1,0:T(8,128)(2,1)}) custom-call(s32[52]{0:T(128)} %concatenate.46.scal, bf16[3072,128]{1,0:T(8,128)(2,1)} %bitcast.201, bf16[3072,128]{1,0:T(8,128)(2,1)} %bitcast.203, bf16[3072,128]{1,0:T(8,128)(2,1)} %bitcast.205, f32[3072,128]{1,0:T(8,128)} %bitcast.199, bf16[3072,1024]{1,0:T(8,128)(2,1)} %bitcast.188, ...), custom_call_target="tpu_custom_call" | custom-call | tf_op jit(solution)/shard_map/head_grad0/pallas_call | solution.py:476
  276.8 2.0 collective-permute-done.35
  279.3 3.0 collective-permute-start.41
  284.0 1.6 collective-permute-start.42
  285.6 2.2 collective-permute-start.43
  290.2 5.8 %collective-permute-done.46 = f32[4,1024]{1,0:T(4,128)S(1)} collective-permute-done((f32[4,1024]{1,0:T(4,128)S(1)}, f32[4,1024]{1,0:T(4,128)S(1)}, u32[]{:S(2)}, u32[]{:S(2)}) %collective-permute-start.46) | collective-permute-done | bytes 16416 | tf_op jit(solution)/shard_map/ppermute | solution.py:864
  298.6 2.9 end_units.1
  302.1 2.5 end_heads.1
  305.6 4.1 %tokens_grad.1 = f32[2,192,1024]{2,1,0:T(8,128)} custom-call(s32[52]{0:T(128)} %concatenate.46.scal, bf16[2,192,1024]{2,1,0:T(8,128)(2,1)} %pad_maximum_fusion.2.mine, bf16[2,192,1024]{2,1,0:T(8,128)(2,1)} %pad_maximum_fusion.3.got, bf16[2,192,1024]{2,1,0:T(8,128)(2,1)} %tokens.1, bf16[2,192,1024]{2,1,0:T(8,128)(2,1)} %cot.1), custom_call_target="tpu_custom_call" | custom-call | tf_op jit(solution)/shard_map/tokens_grad/pallas_call | solution.py:476
  (215 shorter events, 46.3 us)
Async XLA Ops:
  0.7 4.5 %collective-permute-start = (s32[2,3]{1,0:T(2,128)}, s32[2,3]{1,0:T(2,128)S(1)}, u32[]{:S(2)}, u32[]{:S(2)}) collective-permute-start(s32[2,3]{1,0:T(2,128)} %bitcast.237), channel_id=1, source_target_pairs={{0,8},{1,9},{2,10},{3,11},{4,12},{5,13},{6,14},{7,15},{8,0},{9,1},... | collective-permute-start | bytes 80 | tf_op jit(solution)/shard_map/ppermute | solution.py:864
  4.5 2.0 collective-permute-start.1
  4.5 2.0 collective-permute-start.2
  7.6 17.2 %collective-permute-start.7 = (bf16[256,512]{1,0:T(8,128)(2,1)S(1)}, bf16[256,512]{1,0:T(8,128)(2,1)S(1)}, u32[]{:S(2)}, u32[]{:S(2)}) collective-permute-start(bf16[256,512]{1,0:T(8,128)(2,1)S(1)} %maximum_select_fusion.refs_0_), channel_id=1, source_target_pairs={{0,16},{1,17},{2,18},{3,19},{4,20},{5,21},{6,22},{7,23},{8,24},{9,... | collective-permute-start | bytes 786440 | tf_op jit(solution)/shard_map/ppermute | solution.py:864
  10.6 14.7 %collective-permute-start.6 = (bf16[256,512]{1,0:T(8,128)(2,1)S(1)}, bf16[256,512]{1,0:T(8,128)(2,1)S(1)}, u32[]{:S(2)}, u32[]{:S(2)}) collective-permute-start(bf16[256,512]{1,0:T(8,128)(2,1)S(1)} %maximum_select_fusion.refs_0_), channel_id=1, source_target_pairs={{0,4},{1,5},{2,6},{3,7},{4,0},{5,1},{6,2},{7,3},{8,12},{9,13},{10,... | collective-permute-start | bytes 786440 | tf_op jit(solution)/shard_map/ppermute | solution.py:864
  13.2 23.7 %collective-permute-start.5 = (bf16[2,192,1024]{2,1,0:T(8,128)(2,1)}, bf16[2,192,1024]{2,1,0:T(8,128)(2,1)S(1)}, u32[]{:S(2)}, u32[]{:S(2)}) collective-permute-start(bf16[2,192,1024]{2,1,0:T(8,128)(2,1)} %tokens.1), channel_id=1, source_target_pairs={{0,2},{1,3},{2,0},{3,1},{4,6},{5,7},{6,4},{7,5},{8,10},{9,11},{10,... | collective-permute-start | bytes 2359304 | tf_op jit(solution)/shard_map/ppermute | solution.py:864
  14.8 22.1 %collective-permute-start.4 = (bf16[2,192,1024]{2,1,0:T(8,128)(2,1)}, bf16[2,192,1024]{2,1,0:T(8,128)(2,1)S(1)}, u32[]{:S(2)}, u32[]{:S(2)}) collective-permute-start(bf16[2,192,1024]{2,1,0:T(8,128)(2,1)} %tokens.1), channel_id=1, source_target_pairs={{0,1},{1,0},{2,3},{3,2},{4,5},{5,4},{6,7},{7,6},{8,9},{9,8},{10,11... | collective-permute-start | bytes 2359304 | tf_op jit(solution)/shard_map/ppermute | solution.py:864
  17.1 7.7 %collective-permute-start.8 = (bf16[512,256]{1,0:T(8,128)(2,1)}, bf16[512,256]{1,0:T(8,128)(2,1)}, u32[]{:S(2)}, u32[]{:S(2)}) collective-permute-start(bf16[512,256]{1,0:T(8,128)(2,1)} %maximum_select_fusion.1.refs_0_.refs_4_), channel_id=1, source_target_pairs={{0,16},{1,17},{2,18},{3,19},{4,20},{5,21},{6,22},{7,23},{8,24},{9,... | collective-permute-start | bytes 786440 | tf_op jit(solution)/shard_map/ppermute | solution.py:864
  37.0 9.8 %collective-permute-start.9 = (bf16[1,192,1024]{2,1,0:T(8,128)(2,1)S(1)}, bf16[1,192,1024]{2,1,0:T(8,128)(2,1)S(1)}, u32[]{:S(2)}, u32[]{:S(2)}) collective-permute-start(bf16[1,192,1024]{2,1,0:T(8,128)(2,1)S(1)} %slice.177), channel_id=1, source_target_pairs={{0,1},{1,0},{2,3},{3,2},{4,5},{5,4},{6,7},{7,6},{8,9},{9,8},{10,11... | collective-permute-start | bytes 1179656 | tf_op jit(solution)/shard_map/ppermute | solution.py:864
  38.5 9.4 %collective-permute-start.10 = (bf16[1,192,1024]{2,1,0:T(8,128)(2,1)S(1)}, bf16[1,192,1024]{2,1,0:T(8,128)(2,1)S(1)}, u32[]{:S(2)}, u32[]{:S(2)}) collective-permute-start(bf16[1,192,1024]{2,1,0:T(8,128)(2,1)S(1)} %slice.178), channel_id=1, source_target_pairs={{0,2},{1,3},{2,0},{3,1},{4,6},{5,7},{6,4},{7,5},{8,10},{9,11},{10,... | collective-permute-start | bytes 1179656 | tf_op jit(solution)/shard_map/ppermute | solution.py:864
  39.8 6.6 %collective-permute-start.11 = (bf16[256,512]{1,0:T(8,128)(2,1)S(1)}, bf16[256,512]{1,0:T(8,128)(2,1)S(1)}, u32[]{:S(2)}, u32[]{:S(2)}) collective-permute-start(bf16[256,512]{1,0:T(8,128)(2,1)S(1)} %collective-permute-done.6.refs_1_), channel_id=1, source_target_pairs={{0,16},{1,17},{2,18},{3,19},{4,20},{5,21},{6,22},{7,23},{8,24},{9,... | collective-permute-start | bytes 786440 | tf_op jit(solution)/shard_map/ppermute | solution.py:864
  48.8 8.8 %collective-permute-start.12 = (bf16[4,384,1024]{2,1,0:T(8,128)(2,1)S(1)}, bf16[4,384,1024]{2,1,0:T(8,128)(2,1)S(1)}, u32[]{:S(2)}, u32[]{:S(2)}) collective-permute-start(bf16[4,384,1024]{2,1,0:T(8,128)(2,1)S(1)} %bitcast.195), channel_id=1, source_target_pairs={{0,8},{1,9},{2,10},{3,11},{4,12},{5,13},{6,14},{7,15},{8,0},{9,1},... | collective-permute-start | bytes 9437192 | tf_op jit(solution)/shard_map/ppermute | solution.py:864
  48.9 8.7 %collective-permute-start.13 = (bf16[256,512]{1,0:T(8,128)(2,1)S(1)}, bf16[256,512]{1,0:T(8,128)(2,1)S(1)}, u32[]{:S(2)}, u32[]{:S(2)}) collective-permute-start(bf16[256,512]{1,0:T(8,128)(2,1)S(1)} %maximum_select_fusion.2.refs_4_.refs_0_), channel_id=1, source_target_pairs={{0,16},{1,17},{2,18},{3,19},{4,20},{5,21},{6,22},{7,23},{8,24},{9,... | collective-permute-start | bytes 786440 | tf_op jit(solution)/shard_map/ppermute | solution.py:864
  57.6 30.6 %collective-permute-start.17 = (bf16[2,192,1024]{2,1,0:T(8,128)(2,1)}, bf16[2,192,1024]{2,1,0:T(8,128)(2,1)}, u32[]{:S(2)}, u32[]{:S(2)}) collective-permute-start(bf16[2,192,1024]{2,1,0:T(8,128)(2,1)} %cot.1), channel_id=1, source_target_pairs={{0,2},{1,3},{2,0},{3,1},{4,6},{5,7},{6,4},{7,5},{8,10},{9,11},{10,... | collective-permute-start | bytes 2359304 | tf_op jit(solution)/shard_map/ppermute | solution.py:864
  59.2 29.1 %collective-permute-start.16 = (bf16[2,192,1024]{2,1,0:T(8,128)(2,1)}, bf16[2,192,1024]{2,1,0:T(8,128)(2,1)}, u32[]{:S(2)}, u32[]{:S(2)}) collective-permute-start(bf16[2,192,1024]{2,1,0:T(8,128)(2,1)} %cot.1), channel_id=1, source_target_pairs={{0,1},{1,0},{2,3},{3,2},{4,5},{5,4},{6,7},{7,6},{8,9},{9,8},{10,11... | collective-permute-start | bytes 2359304 | tf_op jit(solution)/shard_map/ppermute | solution.py:864
  59.7 27.3 %collective-permute-start.14 = (bf16[512,256]{1,0:T(8,128)(2,1)}, bf16[512,256]{1,0:T(8,128)(2,1)}, u32[]{:S(2)}, u32[]{:S(2)}) collective-permute-start(bf16[512,256]{1,0:T(8,128)(2,1)} %maximum_select_fusion.1.refs_0_.refs_4_), channel_id=1, source_target_pairs={{0,4},{1,5},{2,6},{3,7},{4,0},{5,1},{6,2},{7,3},{8,12},{9,13},{10,... | collective-permute-start | bytes 786440 | tf_op jit(solution)/shard_map/ppermute | solution.py:864
  61.3 26.0 %collective-permute-start.15 = (bf16[512,256]{1,0:T(8,128)(2,1)}, bf16[512,256]{1,0:T(8,128)(2,1)}, u32[]{:S(2)}, u32[]{:S(2)}) collective-permute-start(bf16[512,256]{1,0:T(8,128)(2,1)} %collective-permute-done.8.refs_2_.refs_6_), channel_id=1, source_target_pairs={{0,4},{1,5},{2,6},{3,7},{4,0},{5,1},{6,2},{7,3},{8,12},{9,13},{10,... | collective-permute-start | bytes 786440 | tf_op jit(solution)/shard_map/ppermute | solution.py:864
  90.3 20.4 %collective-permute-start.20 = (bf16[1,192,1024]{2,1,0:T(8,128)(2,1)S(1)}, bf16[1,192,1024]{2,1,0:T(8,128)(2,1)S(1)}, u32[]{:S(2)}, u32[]{:S(2)}) collective-permute-start(bf16[1,192,1024]{2,1,0:T(8,128)(2,1)S(1)} %slice.181), channel_id=1, source_target_pairs={{0,1},{1,0},{2,3},{3,2},{4,5},{5,4},{6,7},{7,6},{8,9},{9,8},{10,11... | collective-permute-start | bytes 1179656 | tf_op jit(solution)/shard_map/ppermute | solution.py:864
  90.9 19.8 %collective-permute-start.21 = (bf16[1,192,1024]{2,1,0:T(8,128)(2,1)S(1)}, bf16[1,192,1024]{2,1,0:T(8,128)(2,1)S(1)}, u32[]{:S(2)}, u32[]{:S(2)}) collective-permute-start(bf16[1,192,1024]{2,1,0:T(8,128)(2,1)S(1)} %slice.182), channel_id=1, source_target_pairs={{0,2},{1,3},{2,0},{3,1},{4,6},{5,7},{6,4},{7,5},{8,10},{9,11},{10,... | collective-permute-start | bytes 1179656 | tf_op jit(solution)/shard_map/ppermute | solution.py:864
  92.3 18.3 %collective-permute-start.19 = (bf16[256,512]{1,0:T(8,128)(2,1)S(1)}, bf16[256,512]{1,0:T(8,128)(2,1)S(1)}, u32[]{:S(2)}, u32[]{:S(2)}) collective-permute-start(bf16[256,512]{1,0:T(8,128)(2,1)S(1)} %copy-done.13), channel_id=1, source_target_pairs={{0,4},{1,5},{2,6},{3,7},{4,0},{5,1},{6,2},{7,3},{8,12},{9,13},{10,... | collective-permute-start | bytes 786440 | tf_op jit(solution)/shard_map/ppermute | solution.py:864
  94.1 16.5 %collective-permute-start.18 = (bf16[4,80,128]{2,1,0:T(8,128)(2,1)S(1)}, bf16[4,80,128]{2,1,0:T(8,128)(2,1)S(1)}, u32[]{:S(2)}, u32[]{:S(2)}) collective-permute-start(bf16[4,80,128]{2,1,0:T(8,128)(2,1)S(1)} %fusion.10), channel_id=1, source_target_pairs={{0,4},{1,5},{2,6},{3,7},{8,12},{9,13},{10,14},{11,15},{16,20},{17,... | collective-permute-start | bytes 245768 | tf_op jit(solution)/shard_map/ppermute | solution.py:864
  112.7 10.1 %collective-permute-start.22 = (bf16[4,384,1024]{2,1,0:T(8,128)(2,1)S(1)}, bf16[4,384,1024]{2,1,0:T(8,128)(2,1)S(1)}, u32[]{:S(2)}, u32[]{:S(2)}) collective-permute-start(bf16[4,384,1024]{2,1,0:T(8,128)(2,1)S(1)} %bitcast.176), channel_id=1, source_target_pairs={{0,8},{1,9},{2,10},{3,11},{4,12},{5,13},{6,14},{7,15},{8,0},{9,1},... | collective-permute-start | bytes 9437192 | tf_op jit(solution)/shard_map/ppermute | solution.py:864
  112.8 10.0 %collective-permute-start.23 = (bf16[256,512]{1,0:T(8,128)(2,1)S(1)}, bf16[256,512]{1,0:T(8,128)(2,1)S(1)}, u32[]{:S(2)}, u32[]{:S(2)}) collective-permute-start(bf16[256,512]{1,0:T(8,128)(2,1)S(1)} %collective-permute-done.19.refs_5_.refs_1_), channel_id=1, source_target_pairs={{0,16},{1,17},{2,18},{3,19},{4,20},{5,21},{6,22},{7,23},{8,24},{9,... | collective-permute-start | bytes 786440 | tf_op jit(solution)/shard_map/ppermute | solution.py:864
  130.3 14.2 %collective-permute-start.24 = (bf16[2,256,512]{2,1,0:T(8,128)(2,1)}, bf16[2,256,512]{2,1,0:T(8,128)(2,1)S(1)}, u32[]{:S(2)}, u32[]{:S(2)}) collective-permute-start(bf16[2,256,512]{2,1,0:T(8,128)(2,1)} %down_grad1.1), channel_id=1, source_target_pairs={{0,16},{1,17},{2,18},{3,19},{4,20},{5,21},{6,22},{7,23},{8,24},{9,... | collective-permute-start | bytes 1572872 | tf_op jit(solution)/shard_map/ppermute | solution.py:864
  144.5 23.0 %collective-permute-start.25 = (bf16[4,384,1024]{2,1,0:T(8,128)(2,1)}, bf16[4,384,1024]{2,1,0:T(8,128)(2,1)S(1)}, u32[]{:S(2)}, u32[]{:S(2)}) collective-permute-start(bf16[4,384,1024]{2,1,0:T(8,128)(2,1)} %get-tuple-element.229), channel_id=1, source_target_pairs={{0,8},{1,9},{2,10},{3,11},{4,12},{5,13},{6,14},{7,15},{8,0},{9,1},... | collective-permute-start | bytes 9437192 | tf_op jit(solution)/shard_map/ppermute | solution.py:864
  169.7 21.5 %collective-permute-start.27 = (bf16[1,2,192,1024]{3,2,1,0:T(8,128)(2,1)S(1)}, bf16[1,2,192,1024]{3,2,1,0:T(8,128)(2,1)S(1)}, u32[]{:S(2)}, u32[]{:S(2)}) collective-permute-start(bf16[1,2,192,1024]{3,2,1,0:T(8,128)(2,1)S(1)} %get-tuple-element.322), channel_id=1, source_target_pairs={{0,1},{1,0},{2,3},{3,2},{4,5},{5,4},{6,7},{7,6},{8,9},{9,8},{10,11... | collective-permute-start | bytes 2359304 | tf_op jit(solution)/shard_map/ppermute | solution.py:864
  171.3 21.2 %collective-permute-start.26 = (bf16[1,2,192,1024]{3,2,1,0:T(8,128)(2,1)S(1)}, bf16[1,2,192,1024]{3,2,1,0:T(8,128)(2,1)S(1)}, u32[]{:S(2)}, u32[]{:S(2)}) collective-permute-start(bf16[1,2,192,1024]{3,2,1,0:T(8,128)(2,1)S(1)} %get-tuple-element.324), channel_id=1, source_target_pairs={{0,2},{1,3},{2,0},{3,1},{4,6},{5,7},{6,4},{7,5},{8,10},{9,11},{10,... | collective-permute-start | bytes 2359304 | tf_op jit(solution)/shard_map/ppermute | solution.py:864
  172.0 12.3 %collective-permute-start.28 = (bf16[4,80,128]{2,1,0:T(8,128)(2,1)S(1)}, bf16[4,80,128]{2,1,0:T(8,128)(2,1)S(1)}, u32[]{:S(2)}, u32[]{:S(2)}) collective-permute-start(bf16[4,80,128]{2,1,0:T(8,128)(2,1)S(1)} %fusion.8), channel_id=1, source_target_pairs={{4,0},{5,1},{6,2},{7,3},{12,8},{13,9},{14,10},{15,11},{20,16},{21,... | collective-permute-start | bytes 245768 | tf_op jit(solution)/shard_map/ppermute | solution.py:864
  190.0 21.1 %collective-permute-start.29 = (bf16[2,256,512]{2,1,0:T(8,128)(2,1)}, bf16[2,256,512]{2,1,0:T(8,128)(2,1)S(1)}, u32[]{:S(2)}, u32[]{:S(2)}) collective-permute-start(bf16[2,256,512]{2,1,0:T(8,128)(2,1)} %up_grad1.1), channel_id=1, source_target_pairs={{0,16},{1,17},{2,18},{3,19},{4,20},{5,21},{6,22},{7,23},{8,24},{9,... | collective-permute-start | bytes 1572872 | tf_op jit(solution)/shard_map/ppermute | solution.py:864
  192.9 18.3 %collective-permute-start.30 = (bf16[1,192,1024]{2,1,0:T(8,128)(2,1)S(1)}, bf16[1,192,1024]{2,1,0:T(8,128)(2,1)S(1)}, u32[]{:S(2)}, u32[]{:S(2)}) collective-permute-start(bf16[1,192,1024]{2,1,0:T(8,128)(2,1)S(1)} %get-tuple-element.333), channel_id=1, source_target_pairs={{0,1},{1,0},{2,3},{3,2},{4,5},{5,4},{6,7},{7,6},{8,9},{9,8},{10,11... | collective-permute-start | bytes 1179656 | tf_op jit(solution)/shard_map/ppermute | solution.py:864
  193.8 17.4 %collective-permute-start.31 = (bf16[1,192,1024]{2,1,0:T(8,128)(2,1)S(1)}, bf16[1,192,1024]{2,1,0:T(8,128)(2,1)S(1)}, u32[]{:S(2)}, u32[]{:S(2)}) collective-permute-start(bf16[1,192,1024]{2,1,0:T(8,128)(2,1)S(1)} %get-tuple-element.331), channel_id=1, source_target_pairs={{0,2},{1,3},{2,0},{3,1},{4,6},{5,7},{6,4},{7,5},{8,10},{9,11},{10,... | collective-permute-start | bytes 1179656 | tf_op jit(solution)/shard_map/ppermute | solution.py:864
  218.1 22.2 %collective-permute-start.32 = (bf16[256,512]{1,0:T(8,128)(2,1)}, bf16[256,512]{1,0:T(8,128)(2,1)S(1)}, u32[]{:S(2)}, u32[]{:S(2)}) collective-permute-start(bf16[256,512]{1,0:T(8,128)(2,1)} %get-tuple-element.262), channel_id=1, source_target_pairs={{0,4},{1,5},{2,6},{3,7},{4,0},{5,1},{6,2},{7,3},{8,12},{9,13},{10,... | collective-permute-start | bytes 786440 | tf_op jit(solution)/shard_map/ppermute | solution.py:864
  240.3 11.1 %collective-permute-start.33 = (bf16[4,384,1024]{2,1,0:T(8,128)(2,1)}, bf16[4,384,1024]{2,1,0:T(8,128)(2,1)S(1)}, u32[]{:S(2)}, u32[]{:S(2)}) collective-permute-start(bf16[4,384,1024]{2,1,0:T(8,128)(2,1)} %get-tuple-element.265), channel_id=1, source_target_pairs={{0,8},{1,9},{2,10},{3,11},{4,12},{5,13},{6,14},{7,15},{8,0},{9,1},... | collective-permute-start | bytes 9437192 | tf_op jit(solution)/shard_map/ppermute | solution.py:864
  241.2 10.3 %collective-permute-start.34 = (f32[4,1024]{1,0:T(4,128)S(1)}, f32[4,1024]{1,0:T(4,128)S(1)}, u32[]{:S(2)}, u32[]{:S(2)}) collective-permute-start(f32[4,1024]{1,0:T(4,128)S(1)} %slice.197), channel_id=1, source_target_pairs={{0,1},{1,0},{2,3},{3,2},{4,5},{5,4},{6,7},{7,6},{8,9},{9,8},{10,11... | collective-permute-start | bytes 49160 | tf_op jit(solution)/shard_map/ppermute | solution.py:864
  250.2 14.3 %collective-permute-start.37 = (bf16[2,256,512]{2,1,0:T(8,128)(2,1)}, bf16[2,256,512]{2,1,0:T(8,128)(2,1)S(1)}, u32[]{:S(2)}, u32[]{:S(2)}) collective-permute-start(bf16[2,256,512]{2,1,0:T(8,128)(2,1)} %head_grad1.1), channel_id=1, source_target_pairs={{0,16},{1,17},{2,18},{3,19},{4,20},{5,21},{6,22},{7,23},{8,24},{9,... | collective-permute-start | bytes 1572872 | tf_op jit(solution)/shard_map/ppermute | solution.py:864
  253.6 23.2 %collective-permute-start.36 = (bf16[1,2,192,1024]{3,2,1,0:T(8,128)(2,1)S(1)}, bf16[1,2,192,1024]{3,2,1,0:T(8,128)(2,1)S(1)}, u32[]{:S(2)}, u32[]{:S(2)}) collective-permute-start(bf16[1,2,192,1024]{3,2,1,0:T(8,128)(2,1)S(1)} %get-tuple-element.318), channel_id=1, source_target_pairs={{0,1},{1,0},{2,3},{3,2},{4,5},{5,4},{6,7},{7,6},{8,9},{9,8},{10,11... | collective-permute-start | bytes 2359304 | tf_op jit(solution)/shard_map/ppermute | solution.py:864
  254.1 24.7 %collective-permute-start.35 = (bf16[1,2,192,1024]{3,2,1,0:T(8,128)(2,1)S(1)}, bf16[1,2,192,1024]{3,2,1,0:T(8,128)(2,1)S(1)}, u32[]{:S(2)}, u32[]{:S(2)}) collective-permute-start(bf16[1,2,192,1024]{3,2,1,0:T(8,128)(2,1)S(1)} %get-tuple-element.320), channel_id=1, source_target_pairs={{0,2},{1,3},{2,0},{3,1},{4,6},{5,7},{6,4},{7,5},{8,10},{9,11},{10,... | collective-permute-start | bytes 2359304 | tf_op jit(solution)/shard_map/ppermute | solution.py:864
  254.3 10.2 %collective-permute-start.38 = (f32[4,1024]{1,0:T(4,128)S(1)}, f32[4,1024]{1,0:T(4,128)S(1)}, u32[]{:S(2)}, u32[]{:S(2)}) collective-permute-start(f32[4,1024]{1,0:T(4,128)S(1)} %slice_add_fusion), channel_id=1, source_target_pairs={{0,8},{1,9},{2,10},{3,11},{4,12},{5,13},{6,14},{7,15},{8,0},{9,1},... | collective-permute-start | bytes 49160 | tf_op jit(solution)/shard_map/ppermute | solution.py:864
  264.4 12.4 %collective-permute-start.40 = (bf16[256,512]{1,0:T(8,128)(2,1)}, bf16[256,512]{1,0:T(8,128)(2,1)S(1)}, u32[]{:S(2)}, u32[]{:S(2)}) collective-permute-start(bf16[256,512]{1,0:T(8,128)(2,1)} %get-tuple-element.276), channel_id=1, source_target_pairs={{0,4},{1,5},{2,6},{3,7},{4,0},{5,1},{6,2},{7,3},{8,12},{9,13},{10,... | collective-permute-start | bytes 786440 | tf_op jit(solution)/shard_map/ppermute | solution.py:864
  267.4 8.6 %collective-permute-start.39 = (f32[4,1024]{1,0:T(4,128)S(1)}, f32[4,1024]{1,0:T(4,128)S(1)}, u32[]{:S(2)}, u32[]{:S(2)}) collective-permute-start(f32[4,1024]{1,0:T(4,128)S(1)} %add.162), channel_id=1, source_target_pairs={{0,16},{1,17},{2,18},{3,19},{4,20},{5,21},{6,22},{7,23},{8,24},{9,... | collective-permute-start | bytes 49160 | tf_op jit(solution)/shard_map/ppermute | solution.py:864
  279.3 4.7 %collective-permute-start.41 = (f32[4,1024]{1,0:T(4,128)S(1)}, f32[4,1024]{1,0:T(4,128)S(1)}, u32[]{:S(2)}, u32[]{:S(2)}) collective-permute-start(f32[4,1024]{1,0:T(4,128)S(1)} %add.165), channel_id=1, source_target_pairs={{0,2},{1,3},{2,0},{3,1},{4,6},{5,7},{6,4},{7,5},{8,10},{9,11},{10,... | collective-permute-start | bytes 49160 | tf_op jit(solution)/shard_map/ppermute | solution.py:864
  282.2 13.7 %collective-permute-start.47 = (bf16[256,512]{1,0:T(8,128)(2,1)S(1)}, bf16[256,512]{1,0:T(8,128)(2,1)S(1)}, u32[]{:S(2)}, u32[]{:S(2)}) collective-permute-start(bf16[256,512]{1,0:T(8,128)(2,1)S(1)} %copy-done.33), channel_id=1, source_target_pairs={{0,4},{1,5},{2,6},{3,7},{4,0},{5,1},{6,2},{7,3},{8,12},{9,13},{10,... | collective-permute-start | bytes 786440 | tf_op jit(solution)/shard_map/ppermute | solution.py:864
  284.0 20.6 %collective-permute-start.42 = (bf16[1,192,1024]{2,1,0:T(8,128)(2,1)S(1)}, bf16[1,192,1024]{2,1,0:T(8,128)(2,1)S(1)}, u32[]{:S(2)}, u32[]{:S(2)}) collective-permute-start(bf16[1,192,1024]{2,1,0:T(8,128)(2,1)S(1)} %get-tuple-element.287), channel_id=1, source_target_pairs={{0,1},{1,0},{2,3},{3,2},{4,5},{5,4},{6,7},{7,6},{8,9},{9,8},{10,11... | collective-permute-start | bytes 1179656 | tf_op jit(solution)/shard_map/ppermute | solution.py:864
  285.6 19.0 %collective-permute-start.43 = (bf16[1,192,1024]{2,1,0:T(8,128)(2,1)S(1)}, bf16[1,192,1024]{2,1,0:T(8,128)(2,1)S(1)}, u32[]{:S(2)}, u32[]{:S(2)}) collective-permute-start(bf16[1,192,1024]{2,1,0:T(8,128)(2,1)S(1)} %get-tuple-element.288), channel_id=1, source_target_pairs={{0,2},{1,3},{2,0},{3,1},{4,6},{5,7},{6,4},{7,5},{8,10},{9,11},{10,... | collective-permute-start | bytes 1179656 | tf_op jit(solution)/shard_map/ppermute | solution.py:864
  288.5 7.5 %collective-permute-start.46 = (f32[4,1024]{1,0:T(4,128)S(1)}, f32[4,1024]{1,0:T(4,128)S(1)}, u32[]{:S(2)}, u32[]{:S(2)}) collective-permute-start(f32[4,1024]{1,0:T(4,128)S(1)} %add.168), channel_id=1, source_target_pairs={{0,4},{1,5},{2,6},{3,7},{4,0},{5,1},{6,2},{7,3},{8,12},{9,13},{10,... | collective-permute-start | bytes 49160 | tf_op jit(solution)/shard_map/ppermute | solution.py:864
  290.2 7.7 %collective-permute-start.44 = (bf16[256,256]{1,0:T(8,128)(2,1)S(1)}, bf16[256,256]{1,0:T(8,128)(2,1)S(1)}, u32[]{:S(2)}, u32[]{:S(2)}) collective-permute-start(bf16[256,256]{1,0:T(8,128)(2,1)S(1)} %get-tuple-element.342), channel_id=1, source_target_pairs={{0,8},{1,9},{2,10},{3,11},{4,12},{5,13},{6,14},{7,15},{8,0},{9,1},... | collective-permute-start | bytes 393224 | tf_op jit(solution)/shard_map/ppermute | solution.py:864
  296.0 1.9 collective-permute-start.45
  296.7 4.7 %collective-permute-start.48 = (bf16[256,256]{1,0:T(8,128)(2,1)S(1)}, bf16[256,256]{1,0:T(8,128)(2,1)S(1)}, u32[]{:S(2)}, u32[]{:S(2)}) collective-permute-start(bf16[256,256]{1,0:T(8,128)(2,1)S(1)} %get-tuple-element.338), channel_id=1, source_target_pairs={{0,8},{1,9},{2,10},{3,11},{4,12},{5,13},{6,14},{7,15},{8,0},{9,1},... | collective-permute-start | bytes 393224 | tf_op jit(solution)/shard_map/ppermute | solution.py:864
  (35 other events, 299.8 us)

commit v3 on v2

--- a/solution.py
+++ b/solution.py
@@ -17,6 +17,7 @@
 BF16 = jnp.bfloat16
 F32 = jnp.float32
 VMEM_LIMIT = 56 * 1024 * 1024
+PER = 2
 NN = (((1,), (0,)), ((), ()))
 NT = (((1,), (1,)), ((), ()))
 TN = (((0,), (0,)), ((), ()))
@@ -451,20 +452,26 @@
     return (array, tuple(array.shape), lambda *_: zeros)
 
 
-def by_seq(array):
+class Seq(tuple):
+    pass
+
+
+def by_seq(array, per=1):
     rest = (0,) * (array.ndim - 1)
-    return (array, (1,) + tuple(array.shape[1:]), lambda i, s: (i,) + rest)
-
-
-def own_seq(array):
-    rest, most = (0,) * (array.ndim - 1), array.shape[0] - 1
-    return (array, (1,) + tuple(array.shape[1:]), lambda i, s: (jnp.minimum(i, most),) + rest)
-
-
-def away_seq(array):
-    rest, count = (0,) * (array.ndim - 1), array.shape[0]
-    return (
-        array, (1,) + tuple(array.shape[1:]), lambda i, s: (jnp.maximum(i - count, 0),) + rest
+    return Seq((array, (per,) + tuple(array.shape[1:]), lambda i, s: (i,) + rest))
+
+
+def own_seq(array, per=1):
+    rest, most = (0,) * (array.ndim - 1), array.shape[0] // per - 1
+    return Seq(
+        (array, (per,) + tuple(array.shape[1:]), lambda i, s: (jnp.minimum(i, most),) + rest)
+    )
+
+
+def away_seq(array, per=1):
+    rest, count = (0,) * (array.ndim - 1), array.shape[0] // per
+    return Seq(
+        (array, (per,) + tuple(array.shape[1:]), lambda i, s: (jnp.maximum(i - count, 0),) + rest)
     )
 
 
@@ -494,12 +501,24 @@
     )(scal, *[array for array, _, _ in ins])
 
 
+def seq_call(name, body, scal, count, ins, outs, scratch=(), per=PER):
+    marks = [isinstance(part, Seq) for part in list(ins) + list(outs)]
+
+    def step(scal, *refs):
+        for k in range(per):
+            views = [ref.at[pl.ds(k, 1)] if mark else ref for ref, mark in zip(refs, marks)]
+            body(k, pl.program_id(0) * per + k, scal, *views, *refs[len(marks) :])
+
+    return call(name, step, scal, (count // per,), ins, outs, scratch)
+
+
 class Shape:
     def __init__(self, pairs, chunks, dim, half_units, half_ff, chunk, docs):
         self.pairs, self.chunks, self.dim = pairs, chunks, dim
         self.hu, self.hf, self.chunk, self.docs = half_units, half_ff, chunk, docs
         self.dp = dim // pairs
         self.width, self.ff = chunks * half_units, chunks * half_ff
+        self.half = 0
 
     def cols(self, scal, slot):
         start = ((scal[0] + slot) % self.pairs) * self.dp
@@ -540,15 +559,17 @@
     two[0] = (n * g2[...] + b2[...]).astype(BF16)
 
 
-def attend_body(sh, scal, normed, cos, sin, ph, pw, wts, *refs):
+def attend_body(sh, k, seq, scal, normed, cos, sin, ph, pw, wts, *refs):
     blocks = refs[: sh.pairs * sh.chunks]
     fq_out, fk_out, v_out, num_out, den_out, st_out, wt = refs[sh.pairs * sh.chunks :]
-    width, seq = sh.width, pl.program_id(0)
-
-    @pl.when(seq == 0)
-    def _():
-        for kind in range(3):
-            fill_rows(sh, wt, blocks, kind * sh.hu, sh.hu, kind * width)
+    width = sh.width
+
+    if k == 0:
+
+        @pl.when(seq == 0)
+        def _():
+            for kind in range(3):
+                fill_rows(sh, wt, blocks, kind * sh.hu, sh.hu, kind * width)
 
     qkv = mm(normed[0, :, sh.cols(scal, 0)], wt[0], NT)
     for slot in range(1, sh.pairs):
@@ -596,15 +617,17 @@
     return state[:HEAD_DIM], state[HEAD_DIM : HEAD_DIM + 1]
 
 
-def up_body(sh, scal, normed, *refs):
+def up_body(sh, k, seq, scal, normed, *refs):
     blocks = refs[: sh.pairs * sh.chunks]
     act_out, slope_out, wu = refs[sh.pairs * sh.chunks :]
 
-    @pl.when(pl.program_id(0) == 0)
-    def _():
-        for slot in range(sh.pairs):
-            for j in range(sh.chunks):
-                wu[slot, :, j * sh.hf : (j + 1) * sh.hf] = blocks[slot * sh.chunks + j][...]
+    if k == 0:
+
+        @pl.when(seq == 0)
+        def _():
+            for slot in range(sh.pairs):
+                for j in range(sh.chunks):
+                    wu[slot, :, j * sh.hf : (j + 1) * sh.hf] = blocks[slot * sh.chunks + j][...]
 
     hidden = mm(normed[0, :, sh.cols(scal, 0)], wu[0])
     for slot in range(1, sh.pairs):
@@ -615,74 +638,76 @@
     slope_out[0] = (cdf + hidden * bell).astype(BF16)
 
 
-def finish_body(sh, scal, num, den, fq, carry, ctx_out, rden_out):
+def finish_body(sh, k, seq, scal, num, den, fq, carry, ctx_out, rden_out):
     fqb = fq[0]
     sums, totals = load_state(sh, scal, carry)
     more_num = mm(fqb, block_diag(sums).astype(BF16))
     more_den = head_sums(fqb.astype(F32) * totals)
-    came = Rows(scal, pl.program_id(0), sh.chunk, sh.docs).came
+    came = Rows(scal, seq, sh.chunk, sh.docs).came
     inverse = 1.0 / (den[0] + jnp.where(came, more_den, 0.0))
     ctx_out[0] = (num[0] + jnp.where(came, more_num, 0.0)) * inverse
     rden_out[0] = inverse
 
 
-def branch_body(sh, scal, ctx, act, *refs):
+def store_half(sh, seq, cols, part, own_out, away_out):
+    own_out[0, :, cols] = jnp.where(seq < sh.half, part, own_out[0, :, cols])
+    away_out[0, :, cols] = part
+
+
+def branch_body(sh, k, seq, scal, ctx, act, *refs):
     count = sh.pairs * sh.chunks
     blocks_a, blocks_d = refs[:count], refs[count : 2 * count]
     own_out, away_out, wo, wd = refs[2 * count :]
-    seq = pl.program_id(0)
-
-    @pl.when(seq == 0)
-    def _():
-        fill_rows(sh, wo, blocks_a, 3 * sh.hu, sh.hu, 0)
-        fill_rows(sh, wd, blocks_d, 0, sh.hf, 0)
+
+    if k == 0:
+
+        @pl.when(seq == 0)
+        def _():
+            fill_rows(sh, wo, blocks_a, 3 * sh.hu, sh.hu, 0)
+            fill_rows(sh, wd, blocks_d, 0, sh.hf, 0)
 
     ctxb = ctx[0].astype(BF16)
-    half = pl.num_programs(0) // 2
     for slot in range(sh.pairs):
         part = (mm(act[0], wd[slot]) + mm(ctxb, wo[slot])).astype(BF16)
-
-        @pl.when(seq < half)
-        def _():
-            own_out[0, :, sh.cols(scal, slot)] = part
-
-        @pl.when(seq >= half)
-        def _():
-            away_out[0, :, sh.cols(scal, slot)] = part
-
-
-def pick(own, away, scal, sh, slot):
-    first = pl.program_id(0) < pl.num_programs(0) // 2
+        store_half(sh, seq, sh.cols(scal, slot), part, own_out, away_out)
+
+
+def pick(own, away, seq, scal, sh, slot):
+    first = seq < sh.half
     cols = sh.cols(scal, slot)
     return jnp.where(first, own[0, :, cols], away[0, :, cols])
 
 
-def hidden_body(sh, scal, own, away, slope, *refs):
+def hidden_body(sh, k, seq, scal, own, away, slope, *refs):
     blocks = refs[: sh.pairs * sh.chunks]
     out, wd = refs[sh.pairs * sh.chunks :]
 
-    @pl.when(pl.program_id(0) == 0)
-    def _():
-        fill_rows(sh, wd, blocks, 0, sh.hf, 0)
-
-    grad = mm(pick(own, away, scal, sh, 0), wd[0], NT)
+    if k == 0:
+
+        @pl.when(seq == 0)
+        def _():
+            fill_rows(sh, wd, blocks, 0, sh.hf, 0)
+
+    grad = mm(pick(own, away, seq, scal, sh, 0), wd[0], NT)
     for slot in range(1, sh.pairs):
-        grad = grad + mm(pick(own, away, scal, sh, slot), wd[slot], NT)
+        grad = grad + mm(pick(own, away, seq, scal, sh, slot), wd[slot], NT)
     out[0] = (grad * slope[0].astype(F32)).astype(BF16)
 
 
-def back_body(sh, scal, own, away, fq, fk, vals, ctx, rden, carry, cos, sin, ph, pw, *refs):
+def back_body(sh, k, seq, scal, own, away, fq, fk, vals, ctx, rden, carry, cos, sin, ph, pw, *refs):
     blocks = refs[: sh.pairs * sh.chunks]
     dq_out, dk_out, dv_out, st_out, wo = refs[sh.pairs * sh.chunks :]
-    width, seq = sh.width, pl.program_id(0)
-
-    @pl.when(seq == 0)
-    def _():
-        fill_rows(sh, wo, blocks, 3 * sh.hu, sh.hu, 0)
-
-    gctx = mm(pick(own, away, scal, sh, 0), wo[0], NT)
+    width = sh.width
+
+    if k == 0:
+
+        @pl.when(seq == 0)
+        def _():
+            fill_rows(sh, wo, blocks, 3 * sh.hu, sh.hu, 0)
+
+    gctx = mm(pick(own, away, seq, scal, sh, 0), wo[0], NT)
     for slot in range(1, sh.pairs):
-        gctx = gctx + mm(pick(own, away, scal, sh, slot), wo[slot], NT)
+        gctx = gctx + mm(pick(own, away, seq, scal, sh, slot), wo[slot], NT)
     inverse = rden[0]
     dnum = gctx * inverse
     dden = -head_sums(gctx * ctx[0]) * inverse
@@ -726,11 +751,11 @@
     dv_out[0] = dv
 
 
-def last_body(sh, scal, dfk, dv, fk, vals, carry, cos, sin, ph, pw, dk_out, dv_out):
+def last_body(sh, k, seq, scal, dfk, dv, fk, vals, carry, cos, sin, ph, pw, dk_out, dv_out):
     fkb = fk[0]
     sums, totals = load_state(sh, scal, carry)
     state = block_diag(sums).astype(BF16)
-    goes = Rows(scal, pl.program_id(0), sh.chunk, sh.docs).goes
+    goes = Rows(scal, seq, sh.chunk, sh.docs).goes
     more_k = mm(vals[0].astype(BF16), state, NT) + totals
     total_k = dfk[0] + jnp.where(goes, more_k, 0.0)
     dv_out[0] = (dv[0] + jnp.where(goes, mm(fkb, state), 0.0)).astype(BF16)
@@ -775,43 +800,35 @@
             refs[0][j] = value.astype(BF16)
 
 
-def rows_grad_body(sh, scal, dq, dk, dv, gh, own, away, g1, g2, *refs):
+def rows_grad_body(sh, k, seq, scal, dq, dk, dv, gh, own, away, g1, g2, *refs):
     count = sh.pairs * sh.chunks
     blocks_a, blocks_u = refs[:count], refs[count : 2 * count]
     own_out, away_out, sums, wt, wu, n_ref = refs[2 * count :]
-    seq = pl.program_id(0)
-    half = pl.num_programs(0) // 2
-
-    @pl.when(seq == 0)
-    def _():
-        for kind in range(3):
-            fill_rows(sh, wt, blocks_a, kind * sh.hu, sh.hu, kind * sh.width)
-        for slot in range(sh.pairs):
-            for j in range(sh.chunks):
-                wu[slot, :, j * sh.hf : (j + 1) * sh.hf] = blocks_u[slot * sh.chunks + j][...]
-        sums[...] = jnp.zeros(sums.shape, F32)
-
-    x = jnp.where(seq < half, own[0], away[0]).astype(F32)
+
+    if k == 0:
+
+        @pl.when(seq == 0)
+        def _():
+            for kind in range(3):
+                fill_rows(sh, wt, blocks_a, kind * sh.hu, sh.hu, kind * sh.width)
+            for slot in range(sh.pairs):
+                for j in range(sh.chunks):
+                    wu[slot, :, j * sh.hf : (j + 1) * sh.hf] = blocks_u[slot * sh.chunks + j][...]
+            sums[...] = jnp.zeros(sums.shape, F32)
+
+    x = jnp.where(seq < sh.half, own[0], away[0]).astype(F32)
     n_ref[...] = normalize(x)[0]
+    qkv = jnp.concatenate([dq[0], dk[0], dv[0]], axis=1)
     for slot in range(sh.pairs):
         cols = sh.cols(scal, slot)
-        one = mm(dq[0], wt[slot, : sh.width, :])
-        one = one + mm(dk[0], wt[slot, sh.width : 2 * sh.width, :])
-        one = one + mm(dv[0], wt[slot, 2 * sh.width :, :])
+        one = mm(qkv, wt[slot])
         two = mm(gh[0], wu[slot], NT)
         n = n_ref[:, cols]
         for at, value in enumerate((one * n, one, two * n, two)):
             line = slice(at, at + 1)
             sums[line, cols] = sums[line, cols] + jnp.sum(value, axis=0, keepdims=True)
         e = (one * g1[:, cols] + two * g2[:, cols]).astype(BF16)
-
-        @pl.when(seq < half)
-        def _():
-            own_out[0, :, cols] = e
-
-        @pl.when(seq >= half)
-        def _():
-            away_out[0, :, cols] = e
+        store_half(sh, seq, cols, e, own_out, away_out)
 
 
 def tokens_grad_body(scal, mine, got, tokens, cot, out):
@@ -969,6 +986,7 @@
     width, ff, dp = sh.width, sh.ff, sh.dp
     half = 2 * micro
     count = 2 * half
+    sh.half = half
     total = count * chunk
     whole_rows = lambda array: array.reshape(total, array.shape[-1])
     bind = lambda body, *first: functools.partial(body, *first)
@@ -1062,7 +1080,8 @@
 
     high, low, weighting = tables(width // HEAD_DIM)
     maps = [whole(jnp.asarray(high)), whole(jnp.asarray(low))]
-    turns = [by_seq(cos), by_seq(sin)]
+    turns = [by_seq(cos, PER), by_seq(sin, PER)]
+    turns_one = [by_seq(cos), by_seq(sin)]
 
     def straddles(first, second):
         lower, higher = jnp.minimum(first, second), jnp.maximum(first, second)
@@ -1071,10 +1090,11 @@
     edges = [(2 * lay.hi + step) * chunk for step in range(3)]
     scale = lambda a, b: straddles(edges[a], edges[b])[:, None, None]
 
-    rows_new = lambda size, kind: by_seq(new((count, chunk, size), kind))
-    state_new = by_seq(new((count, STATE_ROWS, width), BF16))
+    rows_new = lambda size, kind: by_seq(new((count, chunk, size), kind), PER)
+    rows_one = lambda size, kind: by_seq(new((count, chunk, size), kind))
+    state_one = by_seq(new((count, STATE_ROWS, width), BF16))
     norm_ins = [whole(vec) for vec in gains]
-    norm_outs = [rows_new(dim, BF16), rows_new(dim, BF16)]
+    norm_outs = [by_seq(new((count, chunk, dim), BF16))] * 2
     n_one, n_two = call(
         "norms_own", norm_body, core_only, (half,), [by_seq(x_own)] + norm_ins, norm_outs
     )
@@ -1091,11 +1111,12 @@
         [(array, block, rest) for array, block, _ in norm_outs], aliases={6: 0, 7: 1},
     )
     in_a = [whole(block) for block in (block_a, beside_a, cross_a, across_a)]
-    fq, fk, vals, num, den, state = call(
-        "attend", bind(attend_body, sh), scal, (count,),
-        [by_seq(n_one)] + turns + maps + [whole(jnp.asarray(weighting))] + in_a,
-        [rows_new(width, BF16)] * 2 + [rows_new(width, F32)] * 3 + [state_new],
+    fq, fk, vals, num, den, state = seq_call(
+        "attend", bind(attend_body, sh), scal, count,
+        [by_seq(n_one)] + turns_one + maps + [whole(jnp.asarray(weighting))] + in_a,
+        [rows_one(width, BF16)] * 2 + [rows_one(width, F32)] * 3 + [state_one],
         [pltpu.VMEM((sh.pairs, 3 * width, dp), BF16)],
+        per=1,
     )
     n_two, fq, state, beside_u, across_u, cot_y, cot_z = hold(
         (n_two, fq, state, beside_u, across_u, cot_y, cot_z)
@@ -1103,8 +1124,8 @@
     in_u = [whole(block) for block in (block_u, beside_u, cross_u, across_u)]
     state_got = send_states(lay, state, scale, False)
     cot_both = second_swaps(cot_y, cot_z)
-    act, slope = call(
-        "up", bind(up_body, sh), scal, (count,), [by_seq(n_two)] + in_u,
+    act, slope = seq_call(
+        "up", bind(up_body, sh), scal, count, [by_seq(n_two, PER)] + in_u,
         [rows_new(ff, BF16)] * 2, [pltpu.VMEM((sh.pairs, dp, ff), BF16)],
     )
     act, num, state_got, beside_d, cot_both0, cot_both1 = hold(
@@ -1113,9 +1134,9 @@
     across_d = cross(beside_d)
     g_own, g_away = team_rows(cotangent, cot_y, cot_z, (cot_both0, cot_both1))
     carry = combine_states(lay, state, state_got, scale, False)
-    ctx, rden = call(
-        "finish", bind(finish_body, sh), scal, (count,),
-        [by_seq(a) for a in (after(num, g_own), den, fq, carry)], [rows_new(width, F32)] * 2,
+    ctx, rden = seq_call(
+        "finish", bind(finish_body, sh), scal, count,
+        [by_seq(a, PER) for a in (after(num, g_own), den, fq, carry)], [rows_new(width, F32)] * 2,
     )
     g_own, g_away, ctx, across_d = hold((g_own, g_away, ctx, across_d))
     in_d = [whole(block) for block in (block_d, beside_d, cross_d, across_d)]
@@ -1186,12 +1207,16 @@
     down_part, down_got = pair_sums(down_make)
 
     ctx = after(ctx, down_part)
-    halves_new = [
+    halves_one = [
         own_seq(new((half, chunk, dim), BF16)), away_seq(new((half, chunk, dim), BF16))
     ]
-    branch_own, branch_away = call(
-        "branch", bind(branch_body, sh), scal, (count,),
-        [by_seq(ctx), by_seq(act)] + in_a + in_d, halves_new,
+    halves_new = [
+        own_seq(new((half, chunk, dim), BF16), PER),
+        away_seq(new((half, chunk, dim), BF16), PER),
+    ]
+    branch_own, branch_away = seq_call(
+        "branch", bind(branch_body, sh), scal, count,
+        [by_seq(ctx, PER), by_seq(act, PER)] + in_a + in_d, halves_new,
         [pltpu.VMEM((sh.pairs, width, dp), BF16), pltpu.VMEM((sh.pairs, ff, dp), BF16)],
     )
 
@@ -1217,57 +1242,67 @@
     down_got, branch_own, branch_away, ctx = hold((down_got, branch_own, branch_away, ctx))
     m_got = lay.core_swap(branch_away)
 
-    dq, dk_part, dv_part, dstate = call(
-        "attend_back", bind(back_body, sh), scal, (count,),
-        [own_seq(g_own), away_seq(g_away)]
-        + [by_seq(a) for a in (fq, fk, vals, ctx, rden, carry)]
-        + turns + maps + in_a,
-        [rows_new(width, BF16), rows_new(width, F32), rows_new(width, F32), state_new],
-        [pltpu.VMEM((sh.pairs, width, dp), BF16)],
-    )
-    branch_own, m_got, dq, dstate = hold((branch_own, m_got, dq, dstate))
+    (grad_hidden,) = seq_call(
+        "hidden_grad", bind(hidden_body, sh), scal, count,
+        [own_seq(g_own, PER), away_seq(g_away, PER), by_seq(after(slope, branch_own), PER)] + in_d,
+        [rows_new(ff, BF16)], [pltpu.VMEM((sh.pairs, ff, dp), BF16)],
+    )
+    branch_own, m_got, grad_hidden, ctx = hold((branch_own, m_got, grad_hidden, ctx))
     m_keeps, m_sends = first_sums(branch_own, m_got)
     m_gots = round_one(m_sends)
+    ctx_back = after(ctx, *m_sends)
+    dq, dk_part, dv_part, dstate = seq_call(
+        "attend_back", bind(back_body, sh), scal, count,
+        [own_seq(g_own), away_seq(g_away)]
+        + [by_seq(a) for a in (fq, fk, vals, ctx_back, rden, carry)]
+        + turns_one + maps + in_a,
+        [rows_one(width, BF16), rows_one(width, F32), rows_one(width, F32), state_one],
+        [pltpu.VMEM((sh.pairs, width, dp), BF16)],
+        per=1,
+    )
+    dq, dstate, dk_part, grad_hidden, *m_parts = hold(
+        (dq, dstate, dk_part, grad_hidden) + m_keeps + m_gots
+    )
     state_got = send_states(lay, dstate, scale, True)
-    (grad_hidden,) = call(
-        "hidden_grad", bind(hidden_body, sh), scal, (count,),
-        [own_seq(g_own), away_seq(g_away), by_seq(after(slope, *m_sends))] + in_d,
-        [rows_new(ff, BF16)], [pltpu.VMEM((sh.pairs, ff, dp), BF16)],
-    )
-    grad_hidden, state_got = hold((grad_hidden, state_got))
-    dcarry = combine_states(lay, dstate, state_got, scale, True)
+    down_parts = down_make(0, after(down_got, dq))
+    dk_part, state_got, grad_hidden, *down_parts = hold(
+        (dk_part, state_got, grad_hidden) + tuple(down_parts)
+    )
+    down_ends = hi_sums(down_parts)
     up_make = lambda slot, got: unit_grads(
         "up_grad", whole_rows(grad_hidden), [whole_rows(n_two)], slot, got
     )
     up_part, up_got = pair_sums(up_make)
-    dk_part, *m_parts = hold((dk_part,) + m_keeps + m_gots, up_part)
+    dk_part = after(dk_part, up_part)
+    dcarry = combine_states(lay, dstate, state_got, scale, True)
+    dk, dv = seq_call(
+        "keys_back", bind(last_body, sh), scal, count,
+        [by_seq(a, PER) for a in (dk_part, dv_part, fk, vals, dcarry)]
+        + turns + maps,
+        [rows_new(width, BF16)] * 2,
+    )
+    dk, up_got, *m_parts = hold((dk, up_got) + tuple(m_parts))
     m_keeps, m_sends = second_sums(m_parts[:2], m_parts[2:])
     m_gots = round_two(m_sends)
-    dk, dv = call(
-        "keys_back", bind(last_body, sh), scal, (count,),
-        [by_seq(a) for a in (after(dk_part, *m_sends), dv_part, fk, vals, dcarry)]
-        + turns + maps,
-        [rows_new(width, BF16)] * 2,
-    )
-    dk, up_got, *m_parts = hold((dk, up_got) + m_keeps + m_gots)
-    up_parts = up_make(0, up_got)
-    dk, *up_parts = hold((dk,) + tuple(up_parts))
-    up_ends = hi_sums(up_parts)
-    mixed = tokens.astype(F32) + join_micro(m_parts[:2]).astype(F32)
-    mixed = (mixed + join_micro(m_parts[2:]).astype(F32)).astype(BF16)
-    own, away, sums = call(
-        "rows_grad", bind(rows_grad_body, sh), scal, (count,),
-        [by_seq(a) for a in (after(dq, mixed), dk, dv, grad_hidden)]
+    own, away, sums = seq_call(
+        "rows_grad", bind(rows_grad_body, sh), scal, count,
+        [by_seq(a) for a in (after(dq, *m_sends), dk, dv, grad_hidden)]
         + [own_seq(x_own), away_seq(x_away)]
         + [whole(gains[0]), whole(gains[2])] + in_a + in_u,
-        halves_new + [whole(new((8, dim), F32))],
+        halves_one + [whole(new((8, dim), F32))],
         [
             pltpu.VMEM((sh.pairs, 3 * width, dp), BF16),
             pltpu.VMEM((sh.pairs, dp, ff), BF16),
             pltpu.VMEM((chunk, dim), F32),
         ],
-    )
-    own, away, sums, dq, up_ends = hold((own, away, sums, dq, up_ends))
+        per=1,
+    )
+    own, away, sums, dq, down_end0, down_end1, *m_gots = hold(
+        (own, away, sums, dq) + down_ends + m_gots
+    )
+    down_ends = down_end0, down_end1
+    mixed = tokens.astype(F32) + join_micro(m_keeps).astype(F32)
+    mixed = (mixed + join_micro(m_gots).astype(F32)).astype(BF16)
     e_got = lay.core_swap(away)
     sums = sums[:4]
     sums_got = lay.lo_swap(sums, 1)
@@ -1278,29 +1313,28 @@
     sums_got = lay.core_swap(sums)
     e_keeps, e_sends = first_sums(own, e_got)
     e_gots = round_one(e_sends)
-    down_parts = down_make(0, after(down_got, *e_sends))
-    head_got, sums_got, *down_parts = hold((head_got, sums_got) + tuple(down_parts))
-    down_ends = hi_sums(down_parts)
+    up_parts = up_make(0, after(up_got, *e_sends))
+    head_got, sums_got, *up_parts = hold((head_got, sums_got) + tuple(up_parts))
+    up_ends = hi_sums(up_parts)
     sums = sums + sums_got
     sums_got = lay.move(sums, lambda p, c, h, l: (1 - p, c, h, l))
     head_parts = head_make(0, after(head_got, sums))
-    e_keep0, e_keep1, e_got0, e_got1, sums_got, down_end0, down_end1, *head_parts = hold(
-        e_keeps + e_gots + (sums_got,) + down_ends + tuple(head_parts)
-    )
-    down_ends = (down_end0, down_end1)
+    held = hold(e_keeps + e_gots + (sums_got,) + up_ends + tuple(head_parts))
+    e_keeps, e_gots, sums_got = held[:2], held[2:4], held[4]
+    up_ends, head_parts = held[5:7], held[7:]
+    head_ends = hi_sums(head_parts)
     sums = sums + sums_got
-    sums_got = lay.lo_swap(sums, 2)
-    head_ends = hi_sums(head_parts)
-    e_keeps, e_sends = second_sums((e_keep0, e_keep1), (e_got0, e_got1))
-    sums_got, *e_sends = hold((sums_got,) + e_sends)
+    e_keeps, e_sends = second_sums(e_keeps, e_gots)
     e_gots = round_two(e_sends)
-    sums = sums + sums_got
+    sums_got = lay.lo_swap(after(sums, *e_sends), 2)
     units_ends = trade(hold(up_ends, *e_sends)) + trade(hold(down_ends, *e_sends))
     grads_units = call(
         "end_units", bind(end_units_body, sh), core_only, (), units_ends,
         [whole(new(w.shape, F32)) for w in (up_weight, down_weight)],
     )
-    e_gots = hold(e_gots, grads_units[0])
+    e_got0, e_got1, sums_got = hold(e_gots + (sums_got,), grads_units[0])
+    e_gots = e_got0, e_got1
+    sums = sums + sums_got
     mine, got = join_micro(e_keeps), join_micro(e_gots)
     (grad_tokens,) = call(
         "tokens_grad", tokens_grad_body, scal, (micro,),

time: 312 us -> 298 us (0.955)
  Pallas kernels: 179 us -> 167 us
  starting transfers between devices: 56.4 us -> 47.3 us
  waiting for transfers between devices: 35.7 us -> 42.7 us
    pallas_call x20, Pallas kernels: 179 us -> 167 us  [call(): pl.pallas_call(body, name=name, grid_spec=pltpu.PrefetchScalarGridSpec(nu...]
    ppermute x49, starting transfers between devices: 56.4 us -> 47.3 us  [move(): return lax.ppermute(values, AXES, links)]
    ppermute x49, waiting for transfers between devices: 35.7 us -> 42.7 us  [move(): return lax.ppermute(values, AXES, links)]
  transfers between devices with their start and end apart: 49 -> 49, of which waited for: 16 -> 17; matrix products, arithmetic and copies ran while one was open for 8% -> 8% of each run, Pallas kernels for 52% -> 52%
where the time goes in v3:
time: 298 us; the launch traced here: 297 us
  Pallas kernels  167 us (56%)
  starting transfers between devices  47.3 us (16%)
  waiting for transfers between devices  42.7 us (14%)
  other arithmetic  26 us (9%)
  local copies, waits for them, and re-layouts  12.9 us (4%)
    pallas_call x20, Pallas kernels, call(): pl.pallas_call(body, name=name, grid_spec=pltpu.PrefetchScalarGridSpec(nu...  167 us
    ppermute x49, starting transfers between devices, move(): return lax.ppermute(values, AXES, links)  47.3 us
    ppermute x49, waiting for transfers between devices, move(): return lax.ppermute(values, AXES, links)  42.7 us
    mul x1, other arithmetic, team_local(): sin = jnp.sin(angles) * jnp.asarray(side, F32)[None, None, :]  7.03 us
  transfers between devices with their start and end apart: 49, of which 17 were waited for; matrix products, arithmetic and copies ran while one was open for 8% of the time, Pallas kernels for 52%

profile of v3, /device:TPU:0, one launch (start us, length us, event | category | flops | bytes accessed | tf_op | source)
XLA Modules:
  0.0 297.1 jit_solution(5043946363528094543)
XLA Ops:
  1.7 2.7 pack.1
  7.6 2.9 collective-permute-start.7
  10.6 2.6 collective-permute-start.6
  13.2 1.6 collective-permute-start.5
  14.7 1.5 collective-permute-start.4
  17.6 7.0 %fusion = (f32[8,384,128]{2,1,0:T(8,128)}, f32[8,384,128]{2,1,0:T(8,128)}) fusion(f32[128]{0:T(128)S(1)} %copy-done.32, f32[128]{0:T(128)S(1)} %copy-done.33, f32[8,384]{1,0:T(8,128)S(1)} %fusion.13), kind=kLoop, calls=%fused_computation.10 | loop fusion | flops 786432 | bytes 3159040 | tf_op jit(solution)/shard_map/mul | solution.py:1070
  25.2 11.6 %collective-permute-done.5 = bf16[2,192,1024]{2,1,0:T(8,128)(2,1)S(1)} collective-permute-done((bf16[2,192,1024]{2,1,0:T(8,128)(2,1)}, bf16[2,192,1024]{2,1,0:T(8,128)(2,1)S(1)}, u32[]{:S(2)}, u32[]{:S(2)}) %collective-permute-start.5) | collective-permute-done | bytes 786464 | tf_op jit(solution)/shard_map/ppermute | solution.py:881
  36.9 1.6 collective-permute-start.9
  40.5 5.9 %collective-permute-done.11.refs_9_.refs_5_.refs_15_.refs_11_ = bf16[256,512]{1,0:T(8,128)(2,1)S(1)} collective-permute-done((bf16[256,512]{1,0:T(8,128)(2,1)S(1)}, bf16[256,512]{1,0:T(8,128)(2,1)S(1)}, u32[]{:S(2)}, u32[]{:S(2)}) %collective-permute-start.11) | collective-permute-done | bytes 262176 | tf_op jit(solution)/shard_map/ppermute | solution.py:881
  50.4 6.9 %norms_own.1 = (bf16[8,384,1024]{2,1,0:T(8,128)(2,1)}, bf16[8,384,1024]{2,1,0:T(8,128)(2,1)}) custom-call(s32[4]{0:T(128)} %stack.104.scal, bf16[4,384,1024]{2,1,0:T(8,128)(2,1)} %bitcast.196, f32[1,1024]{1,0:T(1,128)} %bitcast.220, f32[1,1024]{1,0:T(1,128)} %bitcast.229, f32[1,1024]{1,0:T(1,128)} %bitcast.223, f32[1,1024]{1,0:T(1,128)} %bitcast.231), custom_call_target="tpu_custom_call" | custom-call | tf_op jit(solution)/shard_map/norms_own/pallas_call | solution.py:483
  57.6 1.6 collective-permute-start.17
  59.7 1.6 collective-permute-start.14
  63.4 6.9 %norms_away.1 = (bf16[8,384,1024]{2,1,0:T(8,128)(2,1)}, bf16[8,384,1024]{2,1,0:T(8,128)(2,1)}) custom-call(s32[4]{0:T(128)} %stack.104.scal, bf16[4,384,1024]{2,1,0:T(8,128)(2,1)} %copy-done.3, f32[1,1024]{1,0:T(1,128)} %bitcast.221, f32[1,1024]{1,0:T(1,128)} %bitcast.230, f32[1,1024]{1,0:T(1,128)} %bitcast.224, ...), custom_call_target="tpu_custom_call", output_to_operand_aliasing={{0}: (6, {}), {1}: (7, {})} | custom-call | tf_op jit(solution)/shard_map/norms_away/pallas_call | solution.py:483
  70.3 16.7 %attend.1 = (bf16[8,384,128]{2,1,0:T(8,128)(2,1)}, bf16[8,384,128]{2,1,0:T(8,128)(2,1)}, f32[8,384,128]{2,1,0:T(8,128)}, f32[8,384,128]{2,1,0:T(8,128)}, f32[8,3...) custom-call(s32[52]{0:T(128)} %concatenate.46.scal, bf16[8,384,1024]{2,1,0:T(8,128)(2,1)} %get-tuple-element.193.refs_0_, ...), custom_call_target="tpu_custom_call" | custom-call | tf_op jit(solution)/shard_map/attend/pallas_call | solution.py:483
  92.3 1.7 collective-permute-start.19
  94.1 3.4 %collective-permute-start.18 = (bf16[4,80,128]{2,1,0:T(8,128)(2,1)S(1)}, bf16[4,80,128]{2,1,0:T(8,128)(2,1)S(1)}, u32[]{:S(2)}, u32[]{:S(2)}) collective-permute-start(bf16[4,80,128]{2,1,0:T(8,128)(2,1)S(1)} %fusion.10), channel_id=1, source_target_pairs={{0,4},{1,5},{2,6},{3,7},{8,12},{9,13},{10,14},{11,15},{16,20},{17,... | collective-permute-start | bytes 245768 | tf_op jit(solution)/shard_map/ppermute | solution.py:881
  97.5 10.1 %up.3 = (bf16[8,384,512]{2,1,0:T(8,128)(2,1)}, bf16[8,384,512]{2,1,0:T(8,128)(2,1)}) custom-call(s32[52]{0:T(128)} %concatenate.46.scal, bf16[8,384,1024]{2,1,0:T(8,128)(2,1)} %get-tuple-element.204.refs_0_, bf16[512,256]{1,0:T(8,128)(2,1)} %maximum_select_fusion.1.refs_1_.refs_12_, bf16[512,256]{1,0:T(8,128)(2,1)} %collective-permute-done.14.refs_2_.refs_13_, ...), custom_call_target="tpu_custom_call" | custom-call | tf_op jit(solution)/shard_map/up/pallas_call | solution.py:483
  107.6 1.5 maximum_bitcast_fusion.2
  113.1 5.9 %finish.1 = (f32[8,384,128]{2,1,0:T(8,128)}, f32[8,384,128]{2,1,0:T(8,128)}) custom-call(s32[52]{0:T(128)} %concatenate.46.scal, f32[8,384,128]{2,1,0:T(8,128)} %get-tuple-element.214.refs_0_, f32[8,384,128]{2,1,0:T(8,128)} %get-tuple-element.215.refs_1_, bf16[8,384,128]{2,1,0:T(8,128)(2,1)} %get-tuple-element.216.refs_2_, f32[8,80,128]{2,1,0:T(8,128)} %bitcast.211), custom_call_target="tpu_custom_call" | custom-call | tf_op jit(solution)/shard_map/finish/pallas_call | solution.py:483
  119.9 1.7 copy-done.1
  121.6 5.8 %down_grad1.1 = bf16[2,256,512]{2,1,0:T(8,128)(2,1)} custom-call(s32[52]{0:T(128)} %concatenate.46.scal, bf16[3072,512]{1,0:T(8,128)(2,1)} %bitcast.193, bf16[1536,1024]{1,0:T(8,128)(2,1)} %bitcast.177, bf16[1536,1024]{1,0:T(8,128)(2,1)} %bitcast.183), custom_call_target="tpu_custom_call" | custom-call | tf_op jit(solution)/shard_map/down_grad1/pallas_call | solution.py:483
  128.3 10.3 %branch.1 = (bf16[4,384,1024]{2,1,0:T(8,128)(2,1)}, bf16[4,384,1024]{2,1,0:T(8,128)(2,1)}) custom-call(s32[52]{0:T(128)} %concatenate.46.scal, f32[8,384,128]{2,1,0:T(8,128)} %get-tuple-element.239.refs_0_.refs_5_, bf16[8,384,512]{2,1,0:T(8,128)(2,1)} %get-tuple-element.224.refs_1_, bf16[256,512]{1,0:T(8,128)(2,1)} %copy-done.6, bf16[256,512]{1,0:T(8,128)(2,1)} %copy-done.8, ...), custom_call_target="tpu_custom_call" | custom-call | tf_op jit(solution)/shard_map/branch/pallas_call | solution.py:483
  138.7 2.4 collective-permute-done.24.refs_2_
  141.0 9.6 %hidden_grad.1.refs_3_ = bf16[8,384,512]{2,1,0:T(8,128)(2,1)} custom-call(s32[52]{0:T(128)} %concatenate.46.scal, bf16[4,384,1024]{2,1,0:T(8,128)(2,1)} %bitcast.178, bf16[4,384,1024]{2,1,0:T(8,128)(2,1)} %copy-done.1, bf16[8,384,512]{2,1,0:T(8,128)(2,1)} %get-tuple-element.234.refs_2_, bf16[256,512]{1,0:T(8,128)(2,1)} %copy-done.12, ...), custom_call_target="tpu_custom_call" | custom-call | tf_op jit(solution)/shard_map/hidden_grad/pallas_call | solution.py:483
  150.6 1.5 convert_add_fusion.1
  152.8 1.6 collective-permute-start.27
  155.0 22.6 %attend_back.1 = (bf16[8,384,128]{2,1,0:T(8,128)(2,1)}, f32[8,384,128]{2,1,0:T(8,128)}, f32[8,384,128]{2,1,0:T(8,128)}, bf16[8,80,128]{2,1,0:T(8,128)(2,1)}) custom-call(s32[52]{0:T(128)} %concatenate.46.scal, bf16[4,384,1024]{2,1,0:T(8,128)(2,1)} %bitcast.179, bf16[4,384,1024]{2,1,0:T(8,128)(2,1)} %copy-done.1, ...), custom_call_target="tpu_custom_call" | custom-call | tf_op jit(solution)/shard_map/attend_back/pallas_call | solution.py:483
  178.6 1.5 collective-permute-start.28
  180.1 6.0 %down_grad0.1 = (bf16[256,512]{1,0:T(8,128)(2,1)}, bf16[256,512]{1,0:T(8,128)(2,1)}) custom-call(s32[52]{0:T(128)} %concatenate.46.scal, bf16[3072,512]{1,0:T(8,128)(2,1)} %bitcast.194, bf16[1536,1024]{1,0:T(8,128)(2,1)} %bitcast.180, bf16[1536,1024]{1,0:T(8,128)(2,1)} %bitcast.184, bf16[2,256,512]{2,1,0:T(8,128)(2,1)} %copy-done.21), custom_call_target="tpu_custom_call" | custom-call | tf_op jit(solution)/shard_map/down_grad0/pallas_call | solution.py:483
  187.2 5.8 %up_grad1.1 = bf16[2,256,512]{2,1,0:T(8,128)(2,1)} custom-call(s32[52]{0:T(128)} %concatenate.46.scal, bf16[3072,512]{1,0:T(8,128)(2,1)} %bitcast.191, bf16[3072,1024]{1,0:T(8,128)(2,1)} %bitcast.189), custom_call_target="tpu_custom_call" | custom-call | tf_op jit(solution)/shard_map/up_grad1/pallas_call | solution.py:483
  194.8 8.0 %keys_back.1 = (bf16[8,384,128]{2,1,0:T(8,128)(2,1)}, bf16[8,384,128]{2,1,0:T(8,128)(2,1)}) custom-call(s32[52]{0:T(128)} %concatenate.46.scal, f32[8,384,128]{2,1,0:T(8,128)} %get-tuple-element.255.refs_0_, f32[8,384,128]{2,1,0:T(8,128)} %get-tuple-element.256.refs_1_, bf16[8,384,128]{2,1,0:T(8,128)(2,1)} %get-tuple-element.222.refs_3_.refs_2_, ...), custom_call_target="tpu_custom_call" | custom-call | tf_op jit(solution)/shard_map/keys_back/pallas_call | solution.py:483
  202.7 2.9 collective-permute-done.29.refs_1_
  207.4 1.5 collective-permute-start.32
  208.9 3.3 %collective-permute-start.30 = (bf16[256,512]{1,0:T(8,128)(2,1)S(1)}, bf16[256,512]{1,0:T(8,128)(2,1)S(1)}, u32[]{:S(2)}, u32[]{:S(2)}) collective-permute-start(bf16[256,512]{1,0:T(8,128)(2,1)S(1)} %copy-done.35), channel_id=1, source_target_pairs={{0,4},{1,5},{2,6},{3,7},{4,0},{5,1},{6,2},{7,3},{8,12},{9,13},{10,... | collective-permute-start | bytes 786440 | tf_op jit(solution)/shard_map/ppermute | solution.py:881
  212.1 19.1 %rows_grad.1 = (bf16[4,384,1024]{2,1,0:T(8,128)(2,1)}, bf16[4,384,1024]{2,1,0:T(8,128)(2,1)}, f32[8,1024]{1,0:T(8,128)}) custom-call(s32[52]{0:T(128)} %concatenate.46.scal, bf16[8,384,128]{2,1,0:T(8,128)(2,1)} %get-tuple-element.280.refs_0_, bf16[8,384,128]{2,1,0:T(8,128)(2,1)} %get-tuple-element.268.refs_1_, ...), custom_call_target="tpu_custom_call" | custom-call | tf_op jit(solution)/shard_map/rows_grad/pallas_call | solution.py:483
  232.1 1.5 collective-permute-start.34
  233.7 7.5 %head_grad1.1 = bf16[2,256,512]{2,1,0:T(8,128)(2,1)} custom-call(s32[52]{0:T(128)} %concatenate.46.scal, bf16[3072,128]{1,0:T(8,128)(2,1)} %bitcast.200, bf16[3072,128]{1,0:T(8,128)(2,1)} %bitcast.202, bf16[3072,128]{1,0:T(8,128)(2,1)} %bitcast.204, f32[3072,128]{1,0:T(8,128)} %bitcast.198, bf16[3072,1024]{1,0:T(8,128)(2,1)} %bitcast.187, ...), custom_call_target="tpu_custom_call" | custom-call | tf_op jit(solution)/shard_map/head_grad1/pallas_call | solution.py:483
  241.9 1.5 convert_add_fusion
  245.4 6.1 %up_grad0.1 = (bf16[256,512]{1,0:T(8,128)(2,1)}, bf16[256,512]{1,0:T(8,128)(2,1)}) custom-call(s32[52]{0:T(128)} %concatenate.46.scal, bf16[3072,512]{1,0:T(8,128)(2,1)} %bitcast.192, bf16[3072,1024]{1,0:T(8,128)(2,1)} %bitcast.190, bf16[2,256,512]{2,1,0:T(8,128)(2,1)} %copy-done.19), custom_call_target="tpu_custom_call" | custom-call | tf_op jit(solution)/shard_map/up_grad0/pallas_call | solution.py:483
  251.5 3.9 %collective-permute-done.37.refs_0_ = bf16[2,256,512]{2,1,0:T(8,128)(2,1)S(1)} collective-permute-done((bf16[2,256,512]{2,1,0:T(8,128)(2,1)}, bf16[2,256,512]{2,1,0:T(8,128)(2,1)S(1)}, u32[]{:S(2)}, u32[]{:S(2)}) %collective-permute-start.37) | collective-permute-done | bytes 524320 | tf_op jit(solution)/shard_map/ppermute | solution.py:881
  257.5 7.3 %head_grad0.1 = (bf16[256,512]{1,0:T(8,128)(2,1)}, bf16[256,512]{1,0:T(8,128)(2,1)}) custom-call(s32[52]{0:T(128)} %concatenate.46.scal, bf16[3072,128]{1,0:T(8,128)(2,1)} %bitcast.201, bf16[3072,128]{1,0:T(8,128)(2,1)} %bitcast.203, bf16[3072,128]{1,0:T(8,128)(2,1)} %bitcast.205, f32[3072,128]{1,0:T(8,128)} %bitcast.199, bf16[3072,1024]{1,0:T(8,128)(2,1)} %bitcast.188, ...), custom_call_target="tpu_custom_call" | custom-call | tf_op jit(solution)/shard_map/head_grad0/pallas_call | solution.py:483
  264.9 5.3 %collective-permute-done.40 = bf16[256,512]{1,0:T(8,128)(2,1)S(1)} collective-permute-done((bf16[256,512]{1,0:T(8,128)(2,1)}, bf16[256,512]{1,0:T(8,128)(2,1)S(1)}, u32[]{:S(2)}, u32[]{:S(2)}) %collective-permute-start.40) | collective-permute-done | bytes 262176 | tf_op jit(solution)/shard_map/ppermute | solution.py:881
  271.8 1.5 collective-permute-start.41
  276.8 2.0 collective-permute-start.43
  279.4 2.9 end_units.1
  283.5 4.7 %collective-permute-done.43 = f32[4,1024]{1,0:T(4,128)S(1)} collective-permute-done((f32[4,1024]{1,0:T(4,128)S(1)}, f32[4,1024]{1,0:T(4,128)S(1)}, u32[]{:S(2)}, u32[]{:S(2)}) %collective-permute-start.43) | collective-permute-done | bytes 16416 | tf_op jit(solution)/shard_map/ppermute | solution.py:881
  289.3 4.1 %tokens_grad.1 = f32[2,192,1024]{2,1,0:T(8,128)} custom-call(s32[52]{0:T(128)} %concatenate.46.scal, bf16[2,192,1024]{2,1,0:T(8,128)(2,1)} %pad_maximum_fusion.2.mine, bf16[2,192,1024]{2,1,0:T(8,128)(2,1)} %pad_maximum_fusion.3.got, bf16[2,192,1024]{2,1,0:T(8,128)(2,1)} %tokens.1, bf16[2,192,1024]{2,1,0:T(8,128)(2,1)} %cot.1), custom_call_target="tpu_custom_call" | custom-call | tf_op jit(solution)/shard_map/tokens_grad/pallas_call | solution.py:483
  294.0 2.5 end_heads.1
  (219 shorter events, 47.5 us)
Async XLA Ops:
  0.7 4.5 %collective-permute-start = (s32[2,3]{1,0:T(2,128)}, s32[2,3]{1,0:T(2,128)S(1)}, u32[]{:S(2)}, u32[]{:S(2)}) collective-permute-start(s32[2,3]{1,0:T(2,128)} %bitcast.237), channel_id=1, source_target_pairs={{0,8},{1,9},{2,10},{3,11},{4,12},{5,13},{6,14},{7,15},{8,0},{9,1},... | collective-permute-start | bytes 80 | tf_op jit(solution)/shard_map/ppermute | solution.py:881
  4.5 2.0 collective-permute-start.1
  4.5 2.0 collective-permute-start.2
  7.6 17.2 %collective-permute-start.7 = (bf16[256,512]{1,0:T(8,128)(2,1)S(1)}, bf16[256,512]{1,0:T(8,128)(2,1)S(1)}, u32[]{:S(2)}, u32[]{:S(2)}) collective-permute-start(bf16[256,512]{1,0:T(8,128)(2,1)S(1)} %maximum_select_fusion.refs_6_.refs_2_.refs_12_.refs_8_), channel_id=1, source_target_pairs={{0,16},{1,17},{2,18},{3,19},{4,20},{5,21},{6,22},{7,23},{8,24},{9,... | collective-permute-start | bytes 786440 | tf_op jit(solution)/shard_map/ppermute | solution.py:881
  10.6 14.7 %collective-permute-start.6 = (bf16[256,512]{1,0:T(8,128)(2,1)S(1)}, bf16[256,512]{1,0:T(8,128)(2,1)S(1)}, u32[]{:S(2)}, u32[]{:S(2)}) collective-permute-start(bf16[256,512]{1,0:T(8,128)(2,1)S(1)} %maximum_select_fusion.refs_6_.refs_2_.refs_12_.refs_8_), channel_id=1, source_target_pairs={{0,4},{1,5},{2,6},{3,7},{4,0},{5,1},{6,2},{7,3},{8,12},{9,13},{10,... | collective-permute-start | bytes 786440 | tf_op jit(solution)/shard_map/ppermute | solution.py:881
  13.2 23.7 %collective-permute-start.5 = (bf16[2,192,1024]{2,1,0:T(8,128)(2,1)}, bf16[2,192,1024]{2,1,0:T(8,128)(2,1)S(1)}, u32[]{:S(2)}, u32[]{:S(2)}) collective-permute-start(bf16[2,192,1024]{2,1,0:T(8,128)(2,1)} %tokens.1), channel_id=1, source_target_pairs={{0,2},{1,3},{2,0},{3,1},{4,6},{5,7},{6,4},{7,5},{8,10},{9,11},{10,... | collective-permute-start | bytes 2359304 | tf_op jit(solution)/shard_map/ppermute | solution.py:881
  14.7 22.1 %collective-permute-start.4 = (bf16[2,192,1024]{2,1,0:T(8,128)(2,1)}, bf16[2,192,1024]{2,1,0:T(8,128)(2,1)S(1)}, u32[]{:S(2)}, u32[]{:S(2)}) collective-permute-start(bf16[2,192,1024]{2,1,0:T(8,128)(2,1)} %tokens.1), channel_id=1, source_target_pairs={{0,1},{1,0},{2,3},{3,2},{4,5},{5,4},{6,7},{7,6},{8,9},{9,8},{10,11... | collective-permute-start | bytes 2359304 | tf_op jit(solution)/shard_map/ppermute | solution.py:881
  17.1 7.7 %collective-permute-start.8 = (bf16[512,256]{1,0:T(8,128)(2,1)}, bf16[512,256]{1,0:T(8,128)(2,1)}, u32[]{:S(2)}, u32[]{:S(2)}) collective-permute-start(bf16[512,256]{1,0:T(8,128)(2,1)} %maximum_select_fusion.1.refs_1_.refs_12_), channel_id=1, source_target_pairs={{0,16},{1,17},{2,18},{3,19},{4,20},{5,21},{6,22},{7,23},{8,24},{9,... | collective-permute-start | bytes 786440 | tf_op jit(solution)/shard_map/ppermute | solution.py:881
  36.9 9.8 %collective-permute-start.9 = (bf16[1,192,1024]{2,1,0:T(8,128)(2,1)S(1)}, bf16[1,192,1024]{2,1,0:T(8,128)(2,1)S(1)}, u32[]{:S(2)}, u32[]{:S(2)}) collective-permute-start(bf16[1,192,1024]{2,1,0:T(8,128)(2,1)S(1)} %slice.177), channel_id=1, source_target_pairs={{0,1},{1,0},{2,3},{3,2},{4,5},{5,4},{6,7},{7,6},{8,9},{9,8},{10,11... | collective-permute-start | bytes 1179656 | tf_op jit(solution)/shard_map/ppermute | solution.py:881
  38.5 9.4 %collective-permute-start.10 = (bf16[1,192,1024]{2,1,0:T(8,128)(2,1)S(1)}, bf16[1,192,1024]{2,1,0:T(8,128)(2,1)S(1)}, u32[]{:S(2)}, u32[]{:S(2)}) collective-permute-start(bf16[1,192,1024]{2,1,0:T(8,128)(2,1)S(1)} %slice.178), channel_id=1, source_target_pairs={{0,2},{1,3},{2,0},{3,1},{4,6},{5,7},{6,4},{7,5},{8,10},{9,11},{10,... | collective-permute-start | bytes 1179656 | tf_op jit(solution)/shard_map/ppermute | solution.py:881
  39.8 6.6 %collective-permute-start.11 = (bf16[256,512]{1,0:T(8,128)(2,1)S(1)}, bf16[256,512]{1,0:T(8,128)(2,1)S(1)}, u32[]{:S(2)}, u32[]{:S(2)}) collective-permute-start(bf16[256,512]{1,0:T(8,128)(2,1)S(1)} %collective-permute-done.6.refs_7_.refs_3_.refs_13_.refs_9_), channel_id=1, source_target_pairs={{0,16},{1,17},{2,18},{3,19},{4,20},{5,21},{6,22},{7,23},{8,24},{9,... | collective-permute-start | bytes 786440 | tf_op jit(solution)/shard_map/ppermute | solution.py:881
  48.8 8.8 %collective-permute-start.12 = (bf16[4,384,1024]{2,1,0:T(8,128)(2,1)S(1)}, bf16[4,384,1024]{2,1,0:T(8,128)(2,1)S(1)}, u32[]{:S(2)}, u32[]{:S(2)}) collective-permute-start(bf16[4,384,1024]{2,1,0:T(8,128)(2,1)S(1)} %bitcast.195), channel_id=1, source_target_pairs={{0,8},{1,9},{2,10},{3,11},{4,12},{5,13},{6,14},{7,15},{8,0},{9,1},... | collective-permute-start | bytes 9437192 | tf_op jit(solution)/shard_map/ppermute | solution.py:881
  48.9 8.7 %collective-permute-start.13 = (bf16[256,512]{1,0:T(8,128)(2,1)S(1)}, bf16[256,512]{1,0:T(8,128)(2,1)S(1)}, u32[]{:S(2)}, u32[]{:S(2)}) collective-permute-start(bf16[256,512]{1,0:T(8,128)(2,1)S(1)} %maximum_select_fusion.2.refs_6_.refs_3_), channel_id=1, source_target_pairs={{0,16},{1,17},{2,18},{3,19},{4,20},{5,21},{6,22},{7,23},{8,24},{9,... | collective-permute-start | bytes 786440 | tf_op jit(solution)/shard_map/ppermute | solution.py:881
  57.6 30.6 %collective-permute-start.17 = (bf16[2,192,1024]{2,1,0:T(8,128)(2,1)}, bf16[2,192,1024]{2,1,0:T(8,128)(2,1)}, u32[]{:S(2)}, u32[]{:S(2)}) collective-permute-start(bf16[2,192,1024]{2,1,0:T(8,128)(2,1)} %cot.1), channel_id=1, source_target_pairs={{0,2},{1,3},{2,0},{3,1},{4,6},{5,7},{6,4},{7,5},{8,10},{9,11},{10,... | collective-permute-start | bytes 2359304 | tf_op jit(solution)/shard_map/ppermute | solution.py:881
  59.2 29.1 %collective-permute-start.16 = (bf16[2,192,1024]{2,1,0:T(8,128)(2,1)}, bf16[2,192,1024]{2,1,0:T(8,128)(2,1)}, u32[]{:S(2)}, u32[]{:S(2)}) collective-permute-start(bf16[2,192,1024]{2,1,0:T(8,128)(2,1)} %cot.1), channel_id=1, source_target_pairs={{0,1},{1,0},{2,3},{3,2},{4,5},{5,4},{6,7},{7,6},{8,9},{9,8},{10,11... | collective-permute-start | bytes 2359304 | tf_op jit(solution)/shard_map/ppermute | solution.py:881
  59.7 27.4 %collective-permute-start.14 = (bf16[512,256]{1,0:T(8,128)(2,1)}, bf16[512,256]{1,0:T(8,128)(2,1)}, u32[]{:S(2)}, u32[]{:S(2)}) collective-permute-start(bf16[512,256]{1,0:T(8,128)(2,1)} %maximum_select_fusion.1.refs_1_.refs_12_), channel_id=1, source_target_pairs={{0,4},{1,5},{2,6},{3,7},{4,0},{5,1},{6,2},{7,3},{8,12},{9,13},{10,... | collective-permute-start | bytes 786440 | tf_op jit(solution)/shard_map/ppermute | solution.py:881
  61.3 26.0 %collective-permute-start.15 = (bf16[512,256]{1,0:T(8,128)(2,1)}, bf16[512,256]{1,0:T(8,128)(2,1)}, u32[]{:S(2)}, u32[]{:S(2)}) collective-permute-start(bf16[512,256]{1,0:T(8,128)(2,1)} %collective-permute-done.8.refs_3_.refs_14_), channel_id=1, source_target_pairs={{0,4},{1,5},{2,6},{3,7},{4,0},{5,1},{6,2},{7,3},{8,12},{9,13},{10,... | collective-permute-start | bytes 786440 | tf_op jit(solution)/shard_map/ppermute | solution.py:881
  90.3 18.8 %collective-permute-start.20 = (bf16[1,192,1024]{2,1,0:T(8,128)(2,1)S(1)}, bf16[1,192,1024]{2,1,0:T(8,128)(2,1)S(1)}, u32[]{:S(2)}, u32[]{:S(2)}) collective-permute-start(bf16[1,192,1024]{2,1,0:T(8,128)(2,1)S(1)} %slice.181), channel_id=1, source_target_pairs={{0,1},{1,0},{2,3},{3,2},{4,5},{5,4},{6,7},{7,6},{8,9},{9,8},{10,11... | collective-permute-start | bytes 1179656 | tf_op jit(solution)/shard_map/ppermute | solution.py:881
  90.9 18.2 %collective-permute-start.21 = (bf16[1,192,1024]{2,1,0:T(8,128)(2,1)S(1)}, bf16[1,192,1024]{2,1,0:T(8,128)(2,1)S(1)}, u32[]{:S(2)}, u32[]{:S(2)}) collective-permute-start(bf16[1,192,1024]{2,1,0:T(8,128)(2,1)S(1)} %slice.182), channel_id=1, source_target_pairs={{0,2},{1,3},{2,0},{3,1},{4,6},{5,7},{6,4},{7,5},{8,10},{9,11},{10,... | collective-permute-start | bytes 1179656 | tf_op jit(solution)/shard_map/ppermute | solution.py:881
  92.3 16.8 %collective-permute-start.19 = (bf16[256,512]{1,0:T(8,128)(2,1)S(1)}, bf16[256,512]{1,0:T(8,128)(2,1)S(1)}, u32[]{:S(2)}, u32[]{:S(2)}) collective-permute-start(bf16[256,512]{1,0:T(8,128)(2,1)S(1)} %copy-done.13), channel_id=1, source_target_pairs={{0,4},{1,5},{2,6},{3,7},{4,0},{5,1},{6,2},{7,3},{8,12},{9,13},{10,... | collective-permute-start | bytes 786440 | tf_op jit(solution)/shard_map/ppermute | solution.py:881
  94.1 15.0 %collective-permute-start.18 = (bf16[4,80,128]{2,1,0:T(8,128)(2,1)S(1)}, bf16[4,80,128]{2,1,0:T(8,128)(2,1)S(1)}, u32[]{:S(2)}, u32[]{:S(2)}) collective-permute-start(bf16[4,80,128]{2,1,0:T(8,128)(2,1)S(1)} %fusion.10), channel_id=1, source_target_pairs={{0,4},{1,5},{2,6},{3,7},{8,12},{9,13},{10,14},{11,15},{16,20},{17,... | collective-permute-start | bytes 245768 | tf_op jit(solution)/shard_map/ppermute | solution.py:881
  111.1 8.8 %collective-permute-start.22 = (bf16[4,384,1024]{2,1,0:T(8,128)(2,1)S(1)}, bf16[4,384,1024]{2,1,0:T(8,128)(2,1)S(1)}, u32[]{:S(2)}, u32[]{:S(2)}) collective-permute-start(bf16[4,384,1024]{2,1,0:T(8,128)(2,1)S(1)} %bitcast.176), channel_id=1, source_target_pairs={{0,8},{1,9},{2,10},{3,11},{4,12},{5,13},{6,14},{7,15},{8,0},{9,1},... | collective-permute-start | bytes 9437192 | tf_op jit(solution)/shard_map/ppermute | solution.py:881
  111.2 8.7 %collective-permute-start.23 = (bf16[256,512]{1,0:T(8,128)(2,1)S(1)}, bf16[256,512]{1,0:T(8,128)(2,1)S(1)}, u32[]{:S(2)}, u32[]{:S(2)}) collective-permute-start(bf16[256,512]{1,0:T(8,128)(2,1)S(1)} %collective-permute-done.19.refs_7_.refs_4_), channel_id=1, source_target_pairs={{0,16},{1,17},{2,18},{3,19},{4,20},{5,21},{6,22},{7,23},{8,24},{9,... | collective-permute-start | bytes 786440 | tf_op jit(solution)/shard_map/ppermute | solution.py:881
  127.4 13.6 %collective-permute-start.24 = (bf16[2,256,512]{2,1,0:T(8,128)(2,1)}, bf16[2,256,512]{2,1,0:T(8,128)(2,1)S(1)}, u32[]{:S(2)}, u32[]{:S(2)}) collective-permute-start(bf16[2,256,512]{2,1,0:T(8,128)(2,1)} %down_grad1.1), channel_id=1, source_target_pairs={{0,16},{1,17},{2,18},{3,19},{4,20},{5,21},{6,22},{7,23},{8,24},{9,... | collective-permute-start | bytes 1572872 | tf_op jit(solution)/shard_map/ppermute | solution.py:881
  141.0 9.6 %collective-permute-start.25 = (bf16[4,384,1024]{2,1,0:T(8,128)(2,1)}, bf16[4,384,1024]{2,1,0:T(8,128)(2,1)S(1)}, u32[]{:S(2)}, u32[]{:S(2)}) collective-permute-start(bf16[4,384,1024]{2,1,0:T(8,128)(2,1)} %get-tuple-element.232), channel_id=1, source_target_pairs={{0,8},{1,9},{2,10},{3,11},{4,12},{5,13},{6,14},{7,15},{8,0},{9,1},... | collective-permute-start | bytes 9437192 | tf_op jit(solution)/shard_map/ppermute | solution.py:881
  152.8 24.7 %collective-permute-start.27 = (bf16[1,2,192,1024]{3,2,1,0:T(8,128)(2,1)S(1)}, bf16[1,2,192,1024]{3,2,1,0:T(8,128)(2,1)S(1)}, u32[]{:S(2)}, u32[]{:S(2)}) collective-permute-start(bf16[1,2,192,1024]{3,2,1,0:T(8,128)(2,1)S(1)} %get-tuple-element.335), channel_id=1, source_target_pairs={{0,1},{1,0},{2,3},{3,2},{4,5},{5,4},{6,7},{7,6},{8,9},{9,8},{10,11... | collective-permute-start | bytes 2359304 | tf_op jit(solution)/shard_map/ppermute | solution.py:881
  154.4 23.2 %collective-permute-start.26 = (bf16[1,2,192,1024]{3,2,1,0:T(8,128)(2,1)S(1)}, bf16[1,2,192,1024]{3,2,1,0:T(8,128)(2,1)S(1)}, u32[]{:S(2)}, u32[]{:S(2)}) collective-permute-start(bf16[1,2,192,1024]{3,2,1,0:T(8,128)(2,1)S(1)} %get-tuple-element.337), channel_id=1, source_target_pairs={{0,2},{1,3},{2,0},{3,1},{4,6},{5,7},{6,4},{7,5},{8,10},{9,11},{10,... | collective-permute-start | bytes 2359304 | tf_op jit(solution)/shard_map/ppermute | solution.py:881
  178.6 8.6 %collective-permute-start.28 = (bf16[4,80,128]{2,1,0:T(8,128)(2,1)S(1)}, bf16[4,80,128]{2,1,0:T(8,128)(2,1)S(1)}, u32[]{:S(2)}, u32[]{:S(2)}) collective-permute-start(bf16[4,80,128]{2,1,0:T(8,128)(2,1)S(1)} %fusion.8), channel_id=1, source_target_pairs={{4,0},{5,1},{6,2},{7,3},{12,8},{13,9},{14,10},{15,11},{20,16},{21,... | collective-permute-start | bytes 245768 | tf_op jit(solution)/shard_map/ppermute | solution.py:881
  193.0 12.7 %collective-permute-start.29 = (bf16[2,256,512]{2,1,0:T(8,128)(2,1)}, bf16[2,256,512]{2,1,0:T(8,128)(2,1)S(1)}, u32[]{:S(2)}, u32[]{:S(2)}) collective-permute-start(bf16[2,256,512]{2,1,0:T(8,128)(2,1)} %up_grad1.1), channel_id=1, source_target_pairs={{0,16},{1,17},{2,18},{3,19},{4,20},{5,21},{6,22},{7,23},{8,24},{9,... | collective-permute-start | bytes 1572872 | tf_op jit(solution)/shard_map/ppermute | solution.py:881
  206.5 24.7 %collective-permute-start.31 = (bf16[1,192,1024]{2,1,0:T(8,128)(2,1)S(1)}, bf16[1,192,1024]{2,1,0:T(8,128)(2,1)S(1)}, u32[]{:S(2)}, u32[]{:S(2)}) collective-permute-start(bf16[1,192,1024]{2,1,0:T(8,128)(2,1)S(1)} %get-tuple-element.344), channel_id=1, source_target_pairs={{0,1},{1,0},{2,3},{3,2},{4,5},{5,4},{6,7},{7,6},{8,9},{9,8},{10,11... | collective-permute-start | bytes 1179656 | tf_op jit(solution)/shard_map/ppermute | solution.py:881
  207.4 23.9 %collective-permute-start.32 = (bf16[1,192,1024]{2,1,0:T(8,128)(2,1)S(1)}, bf16[1,192,1024]{2,1,0:T(8,128)(2,1)S(1)}, u32[]{:S(2)}, u32[]{:S(2)}) collective-permute-start(bf16[1,192,1024]{2,1,0:T(8,128)(2,1)S(1)} %get-tuple-element.342), channel_id=1, source_target_pairs={{0,2},{1,3},{2,0},{3,1},{4,6},{5,7},{6,4},{7,5},{8,10},{9,11},{10,... | collective-permute-start | bytes 1179656 | tf_op jit(solution)/shard_map/ppermute | solution.py:881
  208.9 22.3 %collective-permute-start.30 = (bf16[256,512]{1,0:T(8,128)(2,1)S(1)}, bf16[256,512]{1,0:T(8,128)(2,1)S(1)}, u32[]{:S(2)}, u32[]{:S(2)}) collective-permute-start(bf16[256,512]{1,0:T(8,128)(2,1)S(1)} %copy-done.35), channel_id=1, source_target_pairs={{0,4},{1,5},{2,6},{3,7},{4,0},{5,1},{6,2},{7,3},{8,12},{9,13},{10,... | collective-permute-start | bytes 786440 | tf_op jit(solution)/shard_map/ppermute | solution.py:881
  231.2 10.7 %collective-permute-start.33 = (bf16[4,384,1024]{2,1,0:T(8,128)(2,1)}, bf16[4,384,1024]{2,1,0:T(8,128)(2,1)S(1)}, u32[]{:S(2)}, u32[]{:S(2)}) collective-permute-start(bf16[4,384,1024]{2,1,0:T(8,128)(2,1)} %get-tuple-element.278), channel_id=1, source_target_pairs={{0,8},{1,9},{2,10},{3,11},{4,12},{5,13},{6,14},{7,15},{8,0},{9,1},... | collective-permute-start | bytes 9437192 | tf_op jit(solution)/shard_map/ppermute | solution.py:881
  232.1 9.8 %collective-permute-start.34 = (f32[4,1024]{1,0:T(4,128)S(1)}, f32[4,1024]{1,0:T(4,128)S(1)}, u32[]{:S(2)}, u32[]{:S(2)}) collective-permute-start(f32[4,1024]{1,0:T(4,128)S(1)} %slice.197), channel_id=1, source_target_pairs={{0,1},{1,0},{2,3},{3,2},{4,5},{5,4},{6,7},{7,6},{8,9},{9,8},{10,11... | collective-permute-start | bytes 49160 | tf_op jit(solution)/shard_map/ppermute | solution.py:881
  241.2 14.2 %collective-permute-start.37 = (bf16[2,256,512]{2,1,0:T(8,128)(2,1)}, bf16[2,256,512]{2,1,0:T(8,128)(2,1)S(1)}, u32[]{:S(2)}, u32[]{:S(2)}) collective-permute-start(bf16[2,256,512]{2,1,0:T(8,128)(2,1)} %head_grad1.1), channel_id=1, source_target_pairs={{0,16},{1,17},{2,18},{3,19},{4,20},{5,21},{6,22},{7,23},{8,24},{9,... | collective-permute-start | bytes 1572872 | tf_op jit(solution)/shard_map/ppermute | solution.py:881
  244.1 26.1 %collective-permute-start.36 = (bf16[1,2,192,1024]{3,2,1,0:T(8,128)(2,1)S(1)}, bf16[1,2,192,1024]{3,2,1,0:T(8,128)(2,1)S(1)}, u32[]{:S(2)}, u32[]{:S(2)}) collective-permute-start(bf16[1,2,192,1024]{3,2,1,0:T(8,128)(2,1)S(1)} %get-tuple-element.330), channel_id=1, source_target_pairs={{0,1},{1,0},{2,3},{3,2},{4,5},{5,4},{6,7},{7,6},{8,9},{9,8},{10,11... | collective-permute-start | bytes 2359304 | tf_op jit(solution)/shard_map/ppermute | solution.py:881
  244.7 25.6 %collective-permute-start.35 = (bf16[1,2,192,1024]{3,2,1,0:T(8,128)(2,1)S(1)}, bf16[1,2,192,1024]{3,2,1,0:T(8,128)(2,1)S(1)}, u32[]{:S(2)}, u32[]{:S(2)}) collective-permute-start(bf16[1,2,192,1024]{3,2,1,0:T(8,128)(2,1)S(1)} %get-tuple-element.332), channel_id=1, source_target_pairs={{0,2},{1,3},{2,0},{3,1},{4,6},{5,7},{6,4},{7,5},{8,10},{9,11},{10,... | collective-permute-start | bytes 2359304 | tf_op jit(solution)/shard_map/ppermute | solution.py:881
  245.3 10.1 %collective-permute-start.38 = (f32[4,1024]{1,0:T(4,128)S(1)}, f32[4,1024]{1,0:T(4,128)S(1)}, u32[]{:S(2)}, u32[]{:S(2)}) collective-permute-start(f32[4,1024]{1,0:T(4,128)S(1)} %slice_add_fusion), channel_id=1, source_target_pairs={{0,8},{1,9},{2,10},{3,11},{4,12},{5,13},{6,14},{7,15},{8,0},{9,1},... | collective-permute-start | bytes 49160 | tf_op jit(solution)/shard_map/ppermute | solution.py:881
  255.4 9.5 %collective-permute-start.39 = (f32[4,1024]{1,0:T(4,128)S(1)}, f32[4,1024]{1,0:T(4,128)S(1)}, u32[]{:S(2)}, u32[]{:S(2)}) collective-permute-start(f32[4,1024]{1,0:T(4,128)S(1)} %add.162), channel_id=1, source_target_pairs={{0,16},{1,17},{2,18},{3,19},{4,20},{5,21},{6,22},{7,23},{8,24},{9,... | collective-permute-start | bytes 49160 | tf_op jit(solution)/shard_map/ppermute | solution.py:881
  256.2 14.0 %collective-permute-start.40 = (bf16[256,512]{1,0:T(8,128)(2,1)}, bf16[256,512]{1,0:T(8,128)(2,1)S(1)}, u32[]{:S(2)}, u32[]{:S(2)}) collective-permute-start(bf16[256,512]{1,0:T(8,128)(2,1)} %get-tuple-element.289), channel_id=1, source_target_pairs={{0,4},{1,5},{2,6},{3,7},{4,0},{5,1},{6,2},{7,3},{8,12},{9,13},{10,... | collective-permute-start | bytes 786440 | tf_op jit(solution)/shard_map/ppermute | solution.py:881
  271.2 11.6 %collective-permute-start.47 = (bf16[256,512]{1,0:T(8,128)(2,1)S(1)}, bf16[256,512]{1,0:T(8,128)(2,1)S(1)}, u32[]{:S(2)}, u32[]{:S(2)}) collective-permute-start(bf16[256,512]{1,0:T(8,128)(2,1)S(1)} %copy-done.34), channel_id=1, source_target_pairs={{0,4},{1,5},{2,6},{3,7},{4,0},{5,1},{6,2},{7,3},{8,12},{9,13},{10,... | collective-permute-start | bytes 786440 | tf_op jit(solution)/shard_map/ppermute | solution.py:881
  271.8 16.4 %collective-permute-start.41 = (bf16[1,192,1024]{2,1,0:T(8,128)(2,1)S(1)}, bf16[1,192,1024]{2,1,0:T(8,128)(2,1)S(1)}, u32[]{:S(2)}, u32[]{:S(2)}) collective-permute-start(bf16[1,192,1024]{2,1,0:T(8,128)(2,1)S(1)} %get-tuple-element.340), channel_id=1, source_target_pairs={{0,1},{1,0},{2,3},{3,2},{4,5},{5,4},{6,7},{7,6},{8,9},{9,8},{10,11... | collective-permute-start | bytes 1179656 | tf_op jit(solution)/shard_map/ppermute | solution.py:881
  273.7 14.5 %collective-permute-start.42 = (bf16[1,192,1024]{2,1,0:T(8,128)(2,1)S(1)}, bf16[1,192,1024]{2,1,0:T(8,128)(2,1)S(1)}, u32[]{:S(2)}, u32[]{:S(2)}) collective-permute-start(bf16[1,192,1024]{2,1,0:T(8,128)(2,1)S(1)} %get-tuple-element.338), channel_id=1, source_target_pairs={{0,2},{1,3},{2,0},{3,1},{4,6},{5,7},{6,4},{7,5},{8,10},{9,11},{10,... | collective-permute-start | bytes 1179656 | tf_op jit(solution)/shard_map/ppermute | solution.py:881
  274.5 2.2 collective-permute-start.44
  275.3 3.4 %collective-permute-start.45 = (bf16[256,256]{1,0:T(8,128)(2,1)S(1)}, bf16[256,256]{1,0:T(8,128)(2,1)S(1)}, u32[]{:S(2)}, u32[]{:S(2)}) collective-permute-start(bf16[256,256]{1,0:T(8,128)(2,1)S(1)} %get-tuple-element.352), channel_id=1, source_target_pairs={{0,8},{1,9},{2,10},{3,11},{4,12},{5,13},{6,14},{7,15},{8,0},{9,1},... | collective-permute-start | bytes 393224 | tf_op jit(solution)/shard_map/ppermute | solution.py:881
  276.8 11.4 %collective-permute-start.43 = (f32[4,1024]{1,0:T(4,128)S(1)}, f32[4,1024]{1,0:T(4,128)S(1)}, u32[]{:S(2)}, u32[]{:S(2)}) collective-permute-start(f32[4,1024]{1,0:T(4,128)S(1)} %add.165), channel_id=1, source_target_pairs={{0,2},{1,3},{2,0},{3,1},{4,6},{5,7},{6,4},{7,5},{8,10},{9,11},{10,... | collective-permute-start | bytes 49160 | tf_op jit(solution)/shard_map/ppermute | solution.py:881
  283.5 9.9 %collective-permute-start.48 = (bf16[256,256]{1,0:T(8,128)(2,1)S(1)}, bf16[256,256]{1,0:T(8,128)(2,1)S(1)}, u32[]{:S(2)}, u32[]{:S(2)}) collective-permute-start(bf16[256,256]{1,0:T(8,128)(2,1)S(1)} %get-tuple-element.350), channel_id=1, source_target_pairs={{0,8},{1,9},{2,10},{3,11},{4,12},{5,13},{6,14},{7,15},{8,0},{9,1},... | collective-permute-start | bytes 393224 | tf_op jit(solution)/shard_map/ppermute | solution.py:881
  288.2 8.3 %collective-permute-start.46 = (f32[4,1024]{1,0:T(4,128)S(1)}, f32[4,1024]{1,0:T(4,128)S(1)}, u32[]{:S(2)}, u32[]{:S(2)}) collective-permute-start(f32[4,1024]{1,0:T(4,128)S(1)} %add.168), channel_id=1, source_target_pairs={{0,4},{1,5},{2,6},{3,7},{4,0},{5,1},{6,2},{7,3},{8,12},{9,13},{10,... | collective-permute-start | bytes 49160 | tf_op jit(solution)/shard_map/ppermute | solution.py:881
  (37 other events, 273.5 us)

commit v4 on v3

--- a/solution.py
+++ b/solution.py
@@ -1253,12 +1253,11 @@
     ctx_back = after(ctx, *m_sends)
     dq, dk_part, dv_part, dstate = seq_call(
         "attend_back", bind(back_body, sh), scal, count,
-        [own_seq(g_own), away_seq(g_away)]
-        + [by_seq(a) for a in (fq, fk, vals, ctx_back, rden, carry)]
-        + turns_one + maps + in_a,
-        [rows_one(width, BF16), rows_one(width, F32), rows_one(width, F32), state_one],
+        [own_seq(g_own, PER), away_seq(g_away, PER)]
+        + [by_seq(a, PER) for a in (fq, fk, vals, ctx_back, rden, carry)]
+        + turns + maps + in_a,
+        [rows_new(width, BF16), rows_new(width, F32), rows_new(width, F32), by_seq(new((count, STATE_ROWS, width), BF16), PER)],
         [pltpu.VMEM((sh.pairs, width, dp), BF16)],
-        per=1,
     )
     dq, dstate, dk_part, grad_hidden, *m_parts = hold(
         (dq, dstate, dk_part, grad_hidden) + m_keeps + m_gots

time: 298 us -> 297 us (level)
  no operation moved by 1% of the time
where the time goes in v4:
time: 297 us; the launch traced here: 295 us
  Pallas kernels  166 us (56%)
  starting transfers between devices  46.6 us (16%)
  waiting for transfers between devices  42.9 us (14%)
  other arithmetic  26 us (9%)
  local copies, waits for them, and re-layouts  12.9 us (4%)
    pallas_call x20, Pallas kernels, call(): pl.pallas_call(body, name=name, grid_spec=pltpu.PrefetchScalarGridSpec(nu...  166 us
    ppermute x49, starting transfers between devices, move(): return lax.ppermute(values, AXES, links)  46.6 us
    ppermute x49, waiting for transfers between devices, move(): return lax.ppermute(values, AXES, links)  42.9 us
    mul x1, other arithmetic, team_local(): sin = jnp.sin(angles) * jnp.asarray(side, F32)[None, None, :]  7.03 us
  transfers between devices with their start and end apart: 49, of which 17 were waited for; matrix products, arithmetic and copies ran while one was open for 8% of the time, Pallas kernels for 52%

profile of v4, /device:TPU:0, one launch (start us, length us, event | category | flops | bytes accessed | tf_op | source)
XLA Modules:
  0.0 295.5 jit_solution(16489311253470166971)
XLA Ops:
  1.7 2.7 pack.1
  7.6 2.9 collective-permute-start.7
  10.6 2.6 collective-permute-start.6
  13.2 1.6 collective-permute-start.5
  14.7 1.5 collective-permute-start.4
  17.6 7.0 %fusion = (f32[8,384,128]{2,1,0:T(8,128)}, f32[8,384,128]{2,1,0:T(8,128)}) fusion(f32[128]{0:T(128)S(1)} %copy-done.32, f32[128]{0:T(128)S(1)} %copy-done.33, f32[8,384]{1,0:T(8,128)S(1)} %fusion.13), kind=kLoop, calls=%fused_computation.10 | loop fusion | flops 786432 | bytes 3159040 | tf_op jit(solution)/shard_map/mul | solution.py:1070
  25.2 11.6 %collective-permute-done.5 = bf16[2,192,1024]{2,1,0:T(8,128)(2,1)S(1)} collective-permute-done((bf16[2,192,1024]{2,1,0:T(8,128)(2,1)}, bf16[2,192,1024]{2,1,0:T(8,128)(2,1)S(1)}, u32[]{:S(2)}, u32[]{:S(2)}) %collective-permute-start.5) | collective-permute-done | bytes 786464 | tf_op jit(solution)/shard_map/ppermute | solution.py:881
  36.9 1.6 collective-permute-start.9
  40.5 5.9 %collective-permute-done.11.refs_9_.refs_5_.refs_15_.refs_11_ = bf16[256,512]{1,0:T(8,128)(2,1)S(1)} collective-permute-done((bf16[256,512]{1,0:T(8,128)(2,1)S(1)}, bf16[256,512]{1,0:T(8,128)(2,1)S(1)}, u32[]{:S(2)}, u32[]{:S(2)}) %collective-permute-start.11) | collective-permute-done | bytes 262176 | tf_op jit(solution)/shard_map/ppermute | solution.py:881
  50.4 6.9 %norms_own.1 = (bf16[8,384,1024]{2,1,0:T(8,128)(2,1)}, bf16[8,384,1024]{2,1,0:T(8,128)(2,1)}) custom-call(s32[4]{0:T(128)} %stack.104.scal, bf16[4,384,1024]{2,1,0:T(8,128)(2,1)} %bitcast.196, f32[1,1024]{1,0:T(1,128)} %bitcast.220, f32[1,1024]{1,0:T(1,128)} %bitcast.229, f32[1,1024]{1,0:T(1,128)} %bitcast.223, f32[1,1024]{1,0:T(1,128)} %bitcast.231), custom_call_target="tpu_custom_call" | custom-call | tf_op jit(solution)/shard_map/norms_own/pallas_call | solution.py:483
  57.6 1.6 collective-permute-start.17
  59.7 1.6 collective-permute-start.14
  63.4 6.9 %norms_away.1 = (bf16[8,384,1024]{2,1,0:T(8,128)(2,1)}, bf16[8,384,1024]{2,1,0:T(8,128)(2,1)}) custom-call(s32[4]{0:T(128)} %stack.104.scal, bf16[4,384,1024]{2,1,0:T(8,128)(2,1)} %copy-done.3, f32[1,1024]{1,0:T(1,128)} %bitcast.221, f32[1,1024]{1,0:T(1,128)} %bitcast.230, f32[1,1024]{1,0:T(1,128)} %bitcast.224, ...), custom_call_target="tpu_custom_call", output_to_operand_aliasing={{0}: (6, {}), {1}: (7, {})} | custom-call | tf_op jit(solution)/shard_map/norms_away/pallas_call | solution.py:483
  70.3 16.7 %attend.1 = (bf16[8,384,128]{2,1,0:T(8,128)(2,1)}, bf16[8,384,128]{2,1,0:T(8,128)(2,1)}, f32[8,384,128]{2,1,0:T(8,128)}, f32[8,384,128]{2,1,0:T(8,128)}, f32[8,3...) custom-call(s32[52]{0:T(128)} %concatenate.46.scal, bf16[8,384,1024]{2,1,0:T(8,128)(2,1)} %get-tuple-element.193.refs_0_, ...), custom_call_target="tpu_custom_call" | custom-call | tf_op jit(solution)/shard_map/attend/pallas_call | solution.py:483
  90.9 1.4 collective-permute-start.21
  92.3 1.7 collective-permute-start.19
  94.1 3.2 %collective-permute-start.18 = (bf16[4,80,128]{2,1,0:T(8,128)(2,1)S(1)}, bf16[4,80,128]{2,1,0:T(8,128)(2,1)S(1)}, u32[]{:S(2)}, u32[]{:S(2)}) collective-permute-start(bf16[4,80,128]{2,1,0:T(8,128)(2,1)S(1)} %fusion.10), channel_id=1, source_target_pairs={{0,4},{1,5},{2,6},{3,7},{8,12},{9,13},{10,14},{11,15},{16,20},{17,... | collective-permute-start | bytes 245768 | tf_op jit(solution)/shard_map/ppermute | solution.py:881
  97.3 10.3 %up.3 = (bf16[8,384,512]{2,1,0:T(8,128)(2,1)}, bf16[8,384,512]{2,1,0:T(8,128)(2,1)}) custom-call(s32[52]{0:T(128)} %concatenate.46.scal, bf16[8,384,1024]{2,1,0:T(8,128)(2,1)} %get-tuple-element.204.refs_0_, bf16[512,256]{1,0:T(8,128)(2,1)} %maximum_select_fusion.1.refs_1_.refs_12_, bf16[512,256]{1,0:T(8,128)(2,1)} %collective-permute-done.14.refs_2_.refs_13_, ...), custom_call_target="tpu_custom_call" | custom-call | tf_op jit(solution)/shard_map/up/pallas_call | solution.py:483
  107.6 1.5 maximum_bitcast_fusion.2
  113.1 5.9 %finish.1 = (f32[8,384,128]{2,1,0:T(8,128)}, f32[8,384,128]{2,1,0:T(8,128)}) custom-call(s32[52]{0:T(128)} %concatenate.46.scal, f32[8,384,128]{2,1,0:T(8,128)} %get-tuple-element.214.refs_0_, f32[8,384,128]{2,1,0:T(8,128)} %get-tuple-element.215.refs_1_, bf16[8,384,128]{2,1,0:T(8,128)(2,1)} %get-tuple-element.216.refs_2_, f32[8,80,128]{2,1,0:T(8,128)} %bitcast.211), custom_call_target="tpu_custom_call" | custom-call | tf_op jit(solution)/shard_map/finish/pallas_call | solution.py:483
  119.9 1.7 copy-done.1
  121.6 5.8 %down_grad1.1 = bf16[2,256,512]{2,1,0:T(8,128)(2,1)} custom-call(s32[52]{0:T(128)} %concatenate.46.scal, bf16[3072,512]{1,0:T(8,128)(2,1)} %bitcast.193, bf16[1536,1024]{1,0:T(8,128)(2,1)} %bitcast.177, bf16[1536,1024]{1,0:T(8,128)(2,1)} %bitcast.183), custom_call_target="tpu_custom_call" | custom-call | tf_op jit(solution)/shard_map/down_grad1/pallas_call | solution.py:483
  128.3 10.3 %branch.1 = (bf16[4,384,1024]{2,1,0:T(8,128)(2,1)}, bf16[4,384,1024]{2,1,0:T(8,128)(2,1)}) custom-call(s32[52]{0:T(128)} %concatenate.46.scal, f32[8,384,128]{2,1,0:T(8,128)} %get-tuple-element.239.refs_0_.refs_5_, bf16[8,384,512]{2,1,0:T(8,128)(2,1)} %get-tuple-element.224.refs_1_, bf16[256,512]{1,0:T(8,128)(2,1)} %copy-done.6, bf16[256,512]{1,0:T(8,128)(2,1)} %copy-done.8, ...), custom_call_target="tpu_custom_call" | custom-call | tf_op jit(solution)/shard_map/branch/pallas_call | solution.py:483
  138.7 2.4 collective-permute-done.24.refs_2_
  141.0 9.6 %hidden_grad.1.refs_3_ = bf16[8,384,512]{2,1,0:T(8,128)(2,1)} custom-call(s32[52]{0:T(128)} %concatenate.46.scal, bf16[4,384,1024]{2,1,0:T(8,128)(2,1)} %bitcast.178, bf16[4,384,1024]{2,1,0:T(8,128)(2,1)} %copy-done.1, bf16[8,384,512]{2,1,0:T(8,128)(2,1)} %get-tuple-element.234.refs_2_, bf16[256,512]{1,0:T(8,128)(2,1)} %copy-done.12, ...), custom_call_target="tpu_custom_call" | custom-call | tf_op jit(solution)/shard_map/hidden_grad/pallas_call | solution.py:483
  150.6 1.5 convert_add_fusion.1
  152.8 1.6 collective-permute-start.27
  155.0 21.2 %attend_back.1 = (bf16[8,384,128]{2,1,0:T(8,128)(2,1)}, f32[8,384,128]{2,1,0:T(8,128)}, f32[8,384,128]{2,1,0:T(8,128)}, bf16[8,80,128]{2,1,0:T(8,128)(2,1)}) custom-call(s32[52]{0:T(128)} %concatenate.46.scal, bf16[4,384,1024]{2,1,0:T(8,128)(2,1)} %bitcast.179, bf16[4,384,1024]{2,1,0:T(8,128)(2,1)} %copy-done.1, ...), custom_call_target="tpu_custom_call" | custom-call | tf_op jit(solution)/shard_map/attend_back/pallas_call | solution.py:483
  178.5 6.0 %down_grad0.1 = (bf16[256,512]{1,0:T(8,128)(2,1)}, bf16[256,512]{1,0:T(8,128)(2,1)}) custom-call(s32[52]{0:T(128)} %concatenate.46.scal, bf16[3072,512]{1,0:T(8,128)(2,1)} %bitcast.194, bf16[1536,1024]{1,0:T(8,128)(2,1)} %bitcast.180, bf16[1536,1024]{1,0:T(8,128)(2,1)} %bitcast.184, bf16[2,256,512]{2,1,0:T(8,128)(2,1)} %copy-done.21), custom_call_target="tpu_custom_call" | custom-call | tf_op jit(solution)/shard_map/down_grad0/pallas_call | solution.py:483
  185.8 5.8 %up_grad1.1 = bf16[2,256,512]{2,1,0:T(8,128)(2,1)} custom-call(s32[52]{0:T(128)} %concatenate.46.scal, bf16[3072,512]{1,0:T(8,128)(2,1)} %bitcast.191, bf16[3072,1024]{1,0:T(8,128)(2,1)} %bitcast.189), custom_call_target="tpu_custom_call" | custom-call | tf_op jit(solution)/shard_map/up_grad1/pallas_call | solution.py:483
  193.3 8.0 %keys_back.1 = (bf16[8,384,128]{2,1,0:T(8,128)(2,1)}, bf16[8,384,128]{2,1,0:T(8,128)(2,1)}) custom-call(s32[52]{0:T(128)} %concatenate.46.scal, f32[8,384,128]{2,1,0:T(8,128)} %get-tuple-element.255.refs_0_, f32[8,384,128]{2,1,0:T(8,128)} %get-tuple-element.256.refs_1_, bf16[8,384,128]{2,1,0:T(8,128)(2,1)} %get-tuple-element.222.refs_3_.refs_2_, ...), custom_call_target="tpu_custom_call" | custom-call | tf_op jit(solution)/shard_map/keys_back/pallas_call | solution.py:483
  201.3 2.8 collective-permute-done.29.refs_1_
  205.8 1.5 collective-permute-start.32
  207.3 3.3 %collective-permute-start.30 = (bf16[256,512]{1,0:T(8,128)(2,1)S(1)}, bf16[256,512]{1,0:T(8,128)(2,1)S(1)}, u32[]{:S(2)}, u32[]{:S(2)}) collective-permute-start(bf16[256,512]{1,0:T(8,128)(2,1)S(1)} %copy-done.35), channel_id=1, source_target_pairs={{0,4},{1,5},{2,6},{3,7},{4,0},{5,1},{6,2},{7,3},{8,12},{9,13},{10,... | collective-permute-start | bytes 786440 | tf_op jit(solution)/shard_map/ppermute | solution.py:881
  210.5 19.1 %rows_grad.1 = (bf16[4,384,1024]{2,1,0:T(8,128)(2,1)}, bf16[4,384,1024]{2,1,0:T(8,128)(2,1)}, f32[8,1024]{1,0:T(8,128)}) custom-call(s32[52]{0:T(128)} %concatenate.46.scal, bf16[8,384,128]{2,1,0:T(8,128)(2,1)} %get-tuple-element.280.refs_0_, bf16[8,384,128]{2,1,0:T(8,128)(2,1)} %get-tuple-element.268.refs_1_, ...), custom_call_target="tpu_custom_call" | custom-call | tf_op jit(solution)/shard_map/rows_grad/pallas_call | solution.py:483
  230.5 1.5 collective-permute-start.34
  232.1 7.5 %head_grad1.1 = bf16[2,256,512]{2,1,0:T(8,128)(2,1)} custom-call(s32[52]{0:T(128)} %concatenate.46.scal, bf16[3072,128]{1,0:T(8,128)(2,1)} %bitcast.200, bf16[3072,128]{1,0:T(8,128)(2,1)} %bitcast.202, bf16[3072,128]{1,0:T(8,128)(2,1)} %bitcast.204, f32[3072,128]{1,0:T(8,128)} %bitcast.198, bf16[3072,1024]{1,0:T(8,128)(2,1)} %bitcast.187, ...), custom_call_target="tpu_custom_call" | custom-call | tf_op jit(solution)/shard_map/head_grad1/pallas_call | solution.py:483
  240.2 1.5 convert_add_fusion
  243.7 6.1 %up_grad0.1 = (bf16[256,512]{1,0:T(8,128)(2,1)}, bf16[256,512]{1,0:T(8,128)(2,1)}) custom-call(s32[52]{0:T(128)} %concatenate.46.scal, bf16[3072,512]{1,0:T(8,128)(2,1)} %bitcast.192, bf16[3072,1024]{1,0:T(8,128)(2,1)} %bitcast.190, bf16[2,256,512]{2,1,0:T(8,128)(2,1)} %copy-done.19), custom_call_target="tpu_custom_call" | custom-call | tf_op jit(solution)/shard_map/up_grad0/pallas_call | solution.py:483
  249.8 4.0 %collective-permute-done.37.refs_0_ = bf16[2,256,512]{2,1,0:T(8,128)(2,1)S(1)} collective-permute-done((bf16[2,256,512]{2,1,0:T(8,128)(2,1)}, bf16[2,256,512]{2,1,0:T(8,128)(2,1)S(1)}, u32[]{:S(2)}, u32[]{:S(2)}) %collective-permute-start.37) | collective-permute-done | bytes 524320 | tf_op jit(solution)/shard_map/ppermute | solution.py:881
  255.8 7.3 %head_grad0.1 = (bf16[256,512]{1,0:T(8,128)(2,1)}, bf16[256,512]{1,0:T(8,128)(2,1)}) custom-call(s32[52]{0:T(128)} %concatenate.46.scal, bf16[3072,128]{1,0:T(8,128)(2,1)} %bitcast.201, bf16[3072,128]{1,0:T(8,128)(2,1)} %bitcast.203, bf16[3072,128]{1,0:T(8,128)(2,1)} %bitcast.205, f32[3072,128]{1,0:T(8,128)} %bitcast.199, bf16[3072,1024]{1,0:T(8,128)(2,1)} %bitcast.188, ...), custom_call_target="tpu_custom_call" | custom-call | tf_op jit(solution)/shard_map/head_grad0/pallas_call | solution.py:483
  263.2 5.3 %collective-permute-done.40 = bf16[256,512]{1,0:T(8,128)(2,1)S(1)} collective-permute-done((bf16[256,512]{1,0:T(8,128)(2,1)}, bf16[256,512]{1,0:T(8,128)(2,1)S(1)}, u32[]{:S(2)}, u32[]{:S(2)}) %collective-permute-start.40) | collective-permute-done | bytes 262176 | tf_op jit(solution)/shard_map/ppermute | solution.py:881
  270.1 1.5 collective-permute-start.41
  275.1 2.0 collective-permute-start.43
  277.7 2.9 end_units.1
  281.8 4.7 %collective-permute-done.43 = f32[4,1024]{1,0:T(4,128)S(1)} collective-permute-done((f32[4,1024]{1,0:T(4,128)S(1)}, f32[4,1024]{1,0:T(4,128)S(1)}, u32[]{:S(2)}, u32[]{:S(2)}) %collective-permute-start.43) | collective-permute-done | bytes 16416 | tf_op jit(solution)/shard_map/ppermute | solution.py:881
  287.6 4.1 %tokens_grad.1 = f32[2,192,1024]{2,1,0:T(8,128)} custom-call(s32[52]{0:T(128)} %concatenate.46.scal, bf16[2,192,1024]{2,1,0:T(8,128)(2,1)} %pad_maximum_fusion.2.mine, bf16[2,192,1024]{2,1,0:T(8,128)(2,1)} %pad_maximum_fusion.3.got, bf16[2,192,1024]{2,1,0:T(8,128)(2,1)} %tokens.1, bf16[2,192,1024]{2,1,0:T(8,128)(2,1)} %cot.1), custom_call_target="tpu_custom_call" | custom-call | tf_op jit(solution)/shard_map/tokens_grad/pallas_call | solution.py:483
  292.3 2.5 end_heads.1
  (219 shorter events, 47.3 us)
Async XLA Ops:
  0.7 4.5 %collective-permute-start = (s32[2,3]{1,0:T(2,128)}, s32[2,3]{1,0:T(2,128)S(1)}, u32[]{:S(2)}, u32[]{:S(2)}) collective-permute-start(s32[2,3]{1,0:T(2,128)} %bitcast.237), channel_id=1, source_target_pairs={{0,8},{1,9},{2,10},{3,11},{4,12},{5,13},{6,14},{7,15},{8,0},{9,1},... | collective-permute-start | bytes 80 | tf_op jit(solution)/shard_map/ppermute | solution.py:881
  4.5 2.0 collective-permute-start.1
  4.5 2.0 collective-permute-start.2
  7.6 17.2 %collective-permute-start.7 = (bf16[256,512]{1,0:T(8,128)(2,1)S(1)}, bf16[256,512]{1,0:T(8,128)(2,1)S(1)}, u32[]{:S(2)}, u32[]{:S(2)}) collective-permute-start(bf16[256,512]{1,0:T(8,128)(2,1)S(1)} %maximum_select_fusion.refs_6_.refs_2_.refs_12_.refs_8_), channel_id=1, source_target_pairs={{0,16},{1,17},{2,18},{3,19},{4,20},{5,21},{6,22},{7,23},{8,24},{9,... | collective-permute-start | bytes 786440 | tf_op jit(solution)/shard_map/ppermute | solution.py:881
  10.6 14.7 %collective-permute-start.6 = (bf16[256,512]{1,0:T(8,128)(2,1)S(1)}, bf16[256,512]{1,0:T(8,128)(2,1)S(1)}, u32[]{:S(2)}, u32[]{:S(2)}) collective-permute-start(bf16[256,512]{1,0:T(8,128)(2,1)S(1)} %maximum_select_fusion.refs_6_.refs_2_.refs_12_.refs_8_), channel_id=1, source_target_pairs={{0,4},{1,5},{2,6},{3,7},{4,0},{5,1},{6,2},{7,3},{8,12},{9,13},{10,... | collective-permute-start | bytes 786440 | tf_op jit(solution)/shard_map/ppermute | solution.py:881
  13.2 23.7 %collective-permute-start.5 = (bf16[2,192,1024]{2,1,0:T(8,128)(2,1)}, bf16[2,192,1024]{2,1,0:T(8,128)(2,1)S(1)}, u32[]{:S(2)}, u32[]{:S(2)}) collective-permute-start(bf16[2,192,1024]{2,1,0:T(8,128)(2,1)} %tokens.1), channel_id=1, source_target_pairs={{0,2},{1,3},{2,0},{3,1},{4,6},{5,7},{6,4},{7,5},{8,10},{9,11},{10,... | collective-permute-start | bytes 2359304 | tf_op jit(solution)/shard_map/ppermute | solution.py:881
  14.7 22.1 %collective-permute-start.4 = (bf16[2,192,1024]{2,1,0:T(8,128)(2,1)}, bf16[2,192,1024]{2,1,0:T(8,128)(2,1)S(1)}, u32[]{:S(2)}, u32[]{:S(2)}) collective-permute-start(bf16[2,192,1024]{2,1,0:T(8,128)(2,1)} %tokens.1), channel_id=1, source_target_pairs={{0,1},{1,0},{2,3},{3,2},{4,5},{5,4},{6,7},{7,6},{8,9},{9,8},{10,11... | collective-permute-start | bytes 2359304 | tf_op jit(solution)/shard_map/ppermute | solution.py:881
  17.1 7.7 %collective-permute-start.8 = (bf16[512,256]{1,0:T(8,128)(2,1)}, bf16[512,256]{1,0:T(8,128)(2,1)}, u32[]{:S(2)}, u32[]{:S(2)}) collective-permute-start(bf16[512,256]{1,0:T(8,128)(2,1)} %maximum_select_fusion.1.refs_1_.refs_12_), channel_id=1, source_target_pairs={{0,16},{1,17},{2,18},{3,19},{4,20},{5,21},{6,22},{7,23},{8,24},{9,... | collective-permute-start | bytes 786440 | tf_op jit(solution)/shard_map/ppermute | solution.py:881
  36.9 9.8 %collective-permute-start.9 = (bf16[1,192,1024]{2,1,0:T(8,128)(2,1)S(1)}, bf16[1,192,1024]{2,1,0:T(8,128)(2,1)S(1)}, u32[]{:S(2)}, u32[]{:S(2)}) collective-permute-start(bf16[1,192,1024]{2,1,0:T(8,128)(2,1)S(1)} %slice.177), channel_id=1, source_target_pairs={{0,1},{1,0},{2,3},{3,2},{4,5},{5,4},{6,7},{7,6},{8,9},{9,8},{10,11... | collective-permute-start | bytes 1179656 | tf_op jit(solution)/shard_map/ppermute | solution.py:881
  38.5 9.4 %collective-permute-start.10 = (bf16[1,192,1024]{2,1,0:T(8,128)(2,1)S(1)}, bf16[1,192,1024]{2,1,0:T(8,128)(2,1)S(1)}, u32[]{:S(2)}, u32[]{:S(2)}) collective-permute-start(bf16[1,192,1024]{2,1,0:T(8,128)(2,1)S(1)} %slice.178), channel_id=1, source_target_pairs={{0,2},{1,3},{2,0},{3,1},{4,6},{5,7},{6,4},{7,5},{8,10},{9,11},{10,... | collective-permute-start | bytes 1179656 | tf_op jit(solution)/shard_map/ppermute | solution.py:881
  39.8 6.6 %collective-permute-start.11 = (bf16[256,512]{1,0:T(8,128)(2,1)S(1)}, bf16[256,512]{1,0:T(8,128)(2,1)S(1)}, u32[]{:S(2)}, u32[]{:S(2)}) collective-permute-start(bf16[256,512]{1,0:T(8,128)(2,1)S(1)} %collective-permute-done.6.refs_7_.refs_3_.refs_13_.refs_9_), channel_id=1, source_target_pairs={{0,16},{1,17},{2,18},{3,19},{4,20},{5,21},{6,22},{7,23},{8,24},{9,... | collective-permute-start | bytes 786440 | tf_op jit(solution)/shard_map/ppermute | solution.py:881
  48.8 8.8 %collective-permute-start.12 = (bf16[4,384,1024]{2,1,0:T(8,128)(2,1)S(1)}, bf16[4,384,1024]{2,1,0:T(8,128)(2,1)S(1)}, u32[]{:S(2)}, u32[]{:S(2)}) collective-permute-start(bf16[4,384,1024]{2,1,0:T(8,128)(2,1)S(1)} %bitcast.195), channel_id=1, source_target_pairs={{0,8},{1,9},{2,10},{3,11},{4,12},{5,13},{6,14},{7,15},{8,0},{9,1},... | collective-permute-start | bytes 9437192 | tf_op jit(solution)/shard_map/ppermute | solution.py:881
  48.9 8.7 %collective-permute-start.13 = (bf16[256,512]{1,0:T(8,128)(2,1)S(1)}, bf16[256,512]{1,0:T(8,128)(2,1)S(1)}, u32[]{:S(2)}, u32[]{:S(2)}) collective-permute-start(bf16[256,512]{1,0:T(8,128)(2,1)S(1)} %maximum_select_fusion.2.refs_6_.refs_3_), channel_id=1, source_target_pairs={{0,16},{1,17},{2,18},{3,19},{4,20},{5,21},{6,22},{7,23},{8,24},{9,... | collective-permute-start | bytes 786440 | tf_op jit(solution)/shard_map/ppermute | solution.py:881
  57.6 30.6 %collective-permute-start.17 = (bf16[2,192,1024]{2,1,0:T(8,128)(2,1)}, bf16[2,192,1024]{2,1,0:T(8,128)(2,1)}, u32[]{:S(2)}, u32[]{:S(2)}) collective-permute-start(bf16[2,192,1024]{2,1,0:T(8,128)(2,1)} %cot.1), channel_id=1, source_target_pairs={{0,2},{1,3},{2,0},{3,1},{4,6},{5,7},{6,4},{7,5},{8,10},{9,11},{10,... | collective-permute-start | bytes 2359304 | tf_op jit(solution)/shard_map/ppermute | solution.py:881
  59.2 29.1 %collective-permute-start.16 = (bf16[2,192,1024]{2,1,0:T(8,128)(2,1)}, bf16[2,192,1024]{2,1,0:T(8,128)(2,1)}, u32[]{:S(2)}, u32[]{:S(2)}) collective-permute-start(bf16[2,192,1024]{2,1,0:T(8,128)(2,1)} %cot.1), channel_id=1, source_target_pairs={{0,1},{1,0},{2,3},{3,2},{4,5},{5,4},{6,7},{7,6},{8,9},{9,8},{10,11... | collective-permute-start | bytes 2359304 | tf_op jit(solution)/shard_map/ppermute | solution.py:881
  59.7 27.4 %collective-permute-start.14 = (bf16[512,256]{1,0:T(8,128)(2,1)}, bf16[512,256]{1,0:T(8,128)(2,1)}, u32[]{:S(2)}, u32[]{:S(2)}) collective-permute-start(bf16[512,256]{1,0:T(8,128)(2,1)} %maximum_select_fusion.1.refs_1_.refs_12_), channel_id=1, source_target_pairs={{0,4},{1,5},{2,6},{3,7},{4,0},{5,1},{6,2},{7,3},{8,12},{9,13},{10,... | collective-permute-start | bytes 786440 | tf_op jit(solution)/shard_map/ppermute | solution.py:881
  61.3 26.0 %collective-permute-start.15 = (bf16[512,256]{1,0:T(8,128)(2,1)}, bf16[512,256]{1,0:T(8,128)(2,1)}, u32[]{:S(2)}, u32[]{:S(2)}) collective-permute-start(bf16[512,256]{1,0:T(8,128)(2,1)} %collective-permute-done.8.refs_3_.refs_14_), channel_id=1, source_target_pairs={{0,4},{1,5},{2,6},{3,7},{4,0},{5,1},{6,2},{7,3},{8,12},{9,13},{10,... | collective-permute-start | bytes 786440 | tf_op jit(solution)/shard_map/ppermute | solution.py:881
  90.3 18.8 %collective-permute-start.20 = (bf16[1,192,1024]{2,1,0:T(8,128)(2,1)S(1)}, bf16[1,192,1024]{2,1,0:T(8,128)(2,1)S(1)}, u32[]{:S(2)}, u32[]{:S(2)}) collective-permute-start(bf16[1,192,1024]{2,1,0:T(8,128)(2,1)S(1)} %slice.181), channel_id=1, source_target_pairs={{0,1},{1,0},{2,3},{3,2},{4,5},{5,4},{6,7},{7,6},{8,9},{9,8},{10,11... | collective-permute-start | bytes 1179656 | tf_op jit(solution)/shard_map/ppermute | solution.py:881
  90.9 18.2 %collective-permute-start.21 = (bf16[1,192,1024]{2,1,0:T(8,128)(2,1)S(1)}, bf16[1,192,1024]{2,1,0:T(8,128)(2,1)S(1)}, u32[]{:S(2)}, u32[]{:S(2)}) collective-permute-start(bf16[1,192,1024]{2,1,0:T(8,128)(2,1)S(1)} %slice.182), channel_id=1, source_target_pairs={{0,2},{1,3},{2,0},{3,1},{4,6},{5,7},{6,4},{7,5},{8,10},{9,11},{10,... | collective-permute-start | bytes 1179656 | tf_op jit(solution)/shard_map/ppermute | solution.py:881
  92.3 16.8 %collective-permute-start.19 = (bf16[256,512]{1,0:T(8,128)(2,1)S(1)}, bf16[256,512]{1,0:T(8,128)(2,1)S(1)}, u32[]{:S(2)}, u32[]{:S(2)}) collective-permute-start(bf16[256,512]{1,0:T(8,128)(2,1)S(1)} %copy-done.13), channel_id=1, source_target_pairs={{0,4},{1,5},{2,6},{3,7},{4,0},{5,1},{6,2},{7,3},{8,12},{9,13},{10,... | collective-permute-start | bytes 786440 | tf_op jit(solution)/shard_map/ppermute | solution.py:881
  94.1 15.0 %collective-permute-start.18 = (bf16[4,80,128]{2,1,0:T(8,128)(2,1)S(1)}, bf16[4,80,128]{2,1,0:T(8,128)(2,1)S(1)}, u32[]{:S(2)}, u32[]{:S(2)}) collective-permute-start(bf16[4,80,128]{2,1,0:T(8,128)(2,1)S(1)} %fusion.10), channel_id=1, source_target_pairs={{0,4},{1,5},{2,6},{3,7},{8,12},{9,13},{10,14},{11,15},{16,20},{17,... | collective-permute-start | bytes 245768 | tf_op jit(solution)/shard_map/ppermute | solution.py:881
  111.1 8.8 %collective-permute-start.22 = (bf16[4,384,1024]{2,1,0:T(8,128)(2,1)S(1)}, bf16[4,384,1024]{2,1,0:T(8,128)(2,1)S(1)}, u32[]{:S(2)}, u32[]{:S(2)}) collective-permute-start(bf16[4,384,1024]{2,1,0:T(8,128)(2,1)S(1)} %bitcast.176), channel_id=1, source_target_pairs={{0,8},{1,9},{2,10},{3,11},{4,12},{5,13},{6,14},{7,15},{8,0},{9,1},... | collective-permute-start | bytes 9437192 | tf_op jit(solution)/shard_map/ppermute | solution.py:881
  111.2 8.7 %collective-permute-start.23 = (bf16[256,512]{1,0:T(8,128)(2,1)S(1)}, bf16[256,512]{1,0:T(8,128)(2,1)S(1)}, u32[]{:S(2)}, u32[]{:S(2)}) collective-permute-start(bf16[256,512]{1,0:T(8,128)(2,1)S(1)} %collective-permute-done.19.refs_7_.refs_4_), channel_id=1, source_target_pairs={{0,16},{1,17},{2,18},{3,19},{4,20},{5,21},{6,22},{7,23},{8,24},{9,... | collective-permute-start | bytes 786440 | tf_op jit(solution)/shard_map/ppermute | solution.py:881
  127.4 13.6 %collective-permute-start.24 = (bf16[2,256,512]{2,1,0:T(8,128)(2,1)}, bf16[2,256,512]{2,1,0:T(8,128)(2,1)S(1)}, u32[]{:S(2)}, u32[]{:S(2)}) collective-permute-start(bf16[2,256,512]{2,1,0:T(8,128)(2,1)} %down_grad1.1), channel_id=1, source_target_pairs={{0,16},{1,17},{2,18},{3,19},{4,20},{5,21},{6,22},{7,23},{8,24},{9,... | collective-permute-start | bytes 1572872 | tf_op jit(solution)/shard_map/ppermute | solution.py:881
  141.0 9.6 %collective-permute-start.25 = (bf16[4,384,1024]{2,1,0:T(8,128)(2,1)}, bf16[4,384,1024]{2,1,0:T(8,128)(2,1)S(1)}, u32[]{:S(2)}, u32[]{:S(2)}) collective-permute-start(bf16[4,384,1024]{2,1,0:T(8,128)(2,1)} %get-tuple-element.232), channel_id=1, source_target_pairs={{0,8},{1,9},{2,10},{3,11},{4,12},{5,13},{6,14},{7,15},{8,0},{9,1},... | collective-permute-start | bytes 9437192 | tf_op jit(solution)/shard_map/ppermute | solution.py:881
  152.8 23.4 %collective-permute-start.27 = (bf16[1,2,192,1024]{3,2,1,0:T(8,128)(2,1)S(1)}, bf16[1,2,192,1024]{3,2,1,0:T(8,128)(2,1)S(1)}, u32[]{:S(2)}, u32[]{:S(2)}) collective-permute-start(bf16[1,2,192,1024]{3,2,1,0:T(8,128)(2,1)S(1)} %get-tuple-element.335), channel_id=1, source_target_pairs={{0,1},{1,0},{2,3},{3,2},{4,5},{5,4},{6,7},{7,6},{8,9},{9,8},{10,11... | collective-permute-start | bytes 2359304 | tf_op jit(solution)/shard_map/ppermute | solution.py:881
  154.4 21.8 %collective-permute-start.26 = (bf16[1,2,192,1024]{3,2,1,0:T(8,128)(2,1)S(1)}, bf16[1,2,192,1024]{3,2,1,0:T(8,128)(2,1)S(1)}, u32[]{:S(2)}, u32[]{:S(2)}) collective-permute-start(bf16[1,2,192,1024]{3,2,1,0:T(8,128)(2,1)S(1)} %get-tuple-element.337), channel_id=1, source_target_pairs={{0,2},{1,3},{2,0},{3,1},{4,6},{5,7},{6,4},{7,5},{8,10},{9,11},{10,... | collective-permute-start | bytes 2359304 | tf_op jit(solution)/shard_map/ppermute | solution.py:881
  177.2 8.6 %collective-permute-start.28 = (bf16[4,80,128]{2,1,0:T(8,128)(2,1)S(1)}, bf16[4,80,128]{2,1,0:T(8,128)(2,1)S(1)}, u32[]{:S(2)}, u32[]{:S(2)}) collective-permute-start(bf16[4,80,128]{2,1,0:T(8,128)(2,1)S(1)} %fusion.8), channel_id=1, source_target_pairs={{4,0},{5,1},{6,2},{7,3},{12,8},{13,9},{14,10},{15,11},{20,16},{21,... | collective-permute-start | bytes 245768 | tf_op jit(solution)/shard_map/ppermute | solution.py:881
  191.6 12.5 %collective-permute-start.29 = (bf16[2,256,512]{2,1,0:T(8,128)(2,1)}, bf16[2,256,512]{2,1,0:T(8,128)(2,1)S(1)}, u32[]{:S(2)}, u32[]{:S(2)}) collective-permute-start(bf16[2,256,512]{2,1,0:T(8,128)(2,1)} %up_grad1.1), channel_id=1, source_target_pairs={{0,16},{1,17},{2,18},{3,19},{4,20},{5,21},{6,22},{7,23},{8,24},{9,... | collective-permute-start | bytes 1572872 | tf_op jit(solution)/shard_map/ppermute | solution.py:881
  204.9 24.7 %collective-permute-start.31 = (bf16[1,192,1024]{2,1,0:T(8,128)(2,1)S(1)}, bf16[1,192,1024]{2,1,0:T(8,128)(2,1)S(1)}, u32[]{:S(2)}, u32[]{:S(2)}) collective-permute-start(bf16[1,192,1024]{2,1,0:T(8,128)(2,1)S(1)} %get-tuple-element.344), channel_id=1, source_target_pairs={{0,1},{1,0},{2,3},{3,2},{4,5},{5,4},{6,7},{7,6},{8,9},{9,8},{10,11... | collective-permute-start | bytes 1179656 | tf_op jit(solution)/shard_map/ppermute | solution.py:881
  205.8 23.9 %collective-permute-start.32 = (bf16[1,192,1024]{2,1,0:T(8,128)(2,1)S(1)}, bf16[1,192,1024]{2,1,0:T(8,128)(2,1)S(1)}, u32[]{:S(2)}, u32[]{:S(2)}) collective-permute-start(bf16[1,192,1024]{2,1,0:T(8,128)(2,1)S(1)} %get-tuple-element.342), channel_id=1, source_target_pairs={{0,2},{1,3},{2,0},{3,1},{4,6},{5,7},{6,4},{7,5},{8,10},{9,11},{10,... | collective-permute-start | bytes 1179656 | tf_op jit(solution)/shard_map/ppermute | solution.py:881
  207.3 22.3 %collective-permute-start.30 = (bf16[256,512]{1,0:T(8,128)(2,1)S(1)}, bf16[256,512]{1,0:T(8,128)(2,1)S(1)}, u32[]{:S(2)}, u32[]{:S(2)}) collective-permute-start(bf16[256,512]{1,0:T(8,128)(2,1)S(1)} %copy-done.35), channel_id=1, source_target_pairs={{0,4},{1,5},{2,6},{3,7},{4,0},{5,1},{6,2},{7,3},{8,12},{9,13},{10,... | collective-permute-start | bytes 786440 | tf_op jit(solution)/shard_map/ppermute | solution.py:881
  229.6 10.6 %collective-permute-start.33 = (bf16[4,384,1024]{2,1,0:T(8,128)(2,1)}, bf16[4,384,1024]{2,1,0:T(8,128)(2,1)S(1)}, u32[]{:S(2)}, u32[]{:S(2)}) collective-permute-start(bf16[4,384,1024]{2,1,0:T(8,128)(2,1)} %get-tuple-element.278), channel_id=1, source_target_pairs={{0,8},{1,9},{2,10},{3,11},{4,12},{5,13},{6,14},{7,15},{8,0},{9,1},... | collective-permute-start | bytes 9437192 | tf_op jit(solution)/shard_map/ppermute | solution.py:881
  230.5 9.7 %collective-permute-start.34 = (f32[4,1024]{1,0:T(4,128)S(1)}, f32[4,1024]{1,0:T(4,128)S(1)}, u32[]{:S(2)}, u32[]{:S(2)}) collective-permute-start(f32[4,1024]{1,0:T(4,128)S(1)} %slice.197), channel_id=1, source_target_pairs={{0,1},{1,0},{2,3},{3,2},{4,5},{5,4},{6,7},{7,6},{8,9},{9,8},{10,11... | collective-permute-start | bytes 49160 | tf_op jit(solution)/shard_map/ppermute | solution.py:881
  239.6 14.2 %collective-permute-start.37 = (bf16[2,256,512]{2,1,0:T(8,128)(2,1)}, bf16[2,256,512]{2,1,0:T(8,128)(2,1)S(1)}, u32[]{:S(2)}, u32[]{:S(2)}) collective-permute-start(bf16[2,256,512]{2,1,0:T(8,128)(2,1)} %head_grad1.1), channel_id=1, source_target_pairs={{0,16},{1,17},{2,18},{3,19},{4,20},{5,21},{6,22},{7,23},{8,24},{9,... | collective-permute-start | bytes 1572872 | tf_op jit(solution)/shard_map/ppermute | solution.py:881
  242.4 26.1 %collective-permute-start.36 = (bf16[1,2,192,1024]{3,2,1,0:T(8,128)(2,1)S(1)}, bf16[1,2,192,1024]{3,2,1,0:T(8,128)(2,1)S(1)}, u32[]{:S(2)}, u32[]{:S(2)}) collective-permute-start(bf16[1,2,192,1024]{3,2,1,0:T(8,128)(2,1)S(1)} %get-tuple-element.330), channel_id=1, source_target_pairs={{0,1},{1,0},{2,3},{3,2},{4,5},{5,4},{6,7},{7,6},{8,9},{9,8},{10,11... | collective-permute-start | bytes 2359304 | tf_op jit(solution)/shard_map/ppermute | solution.py:881
  243.0 25.6 %collective-permute-start.35 = (bf16[1,2,192,1024]{3,2,1,0:T(8,128)(2,1)S(1)}, bf16[1,2,192,1024]{3,2,1,0:T(8,128)(2,1)S(1)}, u32[]{:S(2)}, u32[]{:S(2)}) collective-permute-start(bf16[1,2,192,1024]{3,2,1,0:T(8,128)(2,1)S(1)} %get-tuple-element.332), channel_id=1, source_target_pairs={{0,2},{1,3},{2,0},{3,1},{4,6},{5,7},{6,4},{7,5},{8,10},{9,11},{10,... | collective-permute-start | bytes 2359304 | tf_op jit(solution)/shard_map/ppermute | solution.py:881
  243.6 10.2 %collective-permute-start.38 = (f32[4,1024]{1,0:T(4,128)S(1)}, f32[4,1024]{1,0:T(4,128)S(1)}, u32[]{:S(2)}, u32[]{:S(2)}) collective-permute-start(f32[4,1024]{1,0:T(4,128)S(1)} %slice_add_fusion), channel_id=1, source_target_pairs={{0,8},{1,9},{2,10},{3,11},{4,12},{5,13},{6,14},{7,15},{8,0},{9,1},... | collective-permute-start | bytes 49160 | tf_op jit(solution)/shard_map/ppermute | solution.py:881
  253.8 9.4 %collective-permute-start.39 = (f32[4,1024]{1,0:T(4,128)S(1)}, f32[4,1024]{1,0:T(4,128)S(1)}, u32[]{:S(2)}, u32[]{:S(2)}) collective-permute-start(f32[4,1024]{1,0:T(4,128)S(1)} %add.162), channel_id=1, source_target_pairs={{0,16},{1,17},{2,18},{3,19},{4,20},{5,21},{6,22},{7,23},{8,24},{9,... | collective-permute-start | bytes 49160 | tf_op jit(solution)/shard_map/ppermute | solution.py:881
  254.5 14.0 %collective-permute-start.40 = (bf16[256,512]{1,0:T(8,128)(2,1)}, bf16[256,512]{1,0:T(8,128)(2,1)S(1)}, u32[]{:S(2)}, u32[]{:S(2)}) collective-permute-start(bf16[256,512]{1,0:T(8,128)(2,1)} %get-tuple-element.289), channel_id=1, source_target_pairs={{0,4},{1,5},{2,6},{3,7},{4,0},{5,1},{6,2},{7,3},{8,12},{9,13},{10,... | collective-permute-start | bytes 786440 | tf_op jit(solution)/shard_map/ppermute | solution.py:881
  269.5 11.6 %collective-permute-start.47 = (bf16[256,512]{1,0:T(8,128)(2,1)S(1)}, bf16[256,512]{1,0:T(8,128)(2,1)S(1)}, u32[]{:S(2)}, u32[]{:S(2)}) collective-permute-start(bf16[256,512]{1,0:T(8,128)(2,1)S(1)} %copy-done.34), channel_id=1, source_target_pairs={{0,4},{1,5},{2,6},{3,7},{4,0},{5,1},{6,2},{7,3},{8,12},{9,13},{10,... | collective-permute-start | bytes 786440 | tf_op jit(solution)/shard_map/ppermute | solution.py:881
  270.1 16.4 %collective-permute-start.41 = (bf16[1,192,1024]{2,1,0:T(8,128)(2,1)S(1)}, bf16[1,192,1024]{2,1,0:T(8,128)(2,1)S(1)}, u32[]{:S(2)}, u32[]{:S(2)}) collective-permute-start(bf16[1,192,1024]{2,1,0:T(8,128)(2,1)S(1)} %get-tuple-element.340), channel_id=1, source_target_pairs={{0,1},{1,0},{2,3},{3,2},{4,5},{5,4},{6,7},{7,6},{8,9},{9,8},{10,11... | collective-permute-start | bytes 1179656 | tf_op jit(solution)/shard_map/ppermute | solution.py:881
  272.0 14.5 %collective-permute-start.42 = (bf16[1,192,1024]{2,1,0:T(8,128)(2,1)S(1)}, bf16[1,192,1024]{2,1,0:T(8,128)(2,1)S(1)}, u32[]{:S(2)}, u32[]{:S(2)}) collective-permute-start(bf16[1,192,1024]{2,1,0:T(8,128)(2,1)S(1)} %get-tuple-element.338), channel_id=1, source_target_pairs={{0,2},{1,3},{2,0},{3,1},{4,6},{5,7},{6,4},{7,5},{8,10},{9,11},{10,... | collective-permute-start | bytes 1179656 | tf_op jit(solution)/shard_map/ppermute | solution.py:881
  272.9 2.2 collective-permute-start.44
  273.6 3.4 %collective-permute-start.45 = (bf16[256,256]{1,0:T(8,128)(2,1)S(1)}, bf16[256,256]{1,0:T(8,128)(2,1)S(1)}, u32[]{:S(2)}, u32[]{:S(2)}) collective-permute-start(bf16[256,256]{1,0:T(8,128)(2,1)S(1)} %get-tuple-element.352), channel_id=1, source_target_pairs={{0,8},{1,9},{2,10},{3,11},{4,12},{5,13},{6,14},{7,15},{8,0},{9,1},... | collective-permute-start | bytes 393224 | tf_op jit(solution)/shard_map/ppermute | solution.py:881
  275.1 11.4 %collective-permute-start.43 = (f32[4,1024]{1,0:T(4,128)S(1)}, f32[4,1024]{1,0:T(4,128)S(1)}, u32[]{:S(2)}, u32[]{:S(2)}) collective-permute-start(f32[4,1024]{1,0:T(4,128)S(1)} %add.165), channel_id=1, source_target_pairs={{0,2},{1,3},{2,0},{3,1},{4,6},{5,7},{6,4},{7,5},{8,10},{9,11},{10,... | collective-permute-start | bytes 49160 | tf_op jit(solution)/shard_map/ppermute | solution.py:881
  281.8 9.9 %collective-permute-start.48 = (bf16[256,256]{1,0:T(8,128)(2,1)S(1)}, bf16[256,256]{1,0:T(8,128)(2,1)S(1)}, u32[]{:S(2)}, u32[]{:S(2)}) collective-permute-start(bf16[256,256]{1,0:T(8,128)(2,1)S(1)} %get-tuple-element.350), channel_id=1, source_target_pairs={{0,8},{1,9},{2,10},{3,11},{4,12},{5,13},{6,14},{7,15},{8,0},{9,1},... | collective-permute-start | bytes 393224 | tf_op jit(solution)/shard_map/ppermute | solution.py:881
  286.5 8.3 %collective-permute-start.46 = (f32[4,1024]{1,0:T(4,128)S(1)}, f32[4,1024]{1,0:T(4,128)S(1)}, u32[]{:S(2)}, u32[]{:S(2)}) collective-permute-start(f32[4,1024]{1,0:T(4,128)S(1)} %add.168), channel_id=1, source_target_pairs={{0,4},{1,5},{2,6},{3,7},{4,0},{5,1},{6,2},{7,3},{8,12},{9,13},{10,... | collective-permute-start | bytes 49160 | tf_op jit(solution)/shard_map/ppermute | solution.py:881
  (37 other events, 273.3 us)
